TPU v7x, 256 devices: a whole 4x4x8 slice. The times are simulated.
256 devices in a mesh: dp: 64 (over z, y, core), tensor: 4 (over x).
Axes of the slice: x: 4, y: 4, z: 8, core: 2. Of those that a mesh axis runs over, the one named last changes fastest.
Arguments:
- activations: bfloat16 [16384, 8192], P('dp'), may hold values from -16 to 16
- key_value_grads: bfloat16 [16384, 2, 1024], P('dp', None, 'tensor'), may hold values from -6 to 6
- owner_table: int32 [64], replicated, may hold values from 0 to 63, each once
- left_factors: float32 [4, 64, 512, 512], P('tensor', 'dp'), may hold values from -16 to 16, as said below
- right_factors: float32 [4, 64, 128, 128], P('tensor', 'dp'), may hold values from -16 to 16, as said below
Outputs:
- left_updated: float32 [4, 64, 512, 512], P('tensor', 'dp')
- right_updated: float32 [4, 64, 128, 128], P('tensor', 'dp')
- update: bfloat16 [2, 8192, 1024], P(None, 'dp')
Inputs may be any that keep to these rules, and one draw needn't show every extreme that they name: `owner_table`: each block number appears once; slot s lies on index s // 1 of dp. `left_factors`: every block is symmetric positive definite. `right_factors`: every block is symmetric positive definite.
All inputs are finite; a program needn't handle non-finite values.
Results may differ from a plain program's by a relative error of at most 0.012.
The roundings to bfloat16 on the way count: a program that leaves them out, or rounds other values in their place, can miss the bound.
Values may be sent and summed in bfloat16 or wider, within the bound.
No kernel may reach another device: no remote copies, remote signals or barrier semaphores. Data moves between devices by JAX's collectives and lax.ppermute only.
A program may use at most 128 MiB of HBM per device.

v0:
```python
import jax
import jax.numpy as jnp
from jax import lax
from jax.experimental import pallas as pl
from jax.experimental.pallas import tpu as pltpu
from jax.sharding import Mesh
from jax.sharding import PartitionSpec as P

ITERS = 8
NZ = 8
NY = 4
DP = ("dp_0", "dp_1", "dp_2")
Z, Y, CORE = DP
F32 = jnp.float32
BF16 = jnp.bfloat16

MOMENT_DECAY = 0.9
RIDGE_SHARE = 0.0001
def shifted(x, axis, step):
    size = lax.axis_size(axis)
    return lax.ppermute(x, axis, [(i, (i + step) % size) for i in range(size)])


def partial_sums(counts, half_cols, acts, acts_peer, kvt, kvt_peer, acts_at, kvt_at):
    rows = kvt.shape[0] // 4
    total = sum(counts)

    def body(acts_at_ref, kvt_at_ref, a_ref, ap_ref, k_ref, kp_ref, *out_refs):
        n = 0
        for count, out_ref in zip(counts, out_refs):
            for i in range(count):
                cols = pl.ds(pl.multiple_of(acts_at_ref[n] * half_cols, half_cols), half_cols)
                lines = pl.ds(pl.multiple_of(kvt_at_ref[n] * rows, rows), rows)
                summed = jnp.dot(k_ref[lines, :], a_ref[:, cols], preferred_element_type=F32)
                summed += jnp.dot(kp_ref[lines, :], ap_ref[:, cols], preferred_element_type=F32)
                out_ref[i] = summed.astype(BF16)
                n += 1

    vmem = pl.BlockSpec(memory_space=pltpu.VMEM)
    smem = pl.BlockSpec(memory_space=pltpu.SMEM)
    return pl.pallas_call(
        body,
        out_shape=[jax.ShapeDtypeStruct((c, rows, half_cols), BF16) for c in counts],
        in_specs=[smem, smem, vmem, vmem, vmem, vmem],
        out_specs=[vmem for _ in counts],
        compiler_params=pltpu.CompilerParams(vmem_limit_bytes=48 * 1024 * 1024),
        name="partial_sums",
    )(acts_at, kvt_at, acts, acts_peer, kvt, kvt_peer)


def wide(*parts):
    total = parts[0].astype(F32)
    for p in parts[1:]:
        total = total + p.astype(F32)
    return total


def added(*parts):
    return wide(*parts).astype(BF16)


def reduce_ring8(v, axis, four_up, four_down, first_up, first_down):
    up = first_up(v[3], shifted(four_up, axis, 1))
    down = first_down(v[-3], shifted(four_down, axis, -1))
    for d in (2, 1):
        up = added(v[d], shifted(up, axis, 1))
        down = added(v[-d], shifted(down, axis, -1))
    return v[0], shifted(up, axis, 1), shifted(down, axis, -1)


def reduce_ring4(v, axis, two_up, two_down, first_up, first_down):
    up = first_up(v[1], shifted(two_up, axis, 1))
    down = first_down(v[-1], shifted(two_down, axis, -1))
    return v[0], shifted(up, axis, 1), shifted(down, axis, -1)


def low_half(base, part):
    h = part.shape[0]
    return jnp.concatenate([added(base[:h], part), base[h:].astype(BF16)], axis=0)


def high_half(base, part):
    h = part.shape[0]
    return jnp.concatenate([base[:h].astype(BF16), added(base[h:], part)], axis=0)


def transposed_sum(refs):
    total = refs[0][...].astype(F32)
    for ref in refs[1:]:
        total = total + ref[...].astype(F32)
    return total


def spread_eye(n):
    return lax.broadcasted_iota(jnp.int32, (n, n), 0) == lax.broadcasted_iota(jnp.int32, (n, n), 1)


def narrow_factor(powered, eye):
    return ((jnp.where(eye, 5.0, 0.0) - powered) * 0.25).astype(BF16)


def coarse(a, b):
    return jnp.dot(a, b, preferred_element_type=F32)


def exact(a, b):
    return jnp.dot(a, b, precision=lax.Precision.HIGHEST, preferred_element_type=F32)


def start_root(matrix, f_ref, m_ref, x_ref):
    n = matrix.shape[0]
    eye = spread_eye(n)
    trace = jnp.sum(jnp.where(eye, matrix, 0.0), keepdims=True)
    shifted = matrix + jnp.where(eye, RIDGE_SHARE * trace / n, 0.0)
    scaling = 2.5 / jnp.sqrt(jnp.sum(shifted * shifted, keepdims=True))
    powered = scaling * shifted
    factor = narrow_factor(powered, eye)
    first = jnp.sqrt(jnp.sqrt(scaling)).astype(BF16).astype(F32)
    f_ref[...] = factor
    m_ref[...] = powered.astype(BF16)
    x_ref[...] = (first * factor.astype(F32)).astype(BF16)


def advance_power(f_ref, m_ref, eye):
    factor = f_ref[...]
    squared = coarse(factor, factor).astype(BF16)
    fourth = coarse(squared, squared).astype(BF16)
    powered = coarse(fourth, m_ref[...])
    f_ref[...] = narrow_factor(powered, eye)
    m_ref[...] = powered.astype(BF16)


def precondition(parts_a, parts_b, left, right, inverse_tokens):
    n_a, n_b = len(parts_a), len(parts_b)
    order, width = left.shape[0], right.shape[0]

    def body(*refs):
        a_refs, b_refs = refs[:n_a], refs[n_a : n_a + n_b]
        left_ref, right_ref, left_out, right_out, dir_ref = refs[n_a + n_b : n_a + n_b + 5]
        g_ref, spread_ref, fl, ml, xl, fr, mr, xr = refs[n_a + n_b + 5 :]
        gt = jnp.concatenate([transposed_sum(a_refs), transposed_sum(b_refs)], axis=1)
        gt = gt * inverse_tokens
        g = gt.T
        g_ref[...] = g
        share = 1.0 - MOMENT_DECAY
        left_new = MOMENT_DECAY * left_ref[...] + share * exact(g, gt)
        left_out[...] = left_new
        start_root(left_new, fl, ml, xl)
        right_new = MOMENT_DECAY * right_ref[...] + share * exact(gt, g)
        right_out[...] = right_new
        start_root(right_new, fr, mr, xr)

        def step(_, carry):
            advance_power(fl, ml, spread_eye(order))
            advance_power(fr, mr, spread_eye(width))
            xl[...] = coarse(xl[...], fl[...]).astype(BF16)
            xr[...] = coarse(xr[...], fr[...]).astype(BF16)
            return carry

        lax.fori_loop(0, ITERS - 2, step, 0)
        advance_power(fl, ml, spread_eye(order))
        advance_power(fr, mr, spread_eye(width))
        left_root = coarse(xl[...], fl[...])
        right_root = coarse(xr[...], fr[...])
        pre = exact(exact(left_root, g_ref[...]), right_root)
        scale = jnp.sqrt(jnp.mean(pre * pre, keepdims=True) + 1e-06)
        g_ref[...] = pre / scale
        pieces = order // 8
        for q in range(4):
            for i in range(2):
                rows = g_ref[pl.ds((q * 2 + i) * pieces, pieces), :]
                spread_ref[pl.ds(q * 2 + i, pieces, stride=8), :] = rows
        dir_ref[...] = spread_ref[...].astype(BF16)

    vmem = pl.BlockSpec(memory_space=pltpu.VMEM)
    square = lambda n: [pltpu.VMEM((n, n), BF16)] * 3
    return pl.pallas_call(
        body,
        out_shape=[
            jax.ShapeDtypeStruct(left.shape, F32),
            jax.ShapeDtypeStruct(right.shape, F32),
            jax.ShapeDtypeStruct((order, width), BF16),
        ],
        in_specs=[vmem] * (n_a + n_b + 2),
        out_specs=[vmem] * 3,
        scratch_shapes=[pltpu.VMEM((order, width), F32)] * 2 + square(order) + square(width),
        compiler_params=pltpu.CompilerParams(vmem_limit_bytes=48 * 1024 * 1024),
        name="precondition",
    )(*parts_a, *parts_b, left, right)

def placed(got, shards):
    pieces, width = got.shape[0], got.shape[3]

    def body(got_ref, out_ref, wide_ref):
        wide_ref[...] = got_ref[...].astype(F32)
        for t in range(shards):
            for j in range(2):
                for c in range(2):
                    for i in range(2):
                        at = t * 8 + j * 4 + c * 2 + i
                        rows = wide_ref[pl.ds(at, pieces, stride=8 * shards), :]
                        cols = pl.ds((t * 2 + c) * width, width)
                        out_ref[j, pl.ds(i * pieces, pieces), cols] = rows.astype(BF16)

    vmem = pl.BlockSpec(memory_space=pltpu.VMEM)
    total = pieces * shards * 8
    return pl.pallas_call(
        body,
        out_shape=jax.ShapeDtypeStruct((2, 2 * pieces, shards * 2 * width), BF16),
        in_specs=[vmem],
        out_specs=vmem,
        scratch_shapes=[pltpu.VMEM((total, width), F32)],
        compiler_params=pltpu.CompilerParams(vmem_limit_bytes=16 * 1024 * 1024),
        name="placed",
    )(got.reshape(total, width))


def routed(directions, owner_table, row_blocks, col_blocks):
    slots = owner_table.shape[0]
    width = directions.shape[1]
    shards = lax.axis_size("tensor")
    held = lax.all_to_all(directions.reshape(slots, 8, width), DP, 0, 0, tiled=True)
    shape = (row_blocks, 4, 2, col_blocks, 2)
    r, q, j, c, i = (lax.broadcasted_iota(jnp.int32, shape, k) for k in range(5))
    wanted = ((((j * row_blocks + r) * col_blocks + c) * 4 + q) * 2 + i).reshape(-1)
    present = (owner_table[:, None] * 8 + jnp.arange(8, dtype=jnp.int32)[None, :]).reshape(-1)
    pick = (wanted[:, None] == present[None, :]).astype(BF16)
    chosen = jnp.dot(pick, held.reshape(slots * 8, width), preferred_element_type=F32)
    chosen = chosen.astype(BF16).reshape(slots, 1, 8, width)
    copies = jnp.broadcast_to(chosen, (slots, shards, 8, width)).reshape(slots * shards, 8, width)
    got = lax.all_to_all(copies, (*DP, "tensor"), 0, 0, tiled=True)
    return placed(got.reshape(slots, shards, 8, width), shards)


def own_gradient(activations, key_value_grads, owner_table, block_rows, block_cols):
    tokens, features = activations.shape
    half_cols = block_rows // 2
    kvt = key_value_grads.reshape(tokens, -1).T
    pair = [(0, 1), (1, 0)]
    acts_peer = lax.ppermute(activations, CORE, pair)
    kvt_peer = lax.ppermute(kvt, CORE, pair)

    z, y, core = (lax.axis_index(a) for a in DP)
    col_blocks = key_value_grads.shape[2] // block_cols
    row_blocks = features // block_rows

    dz_all = jnp.arange(NZ, dtype=jnp.int32)
    dy_all = jnp.arange(NY, dtype=jnp.int32)
    slots = ((z + dz_all[:, None]) % NZ * NY + (y + dy_all[None, :]) % NY) * 2 + core
    blocks = jnp.take(owner_table, slots)
    projection = blocks // (row_blocks * col_blocks)
    row = blocks % (row_blocks * col_blocks) // col_blocks
    line = projection * col_blocks + blocks % col_blocks

    def listing(pairs):
        dzs = jnp.array([p[0] % NZ for p in pairs], jnp.int32)
        dys = jnp.array([p[1] % NY for p in pairs], jnp.int32)
        halves = jnp.array([p[2] for p in pairs], jnp.int32)
        at = dzs * NY + dys
        return jnp.take(row.reshape(-1), at) * 2 + halves, jnp.take(line.reshape(-1), at)

    def sums(groups):
        a_at, k_at = listing([p for g in groups for p in g])
        counts = [len(g) for g in groups]
        return partial_sums(counts, half_cols, activations, acts_peer, kvt, kvt_peer, a_at, k_at)

    first = [
        [(4, dy, 0) for dy in (0, 1)],
        [(4, dy, 0) for dy in (2, 3)],
        [(dz, 2, 1) for dz in (0, 1, 2, 3)],
        [(dz, 2, 1) for dz in (4, 5, 6, 7)],
    ]
    a_up, a_down, b_up, b_down = sums(first)
    az = (3, -3, 2, -2, 1, -1, 0)
    by = (1, -1, 0)
    rest = [[(dz, dy, 0) for dy in range(NY)] for dz in az]
    rest += [[(dz, dy, 1) for dz in range(NZ)] for dy in by]
    later = sums(rest)
    va = dict(zip(az, later[: len(az)]))
    vb = dict(zip(by, later[len(az) :]))

    ta = wide(*reduce_ring8(va, Z, a_up, a_down, low_half, high_half))
    tb = wide(*reduce_ring4(vb, Y, b_up, b_down, low_half, high_half))

    h = block_cols // 2
    two = ta[2].astype(BF16)
    ga = reduce_ring4({0: ta[0], 1: ta[1], -1: ta[3]}, Y, two[:h], two[h:], low_half, high_half)
    four = tb[4].astype(BF16)
    vz = {d: tb[d % NZ] for d in range(-3, 4)}
    gb = reduce_ring8(vz, Z, four[:h], four[h:], low_half, high_half)
    return ga, gb


def local(activations, key_value_grads, owner_table, left_factors, right_factors):
    rows_block = left_factors.shape[2]
    cols_block = right_factors.shape[2]
    row_blocks = activations.shape[1] // rows_block
    col_blocks = key_value_grads.shape[2] // cols_block
    inverse_tokens = 1.0 / (activations.shape[0] * lax.axis_size(DP))

    ga, gb = own_gradient(activations, key_value_grads, owner_table, rows_block, cols_block)
    left_new, right_new, directions = precondition(
        ga, gb, left_factors[0, 0], right_factors[0, 0], inverse_tokens
    )
    update = routed(directions, owner_table, row_blocks, col_blocks)
    return (left_new[None, None], right_new[None, None], update)


def solution(mesh):
    split = Mesh(
        mesh.devices.reshape(8, 4, 2, mesh.shape["tensor"]), ("dp_0", "dp_1", "dp_2", "tensor")
    )
    return jax.shard_map(
        local,
        mesh=split,
        in_specs=(
            P(DP, None),
            P(DP, None, "tensor"),
            P(),
            P("tensor", DP, None, None),
            P("tensor", DP, None, None),
        ),
        out_specs=(P("tensor", DP, None, None), P("tensor", DP, None, None), P(None, DP, None)),
        check_vma=False,
    )
```

profile of v0, /device:TPU:1, one launch (start us, length us, event | category | flops | bytes accessed | tf_op | source)
XLA Modules:
  0.0 147.1 jit_solution(11816206359743737815)
XLA Ops:
  0.7 3.3 %collective-permute-start = (bf16[256,8192]{1,0:T(8,128)(2,1)}, bf16[256,8192]{1,0:T(8,128)(2,1)}, u32[]{:S(2)}, u32[]{:S(2)}) collective-permute-start(bf16[256,8192]{1,0:T(8,128)(2,1)} %a_ref.3), channel_id=1, source_target_pairs={{0,4},{4,0},{1,5},{5,1},{2,6},{6,2},{3,7},{7,3},{8,12},{12,8},{9,1... | collective-permute-start | bytes 12582920 | tf_op jit(solution)/shard_map/ppermute | solution.py:240
  4.0 1.1 copy.16
  5.7 1.4 gather_fusion
  9.2 1.9 %collective-permute-done.1.kp_ref = bf16[512,256]{1,0:T(8,128)(2,1)S(1)} collective-permute-done((bf16[512,256]{1,0:T(8,128)(2,1)S(1)}, bf16[512,256]{1,0:T(8,128)(2,1)S(1)}, u32[]{:S(2)}, u32[]{:S(2)}) %collective-permute-start.1) | collective-permute-done | bytes 262176 | tf_op jit(solution)/shard_map/ppermute | solution.py:241
  11.2 2.2 %copy-done = bf16[256,8192]{1,0:T(8,128)(2,1)S(1)} copy-done((bf16[256,8192]{1,0:T(8,128)(2,1)S(1)}, bf16[256,8192]{1,0:T(8,128)(2,1)}, u32[]{:S(2)}) %copy-start) | copy-done | bytes 4194328
  13.3 2.9 %partial_sums.3 = (bf16[2,128,256]{2,1,0:T(8,128)(2,1)S(1)}, bf16[2,128,256]{2,1,0:T(8,128)(2,1)S(1)}, bf16[4,128,256]{2,1,0:T(8,128)(2,1)S(1)}, bf16[4,128,256]{2,1,0:T(8,128)(2,1)S(1)}) custom-call(s32[12]{0:T(128)S(1)} %multiply_add_fusion.1.acts_at_ref, s32[12]{0:T(128)S(1)} %gather_fusion.4, bf16[256,8192]{1,0:T(8,128)(2,1)S(1)} %copy-done, ...), custom_call_target="tpu_custom_call" | custom-call | tf_op jit(solution)/shard_map/partial_sums/pallas_call | solution.py:41
  16.3 0.8 gather_fusion.2
  17.1 1.2 collective-permute-start.14
  18.4 5.8 %partial_sums.2 = (bf16[4,128,256]{2,1,0:T(8,128)(2,1)S(1)}, bf16[4,128,256]{2,1,0:T(8,128)(2,1)S(1)}, bf16[4,128,256]{2,1,0:T(8,128)(2,1)S(1)}, bf16[4,128,256]...) custom-call(s32[52]{0:T(128)S(1)} %multiply_add_fusion.2.acts_at_ref, ...), custom_call_target="tpu_custom_call" | custom-call | tf_op jit(solution)/shard_map/partial_sums/pallas_call | solution.py:41
  24.2 1.6 %collective-permute-start.16 = (bf16[4,128,256]{2,1,0:T(8,128)(2,1)S(1)}, bf16[4,128,256]{2,1,0:T(8,128)(2,1)S(1)}, u32[]{:S(2)}, u32[]{:S(2)}) collective-permute-start(bf16[4,128,256]{2,1,0:T(8,128)(2,1)S(1)} %get-tuple-element.35), channel_id=1, source_target_pairs={{0,24},{8,0},{16,8},{24,16},{1,25},{9,1},{17,9},{25,17},{2,26},{10... | collective-permute-start | bytes 786440 | tf_op jit(solution)/shard_map/ppermute | solution.py:21
  25.9 4.0 %collective-permute-start.6 = (bf16[2,128,256]{2,1,0:T(8,128)(2,1)S(1)}, bf16[2,128,256]{2,1,0:T(8,128)(2,1)S(1)}, u32[]{:S(2)}, u32[]{:S(2)}) collective-permute-start(bf16[2,128,256]{2,1,0:T(8,128)(2,1)S(1)} %get-tuple-element.30), channel_id=1, source_target_pairs={{0,224},{32,0},{64,32},{96,64},{128,96},{160,128},{192,160},{224,1... | collective-permute-start | bytes 393224 | tf_op jit(solution)/shard_map/ppermute | solution.py:21
  30.1 1.8 %collective-permute-done.6 = bf16[2,128,256]{2,1,0:T(8,128)(2,1)S(1)} collective-permute-done((bf16[2,128,256]{2,1,0:T(8,128)(2,1)S(1)}, bf16[2,128,256]{2,1,0:T(8,128)(2,1)S(1)}, u32[]{:S(2)}, u32[]{:S(2)}) %collective-permute-start.6) | collective-permute-done | bytes 131104 | tf_op jit(solution)/shard_map/ppermute | solution.py:21
  31.9 3.6 %collective-permute-start.7 = (bf16[4,128,256]{2,1,0:T(8,128)(2,1)S(1)}, bf16[4,128,256]{2,1,0:T(8,128)(2,1)S(1)}, u32[]{:S(2)}, u32[]{:S(2)}) collective-permute-start(bf16[4,128,256]{2,1,0:T(8,128)(2,1)S(1)} %pad_maximum_fusion.3), channel_id=1, source_target_pairs={{0,224},{32,0},{64,32},{96,64},{128,96},{160,128},{192,160},{224,1... | collective-permute-start | bytes 786440 | tf_op jit(solution)/shard_map/ppermute | solution.py:21
  35.8 2.7 %collective-permute-start.17 = (bf16[8,128,256]{2,1,0:T(8,128)(2,1)S(1)}, bf16[8,128,256]{2,1,0:T(8,128)(2,1)S(1)}, u32[]{:S(2)}, u32[]{:S(2)}) collective-permute-start(bf16[8,128,256]{2,1,0:T(8,128)(2,1)S(1)} %pad_maximum_fusion.1), channel_id=1, source_target_pairs={{0,24},{8,0},{16,8},{24,16},{1,25},{9,1},{17,9},{25,17},{2,26},{10... | collective-permute-start | bytes 1572872 | tf_op jit(solution)/shard_map/ppermute | solution.py:21
  39.5 3.5 %collective-permute-start.8 = (bf16[4,128,256]{2,1,0:T(8,128)(2,1)S(1)}, bf16[4,128,256]{2,1,0:T(8,128)(2,1)S(1)}, u32[]{:S(2)}, u32[]{:S(2)}) collective-permute-start(bf16[4,128,256]{2,1,0:T(8,128)(2,1)S(1)} %add_convert_fusion.3), channel_id=1, source_target_pairs={{0,224},{32,0},{64,32},{96,64},{128,96},{160,128},{192,160},{224,1... | collective-permute-start | bytes 786440 | tf_op jit(solution)/shard_map/ppermute | solution.py:21
  43.0 2.6 %collective-permute-done.4 = bf16[4,128,256]{2,1,0:T(8,128)(2,1)S(1)} collective-permute-done((bf16[4,128,256]{2,1,0:T(8,128)(2,1)S(1)}, bf16[4,128,256]{2,1,0:T(8,128)(2,1)S(1)}, u32[]{:S(2)}, u32[]{:S(2)}) %collective-permute-start.4) | collective-permute-done | bytes 262176 | tf_op jit(solution)/shard_map/ppermute | solution.py:21
  46.3 3.5 %collective-permute-start.9 = (bf16[4,128,256]{2,1,0:T(8,128)(2,1)S(1)}, bf16[4,128,256]{2,1,0:T(8,128)(2,1)S(1)}, u32[]{:S(2)}, u32[]{:S(2)}) collective-permute-start(bf16[4,128,256]{2,1,0:T(8,128)(2,1)S(1)} %add_convert_fusion.2), channel_id=1, source_target_pairs={{0,224},{32,0},{64,32},{96,64},{128,96},{160,128},{192,160},{224,1... | collective-permute-start | bytes 786440 | tf_op jit(solution)/shard_map/ppermute | solution.py:21
  50.2 2.7 %collective-permute-start.22 = (bf16[64,256]{1,0:T(8,128)(2,1)S(1)}, bf16[64,256]{1,0:T(8,128)(2,1)S(1)}, u32[]{:S(2)}, u32[]{:S(2)}) collective-permute-start(bf16[64,256]{1,0:T(8,128)(2,1)S(1)} %get-tuple-element.50), channel_id=1, source_target_pairs={{0,224},{32,0},{64,32},{96,64},{128,96},{160,128},{192,160},{224,1... | collective-permute-start | bytes 98312 | tf_op jit(solution)/shard_map/ppermute | solution.py:21
  52.8 1.9 %collective-permute-done.18 = bf16[64,256]{1,0:T(8,128)(2,1)S(1)} collective-permute-done((bf16[64,256]{1,0:T(8,128)(2,1)S(1)}, bf16[64,256]{1,0:T(8,128)(2,1)S(1)}, u32[]{:S(2)}, u32[]{:S(2)}) %collective-permute-start.18) | collective-permute-done | bytes 32800 | tf_op jit(solution)/shard_map/ppermute | solution.py:21
  54.7 2.2 %collective-permute-start.23 = (bf16[128,256]{1,0:T(8,128)(2,1)S(1)}, bf16[128,256]{1,0:T(8,128)(2,1)S(1)}, u32[]{:S(2)}, u32[]{:S(2)}) collective-permute-start(bf16[128,256]{1,0:T(8,128)(2,1)S(1)} %pad_maximum_fusion.7), channel_id=1, source_target_pairs={{0,224},{32,0},{64,32},{96,64},{128,96},{160,128},{192,160},{224,1... | collective-permute-start | bytes 196616 | tf_op jit(solution)/shard_map/ppermute | solution.py:21
  56.9 1.6 %collective-permute-done.23 = bf16[128,256]{1,0:T(8,128)(2,1)S(1)} collective-permute-done((bf16[128,256]{1,0:T(8,128)(2,1)S(1)}, bf16[128,256]{1,0:T(8,128)(2,1)S(1)}, u32[]{:S(2)}, u32[]{:S(2)}) %collective-permute-start.23) | collective-permute-done | bytes 65568 | tf_op jit(solution)/shard_map/ppermute | solution.py:21
  58.5 3.4 %collective-permute-start.24 = (bf16[128,256]{1,0:T(8,128)(2,1)S(1)}, bf16[128,256]{1,0:T(8,128)(2,1)S(1)}, u32[]{:S(2)}, u32[]{:S(2)}) collective-permute-start(bf16[128,256]{1,0:T(8,128)(2,1)S(1)} %fusion.5), channel_id=1, source_target_pairs={{0,224},{32,0},{64,32},{96,64},{128,96},{160,128},{192,160},{224,1... | collective-permute-start | bytes 196616 | tf_op jit(solution)/shard_map/ppermute | solution.py:21
  62.1 2.7 %collective-permute-start.12 = (bf16[64,256]{1,0:T(8,128)(2,1)S(1)}, bf16[64,256]{1,0:T(8,128)(2,1)S(1)}, u32[]{:S(2)}, u32[]{:S(2)}) collective-permute-start(bf16[64,256]{1,0:T(8,128)(2,1)S(1)} %get-tuple-element.56), channel_id=1, source_target_pairs={{0,24},{8,0},{16,8},{24,16},{1,25},{9,1},{17,9},{25,17},{2,26},{10... | collective-permute-start | bytes 98312 | tf_op jit(solution)/shard_map/ppermute | solution.py:21
  64.9 2.7 %collective-permute-start.25 = (bf16[128,256]{1,0:T(8,128)(2,1)S(1)}, bf16[128,256]{1,0:T(8,128)(2,1)S(1)}, u32[]{:S(2)}, u32[]{:S(2)}) collective-permute-start(bf16[128,256]{1,0:T(8,128)(2,1)S(1)} %get-tuple-element.45), channel_id=1, source_target_pairs={{0,224},{32,0},{64,32},{96,64},{128,96},{160,128},{192,160},{224,1... | collective-permute-start | bytes 196616 | tf_op jit(solution)/shard_map/ppermute | solution.py:21
  67.6 1.5 %collective-permute-start.13 = (bf16[128,256]{1,0:T(8,128)(2,1)S(1)}, bf16[128,256]{1,0:T(8,128)(2,1)S(1)}, u32[]{:S(2)}, u32[]{:S(2)}) collective-permute-start(bf16[128,256]{1,0:T(8,128)(2,1)S(1)} %pad_maximum_fusion.5), channel_id=1, source_target_pairs={{0,24},{8,0},{16,8},{24,16},{1,25},{9,1},{17,9},{25,17},{2,26},{10... | collective-permute-start | bytes 196616 | tf_op jit(solution)/shard_map/ppermute | solution.py:21
  69.6 1.2 collective-permute-done.13.refs_2_
  70.8 2.7 %collective-permute-done.11.refs_1_ = bf16[128,256]{1,0:T(8,128)(2,1)S(1)} collective-permute-done((bf16[128,256]{1,0:T(8,128)(2,1)S(1)}, bf16[128,256]{1,0:T(8,128)(2,1)S(1)}, u32[]{:S(2)}, u32[]{:S(2)}) %collective-permute-start.11) | collective-permute-done | bytes 65568 | tf_op jit(solution)/shard_map/ppermute | solution.py:21
  73.9 17.0 %precondition.1 = (f32[512,512]{1,0:T(8,128)}, f32[128,128]{1,0:T(8,128)}, bf16[512,128]{1,0:T(8,128)(2,1)}) custom-call(f32[128,256]{1,0:T(8,128)S(1)} %slice_bitcast_fusion.5.refs_0_, bf16[128,256]{1,0:T(8,128)(2,1)S(1)} %collective-permute-done.11.refs_1_, bf16[128,256]{1,0:T(8,128)(2,1)S(1)} %collective-permute-done.13.refs_2_, ...), custom_call_target="tpu_custom_call" | custom-call | tf_op jit(solution)/shard_map/precondition/pallas_call | solution.py:177
  90.9 16.9 %all-to-all-start = ((bf16[64,8,128]{2,1,0:T(8,128)(2,1)}), bf16[64,8,128]{2,1,0:T(8,128)(2,1)S(1)}, u32[]{:S(2)}, u32[]{:S(2)}) async-start(bf16[64,8,128]{2,1,0:T(8,128)(2,1)} %bitcast.25), calls=%async_computation | async-start | bytes 262144 | tf_op jit(solution)/shard_map/all_to_all | solution.py:222
  108.4 10.5 %all-to-all-done = bf16[64,8,128]{2,1,0:T(8,128)(2,1)S(1)} async-done(((bf16[64,8,128]{2,1,0:T(8,128)(2,1)}), bf16[64,8,128]{2,1,0:T(8,128)(2,1)S(1)}, u32[]{:S(2)}, u32[]{:S(2)}) %all-to-all-start) | async-done | bytes 131104 | tf_op jit(solution)/shard_map/all_to_all | solution.py:222
  119.4 26.3 %all_to_all.10 = bf16[256,8,128]{2,1,0:T(8,128)(2,1)S(1)} all-to-all(bf16[256,8,128]{2,1,0:T(8,128)(2,1)S(1)} %bitcast.93), channel_id=1, replica_groups=mesh['dp_0'=8,'dp_1'=4,'dp_2'=2,'tensor'=4] {'dp_0','dp_1','dp_2','tensor'}, dimensions={0} | all-to-all | bytes 1048576 | tf_op jit(solution)/shard_map/all_to_all | solution.py:231
  145.7 1.5 placed.1
  (104 shorter events, 7.5 us)
Async XLA Ops:
  0.7 8.5 %copy-start.7 = (s32[12]{0:T(128)S(1)}, s32[12]{0:T(128)}, u32[]{:S(2)}) copy-start(s32[12]{0:T(128)} %constant.149.clone) | copy-start | bytes 148
  0.7 10.5 %collective-permute-start = (bf16[256,8192]{1,0:T(8,128)(2,1)}, bf16[256,8192]{1,0:T(8,128)(2,1)}, u32[]{:S(2)}, u32[]{:S(2)}) collective-permute-start(bf16[256,8192]{1,0:T(8,128)(2,1)} %a_ref.3), channel_id=1, source_target_pairs={{0,4},{4,0},{1,5},{5,1},{2,6},{6,2},{3,7},{7,3},{8,12},{12,8},{9,1... | collective-permute-start | bytes 12582920 | tf_op jit(solution)/shard_map/ppermute | solution.py:240
  5.1 6.1 %collective-permute-start.1 = (bf16[512,256]{1,0:T(8,128)(2,1)S(1)}, bf16[512,256]{1,0:T(8,128)(2,1)S(1)}, u32[]{:S(2)}, u32[]{:S(2)}) collective-permute-start(bf16[512,256]{1,0:T(8,128)(2,1)S(1)} %bitcast.87), channel_id=1, source_target_pairs={{0,4},{4,0},{1,5},{5,1},{2,6},{6,2},{3,7},{7,3},{8,12},{12,8},{9,1... | collective-permute-start | bytes 786440 | tf_op jit(solution)/shard_map/ppermute | solution.py:241
  9.2 7.1 %copy-start.6 = (s32[52]{0:T(128)S(1)}, s32[52]{0:T(128)}, u32[]{:S(2)}) copy-start(s32[52]{0:T(128)} %constant.152.clone) | copy-start | bytes 628
  16.2 13.7 %collective-permute-start.2 = (bf16[2,128,256]{2,1,0:T(8,128)(2,1)S(1)}, bf16[2,128,256]{2,1,0:T(8,128)(2,1)S(1)}, u32[]{:S(2)}, u32[]{:S(2)}) collective-permute-start(bf16[2,128,256]{2,1,0:T(8,128)(2,1)S(1)} %get-tuple-element.26), channel_id=1, source_target_pairs={{0,32},{32,64},{64,96},{96,128},{128,160},{160,192},{192,224},{224... | collective-permute-start | bytes 393224 | tf_op jit(solution)/shard_map/ppermute | solution.py:21
  17.1 18.3 %collective-permute-start.14 = (bf16[4,128,256]{2,1,0:T(8,128)(2,1)S(1)}, bf16[4,128,256]{2,1,0:T(8,128)(2,1)S(1)}, u32[]{:S(2)}, u32[]{:S(2)}) collective-permute-start(bf16[4,128,256]{2,1,0:T(8,128)(2,1)S(1)} %get-tuple-element.33), channel_id=1, source_target_pairs={{0,8},{8,16},{16,24},{24,0},{1,9},{9,17},{17,25},{25,1},{2,10},{10... | collective-permute-start | bytes 786440 | tf_op jit(solution)/shard_map/ppermute | solution.py:21
  24.2 11.4 %collective-permute-start.16 = (bf16[4,128,256]{2,1,0:T(8,128)(2,1)S(1)}, bf16[4,128,256]{2,1,0:T(8,128)(2,1)S(1)}, u32[]{:S(2)}, u32[]{:S(2)}) collective-permute-start(bf16[4,128,256]{2,1,0:T(8,128)(2,1)S(1)} %get-tuple-element.35), channel_id=1, source_target_pairs={{0,24},{8,0},{16,8},{24,16},{1,25},{9,1},{17,9},{25,17},{2,26},{10... | collective-permute-start | bytes 786440 | tf_op jit(solution)/shard_map/ppermute | solution.py:21
  25.9 5.9 %collective-permute-start.6 = (bf16[2,128,256]{2,1,0:T(8,128)(2,1)S(1)}, bf16[2,128,256]{2,1,0:T(8,128)(2,1)S(1)}, u32[]{:S(2)}, u32[]{:S(2)}) collective-permute-start(bf16[2,128,256]{2,1,0:T(8,128)(2,1)S(1)} %get-tuple-element.30), channel_id=1, source_target_pairs={{0,224},{32,0},{64,32},{96,64},{128,96},{160,128},{192,160},{224,1... | collective-permute-start | bytes 393224 | tf_op jit(solution)/shard_map/ppermute | solution.py:21
  30.0 8.6 %collective-permute-start.3 = (bf16[4,128,256]{2,1,0:T(8,128)(2,1)S(1)}, bf16[4,128,256]{2,1,0:T(8,128)(2,1)S(1)}, u32[]{:S(2)}, u32[]{:S(2)}) collective-permute-start(bf16[4,128,256]{2,1,0:T(8,128)(2,1)S(1)} %pad_maximum_fusion.2), channel_id=1, source_target_pairs={{0,32},{32,64},{64,96},{96,128},{128,160},{160,192},{192,224},{224... | collective-permute-start | bytes 786440 | tf_op jit(solution)/shard_map/ppermute | solution.py:21
  31.9 7.5 %collective-permute-start.7 = (bf16[4,128,256]{2,1,0:T(8,128)(2,1)S(1)}, bf16[4,128,256]{2,1,0:T(8,128)(2,1)S(1)}, u32[]{:S(2)}, u32[]{:S(2)}) collective-permute-start(bf16[4,128,256]{2,1,0:T(8,128)(2,1)S(1)} %pad_maximum_fusion.3), channel_id=1, source_target_pairs={{0,224},{32,0},{64,32},{96,64},{128,96},{160,128},{192,160},{224,1... | collective-permute-start | bytes 786440 | tf_op jit(solution)/shard_map/ppermute | solution.py:21
  35.6 14.2 %collective-permute-start.15 = (bf16[8,128,256]{2,1,0:T(8,128)(2,1)S(1)}, bf16[8,128,256]{2,1,0:T(8,128)(2,1)S(1)}, u32[]{:S(2)}, u32[]{:S(2)}) collective-permute-start(bf16[8,128,256]{2,1,0:T(8,128)(2,1)S(1)} %pad_maximum_fusion), channel_id=1, source_target_pairs={{0,8},{8,16},{16,24},{24,0},{1,9},{9,17},{17,25},{25,1},{2,10},{10... | collective-permute-start | bytes 1572872 | tf_op jit(solution)/shard_map/ppermute | solution.py:21
  35.8 14.0 %collective-permute-start.17 = (bf16[8,128,256]{2,1,0:T(8,128)(2,1)S(1)}, bf16[8,128,256]{2,1,0:T(8,128)(2,1)S(1)}, u32[]{:S(2)}, u32[]{:S(2)}) collective-permute-start(bf16[8,128,256]{2,1,0:T(8,128)(2,1)S(1)} %pad_maximum_fusion.1), channel_id=1, source_target_pairs={{0,24},{8,0},{16,8},{24,16},{1,25},{9,1},{17,9},{25,17},{2,26},{10... | collective-permute-start | bytes 1572872 | tf_op jit(solution)/shard_map/ppermute | solution.py:21
  38.6 7.0 %collective-permute-start.4 = (bf16[4,128,256]{2,1,0:T(8,128)(2,1)S(1)}, bf16[4,128,256]{2,1,0:T(8,128)(2,1)S(1)}, u32[]{:S(2)}, u32[]{:S(2)}) collective-permute-start(bf16[4,128,256]{2,1,0:T(8,128)(2,1)S(1)} %add_convert_fusion.5), channel_id=1, source_target_pairs={{0,32},{32,64},{64,96},{96,128},{128,160},{160,192},{192,224},{224... | collective-permute-start | bytes 786440 | tf_op jit(solution)/shard_map/ppermute | solution.py:21
  39.5 6.8 %collective-permute-start.8 = (bf16[4,128,256]{2,1,0:T(8,128)(2,1)S(1)}, bf16[4,128,256]{2,1,0:T(8,128)(2,1)S(1)}, u32[]{:S(2)}, u32[]{:S(2)}) collective-permute-start(bf16[4,128,256]{2,1,0:T(8,128)(2,1)S(1)} %add_convert_fusion.3), channel_id=1, source_target_pairs={{0,224},{32,0},{64,32},{96,64},{128,96},{160,128},{192,160},{224,1... | collective-permute-start | bytes 786440 | tf_op jit(solution)/shard_map/ppermute | solution.py:21
  45.7 16.2 %collective-permute-start.5 = (bf16[4,128,256]{2,1,0:T(8,128)(2,1)S(1)}, bf16[4,128,256]{2,1,0:T(8,128)(2,1)S(1)}, u32[]{:S(2)}, u32[]{:S(2)}) collective-permute-start(bf16[4,128,256]{2,1,0:T(8,128)(2,1)S(1)} %add_convert_fusion.4), channel_id=1, source_target_pairs={{0,32},{32,64},{64,96},{96,128},{128,160},{160,192},{192,224},{224... | collective-permute-start | bytes 786440 | tf_op jit(solution)/shard_map/ppermute | solution.py:21
  46.3 27.6 %copy-start.1 = (f32[1,1,512,512]{3,2,1,0:T(8,128)S(1)}, f32[1,1,512,512]{3,2,1,0:T(8,128)}, u32[]{:S(2)}) copy-start(f32[1,1,512,512]{3,2,1,0:T(8,128)} %param.18) | copy-start | bytes 3145732
  46.3 27.6 %copy-start.2 = (f32[1,1,128,128]{3,2,1,0:T(8,128)S(1)}, f32[1,1,128,128]{3,2,1,0:T(8,128)}, u32[]{:S(2)}) copy-start(f32[1,1,128,128]{3,2,1,0:T(8,128)} %param.19) | copy-start | bytes 196612
  46.3 15.6 %collective-permute-start.9 = (bf16[4,128,256]{2,1,0:T(8,128)(2,1)S(1)}, bf16[4,128,256]{2,1,0:T(8,128)(2,1)S(1)}, u32[]{:S(2)}, u32[]{:S(2)}) collective-permute-start(bf16[4,128,256]{2,1,0:T(8,128)(2,1)S(1)} %add_convert_fusion.2), channel_id=1, source_target_pairs={{0,224},{32,0},{64,32},{96,64},{128,96},{160,128},{192,160},{224,1... | collective-permute-start | bytes 786440 | tf_op jit(solution)/shard_map/ppermute | solution.py:21
  49.8 58.0 %copy-start.3 = (s32[64]{0:T(128)S(1)}, s32[64]{0:T(128)}, u32[]{:S(2)}) copy-start(s32[64]{0:T(128)} %param.17) | copy-start | bytes 772
  50.1 4.6 %collective-permute-start.18 = (bf16[64,256]{1,0:T(8,128)(2,1)S(1)}, bf16[64,256]{1,0:T(8,128)(2,1)S(1)}, u32[]{:S(2)}, u32[]{:S(2)}) collective-permute-start(bf16[64,256]{1,0:T(8,128)(2,1)S(1)} %get-tuple-element.52), channel_id=1, source_target_pairs={{0,32},{32,64},{64,96},{96,128},{128,160},{160,192},{192,224},{224... | collective-permute-start | bytes 98312 | tf_op jit(solution)/shard_map/ppermute | solution.py:21
  50.2 4.5 %collective-permute-start.22 = (bf16[64,256]{1,0:T(8,128)(2,1)S(1)}, bf16[64,256]{1,0:T(8,128)(2,1)S(1)}, u32[]{:S(2)}, u32[]{:S(2)}) collective-permute-start(bf16[64,256]{1,0:T(8,128)(2,1)S(1)} %get-tuple-element.50), channel_id=1, source_target_pairs={{0,224},{32,0},{64,32},{96,64},{128,96},{160,128},{192,160},{224,1... | collective-permute-start | bytes 98312 | tf_op jit(solution)/shard_map/ppermute | solution.py:21
  54.7 3.8 %collective-permute-start.23 = (bf16[128,256]{1,0:T(8,128)(2,1)S(1)}, bf16[128,256]{1,0:T(8,128)(2,1)S(1)}, u32[]{:S(2)}, u32[]{:S(2)}) collective-permute-start(bf16[128,256]{1,0:T(8,128)(2,1)S(1)} %pad_maximum_fusion.7), channel_id=1, source_target_pairs={{0,224},{32,0},{64,32},{96,64},{128,96},{160,128},{192,160},{224,1... | collective-permute-start | bytes 196616 | tf_op jit(solution)/shard_map/ppermute | solution.py:21
  56.9 7.9 %collective-permute-start.19 = (bf16[128,256]{1,0:T(8,128)(2,1)S(1)}, bf16[128,256]{1,0:T(8,128)(2,1)S(1)}, u32[]{:S(2)}, u32[]{:S(2)}) collective-permute-start(bf16[128,256]{1,0:T(8,128)(2,1)S(1)} %pad_maximum_fusion.6), channel_id=1, source_target_pairs={{0,32},{32,64},{64,96},{96,128},{128,160},{160,192},{192,224},{224... | collective-permute-start | bytes 196616 | tf_op jit(solution)/shard_map/ppermute | solution.py:21
  58.5 6.3 %collective-permute-start.24 = (bf16[128,256]{1,0:T(8,128)(2,1)S(1)}, bf16[128,256]{1,0:T(8,128)(2,1)S(1)}, u32[]{:S(2)}, u32[]{:S(2)}) collective-permute-start(bf16[128,256]{1,0:T(8,128)(2,1)S(1)} %fusion.5), channel_id=1, source_target_pairs={{0,224},{32,0},{64,32},{96,64},{128,96},{160,128},{192,160},{224,1... | collective-permute-start | bytes 196616 | tf_op jit(solution)/shard_map/ppermute | solution.py:21
  62.0 5.6 %collective-permute-start.10 = (bf16[64,256]{1,0:T(8,128)(2,1)S(1)}, bf16[64,256]{1,0:T(8,128)(2,1)S(1)}, u32[]{:S(2)}, u32[]{:S(2)}) collective-permute-start(bf16[64,256]{1,0:T(8,128)(2,1)S(1)} %get-tuple-element.58), channel_id=1, source_target_pairs={{0,8},{8,16},{16,24},{24,0},{1,9},{9,17},{17,25},{25,1},{2,10},{10... | collective-permute-start | bytes 98312 | tf_op jit(solution)/shard_map/ppermute | solution.py:21
  62.1 5.5 %collective-permute-start.12 = (bf16[64,256]{1,0:T(8,128)(2,1)S(1)}, bf16[64,256]{1,0:T(8,128)(2,1)S(1)}, u32[]{:S(2)}, u32[]{:S(2)}) collective-permute-start(bf16[64,256]{1,0:T(8,128)(2,1)S(1)} %get-tuple-element.56), channel_id=1, source_target_pairs={{0,24},{8,0},{16,8},{24,16},{1,25},{9,1},{17,9},{25,17},{2,26},{10... | collective-permute-start | bytes 98312 | tf_op jit(solution)/shard_map/ppermute | solution.py:21
  64.8 4.4 %collective-permute-start.20 = (bf16[128,256]{1,0:T(8,128)(2,1)S(1)}, bf16[128,256]{1,0:T(8,128)(2,1)S(1)}, u32[]{:S(2)}, u32[]{:S(2)}) collective-permute-start(bf16[128,256]{1,0:T(8,128)(2,1)S(1)} %get-tuple-element.46), channel_id=1, source_target_pairs={{0,32},{32,64},{64,96},{96,128},{128,160},{160,192},{192,224},{224... | collective-permute-start | bytes 196616 | tf_op jit(solution)/shard_map/ppermute | solution.py:21
  64.9 4.7 %collective-permute-start.25 = (bf16[128,256]{1,0:T(8,128)(2,1)S(1)}, bf16[128,256]{1,0:T(8,128)(2,1)S(1)}, u32[]{:S(2)}, u32[]{:S(2)}) collective-permute-start(bf16[128,256]{1,0:T(8,128)(2,1)S(1)} %get-tuple-element.45), channel_id=1, source_target_pairs={{0,224},{32,0},{64,32},{96,64},{128,96},{160,128},{192,160},{224,1... | collective-permute-start | bytes 196616 | tf_op jit(solution)/shard_map/ppermute | solution.py:21
  67.6 3.2 %collective-permute-start.13 = (bf16[128,256]{1,0:T(8,128)(2,1)S(1)}, bf16[128,256]{1,0:T(8,128)(2,1)S(1)}, u32[]{:S(2)}, u32[]{:S(2)}) collective-permute-start(bf16[128,256]{1,0:T(8,128)(2,1)S(1)} %pad_maximum_fusion.5), channel_id=1, source_target_pairs={{0,24},{8,0},{16,8},{24,16},{1,25},{9,1},{17,9},{25,17},{2,26},{10... | collective-permute-start | bytes 196616 | tf_op jit(solution)/shard_map/ppermute | solution.py:21
  69.2 4.3 %collective-permute-start.11 = (bf16[128,256]{1,0:T(8,128)(2,1)S(1)}, bf16[128,256]{1,0:T(8,128)(2,1)S(1)}, u32[]{:S(2)}, u32[]{:S(2)}) collective-permute-start(bf16[128,256]{1,0:T(8,128)(2,1)S(1)} %pad_maximum_fusion.4), channel_id=1, source_target_pairs={{0,8},{8,16},{16,24},{24,0},{1,9},{9,17},{17,25},{25,1},{2,10},{10... | collective-permute-start | bytes 196616 | tf_op jit(solution)/shard_map/ppermute | solution.py:21
  69.3 4.6 %collective-permute-start.21 = (bf16[128,256]{1,0:T(8,128)(2,1)S(1)}, bf16[128,256]{1,0:T(8,128)(2,1)S(1)}, u32[]{:S(2)}, u32[]{:S(2)}) collective-permute-start(bf16[128,256]{1,0:T(8,128)(2,1)S(1)} %fusion.11), channel_id=1, source_target_pairs={{0,32},{32,64},{64,96},{96,128},{128,160},{160,192},{192,224},{224... | collective-permute-start | bytes 196616 | tf_op jit(solution)/shard_map/ppermute | solution.py:21
  90.9 28.0 %all-to-all-start = ((bf16[64,8,128]{2,1,0:T(8,128)(2,1)}), bf16[64,8,128]{2,1,0:T(8,128)(2,1)S(1)}, u32[]{:S(2)}, u32[]{:S(2)}) async-start(bf16[64,8,128]{2,1,0:T(8,128)(2,1)} %bitcast.25), calls=%async_computation | async-start | bytes 262144 | tf_op jit(solution)/shard_map/all_to_all | solution.py:222
  (3 other events, 15.0 us)
where the time goes:
time: 147 us
  starting transfers between devices  56.7 us (39%)
  Pallas kernels  27.2 us (19%)
  blocking collectives  26.3 us (18%)
  waiting for transfers between devices  25.6 us (17%)
  local copies, waits for them, and re-layouts  8.53 us (6%)
    ppermute x24, starting transfers between devices, shifted(): return lax.ppermute(x, axis, [(i, (i + step) % size) for i in range(size)])  36.4 us
    all_to_all x1, blocking collectives, routed(): got = lax.all_to_all(copies, (*DP, 'tensor'), 0, 0, tiled=True)  26.3 us
    pallas_call x1, Pallas kernels, precondition(): pl.pallas_call(body, out_shape=[jax.ShapeDtypeStruct(left.shape, F32), ja...  17 us
    all_to_all x1, starting transfers between devices, routed(): lax.all_to_all(directions.reshape(slots, 8, width), DP, 0, 0, tiled=True)  16.9 us
    ppermute x24, waiting for transfers between devices, shifted(): return lax.ppermute(x, axis, [(i, (i + step) % size) for i in range(size)])  13.1 us
    all_to_all x1, waiting for transfers between devices, routed(): lax.all_to_all(directions.reshape(slots, 8, width), DP, 0, 0, tiled=True)  10.5 us
    pallas_call x2, Pallas kernels, partial_sums(): pl.pallas_call(body, out_shape=[jax.ShapeDtypeStruct((c, rows, half_cols)...  8.71 us
    ppermute x1, starting transfers between devices, own_gradient(): acts_peer = lax.ppermute(activations, CORE, pair)  3.33 us
  transfers between devices with their start and end apart: 27, of which 11 were waited for; matrix products, arithmetic and copies ran while one was open for 5% of the time, Pallas kernels for 4%

commit v1 on v0

--- a/solution.py
+++ b/solution.py
@@ -16,36 +16,17 @@
 
 MOMENT_DECAY = 0.9
 RIDGE_SHARE = 0.0001
-def shifted(x, axis, step):
+def directed(x, axis):
     size = lax.axis_size(axis)
-    return lax.ppermute(x, axis, [(i, (i + step) % size) for i in range(size)])
-
-
-def partial_sums(counts, half_cols, acts, acts_peer, kvt, kvt_peer, acts_at, kvt_at):
-    rows = kvt.shape[0] // 4
-    total = sum(counts)
-
-    def body(acts_at_ref, kvt_at_ref, a_ref, ap_ref, k_ref, kp_ref, *out_refs):
-        n = 0
-        for count, out_ref in zip(counts, out_refs):
-            for i in range(count):
-                cols = pl.ds(pl.multiple_of(acts_at_ref[n] * half_cols, half_cols), half_cols)
-                lines = pl.ds(pl.multiple_of(kvt_at_ref[n] * rows, rows), rows)
-                summed = jnp.dot(k_ref[lines, :], a_ref[:, cols], preferred_element_type=F32)
-                summed += jnp.dot(kp_ref[lines, :], ap_ref[:, cols], preferred_element_type=F32)
-                out_ref[i] = summed.astype(BF16)
-                n += 1
-
-    vmem = pl.BlockSpec(memory_space=pltpu.VMEM)
-    smem = pl.BlockSpec(memory_space=pltpu.SMEM)
-    return pl.pallas_call(
-        body,
-        out_shape=[jax.ShapeDtypeStruct((c, rows, half_cols), BF16) for c in counts],
-        in_specs=[smem, smem, vmem, vmem, vmem, vmem],
-        out_specs=[vmem for _ in counts],
-        compiler_params=pltpu.CompilerParams(vmem_limit_bytes=48 * 1024 * 1024),
-        name="partial_sums",
-    )(acts_at, kvt_at, acts, acts_peer, kvt, kvt_peer)
+    pairs = []
+    for i in range(size):
+        for core, step in enumerate((1, -1)):
+            pairs.append((i * 2 + core, (i + step) % size * 2 + core))
+    return lax.ppermute(x, (axis, CORE), pairs)
+
+
+def swapped(x):
+    return lax.ppermute(x, CORE, [(0, 1), (1, 0)])
 
 
 def wide(*parts):
@@ -59,29 +40,74 @@
     return wide(*parts).astype(BF16)
 
 
-def reduce_ring8(v, axis, four_up, four_down, first_up, first_down):
-    up = first_up(v[3], shifted(four_up, axis, 1))
-    down = first_down(v[-3], shifted(four_down, axis, -1))
-    for d in (2, 1):
-        up = added(v[d], shifted(up, axis, 1))
-        down = added(v[-d], shifted(down, axis, -1))
-    return v[0], shifted(up, axis, 1), shifted(down, axis, -1)
-
-
-def reduce_ring4(v, axis, two_up, two_down, first_up, first_down):
-    up = first_up(v[1], shifted(two_up, axis, 1))
-    down = first_down(v[-1], shifted(two_down, axis, -1))
-    return v[0], shifted(up, axis, 1), shifted(down, axis, -1)
-
-
-def low_half(base, part):
-    h = part.shape[0]
-    return jnp.concatenate([added(base[:h], part), base[h:].astype(BF16)], axis=0)
-
-
-def high_half(base, part):
-    h = part.shape[0]
-    return jnp.concatenate([base[:h].astype(BF16), added(base[h:], part)], axis=0)
+def added_first(base, part):
+    n = part.shape[0]
+    return jnp.concatenate([added(base[:n], part), base[n:].astype(BF16)], axis=0)
+
+
+def group_a(k):
+    if k == 4:
+        return [(0, ("fix", 4), ("turn", j), d) for j in range(2) for d in range(2)]
+    return [(0, ("sign", k), ("turn", j), d) for j in range(4) for d in range(2)]
+
+
+def group_b(k):
+    if k == 2:
+        return [(1, ("turn", j), ("fix", 2), d) for j in range(4) for d in range(2)]
+    return [(1, ("turn", j), ("sign", 1), d) for j in range(8) for d in range(2)]
+
+
+KEPT_A = [(0, ("fix", 0), ("sign", 1), d) for d in range(2)]
+KEPT_A += [(0, ("fix", 0), ("fix", dy), 0) for dy in (2, 0)]
+KEPT_B = [(1, ("sign", k), ("fix", 0), d) for k in (3, 2, 1) for d in range(2)]
+KEPT_B += [(1, ("fix", dz), ("fix", 0), 0) for dz in (4, 0)]
+
+
+def offset(what, size, core):
+    kind, k = what
+    if kind == "sign":
+        return k + core * (size - 2 * k)
+    if kind == "turn":
+        return k + core * (size // 2)
+    return k
+
+
+def block_sums(groups, acts, kvt, block_rows, row_blocks, owner_table, before=None):
+    half_cols = block_rows // 2
+    rows = kvt.shape[0] // 4
+    held = F32 if before is None else BF16
+    col_blocks = 2
+
+    def body(owner_ref, a_ref, k_ref, *refs):
+        base_refs = [] if before is None else refs[: len(groups)]
+        out_refs = refs[len(base_refs) :]
+        z, y, core = (lax.axis_index(a) for a in DP)
+        for g, group in enumerate(groups):
+            for n, (half, dz, dy, flip) in enumerate(group):
+                to_z = (z + offset(dz, NZ, core)) % NZ
+                to_y = (y + offset(dy, NY, core)) % NY
+                to_core = core if flip == 0 else 1 - core
+                block = owner_ref[(to_z * NY + to_y) * 2 + to_core]
+                row = block // col_blocks % row_blocks
+                line = block // (row_blocks * col_blocks) * col_blocks + block % col_blocks
+                cols = pl.ds(pl.multiple_of((row * 2 + half) * half_cols, half_cols), half_cols)
+                lines = pl.ds(pl.multiple_of(line * rows, rows), rows)
+                summed = jnp.dot(k_ref[lines, :], a_ref[:, cols], preferred_element_type=F32)
+                if before is not None:
+                    summed = base_refs[g][n] + summed
+                out_refs[g][n] = summed.astype(held)
+
+    vmem = pl.BlockSpec(memory_space=pltpu.VMEM)
+    smem = pl.BlockSpec(memory_space=pltpu.SMEM)
+    inputs = [] if before is None else list(before)
+    return pl.pallas_call(
+        body,
+        out_shape=[jax.ShapeDtypeStruct((len(g), rows, half_cols), held) for g in groups],
+        in_specs=[smem, vmem, vmem] + [vmem] * len(inputs),
+        out_specs=[vmem for _ in groups],
+        compiler_params=pltpu.CompilerParams(vmem_limit_bytes=40 * 1024 * 1024),
+        name="block_sums",
+    )(owner_table, acts, kvt, *inputs)
 
 
 def transposed_sum(refs):
@@ -232,62 +258,56 @@
     return placed(got.reshape(slots, shards, 8, width), shards)
 
 
-def own_gradient(activations, key_value_grads, owner_table, block_rows, block_cols):
+def own_gradient(activations, key_value_grads, owner_table, block_rows):
     tokens, features = activations.shape
-    half_cols = block_rows // 2
+    row_blocks = features // block_rows
     kvt = key_value_grads.reshape(tokens, -1).T
-    pair = [(0, 1), (1, 0)]
-    acts_peer = lax.ppermute(activations, CORE, pair)
-    kvt_peer = lax.ppermute(kvt, CORE, pair)
-
-    z, y, core = (lax.axis_index(a) for a in DP)
-    col_blocks = key_value_grads.shape[2] // block_cols
-    row_blocks = features // block_rows
-
-    dz_all = jnp.arange(NZ, dtype=jnp.int32)
-    dy_all = jnp.arange(NY, dtype=jnp.int32)
-    slots = ((z + dz_all[:, None]) % NZ * NY + (y + dy_all[None, :]) % NY) * 2 + core
-    blocks = jnp.take(owner_table, slots)
-    projection = blocks // (row_blocks * col_blocks)
-    row = blocks % (row_blocks * col_blocks) // col_blocks
-    line = projection * col_blocks + blocks % col_blocks
-
-    def listing(pairs):
-        dzs = jnp.array([p[0] % NZ for p in pairs], jnp.int32)
-        dys = jnp.array([p[1] % NY for p in pairs], jnp.int32)
-        halves = jnp.array([p[2] for p in pairs], jnp.int32)
-        at = dzs * NY + dys
-        return jnp.take(row.reshape(-1), at) * 2 + halves, jnp.take(line.reshape(-1), at)
-
-    def sums(groups):
-        a_at, k_at = listing([p for g in groups for p in g])
-        counts = [len(g) for g in groups]
-        return partial_sums(counts, half_cols, activations, acts_peer, kvt, kvt_peer, a_at, k_at)
-
-    first = [
-        [(4, dy, 0) for dy in (0, 1)],
-        [(4, dy, 0) for dy in (2, 3)],
-        [(dz, 2, 1) for dz in (0, 1, 2, 3)],
-        [(dz, 2, 1) for dz in (4, 5, 6, 7)],
-    ]
-    a_up, a_down, b_up, b_down = sums(first)
-    az = (3, -3, 2, -2, 1, -1, 0)
-    by = (1, -1, 0)
-    rest = [[(dz, dy, 0) for dy in range(NY)] for dz in az]
-    rest += [[(dz, dy, 1) for dz in range(NZ)] for dy in by]
-    later = sums(rest)
-    va = dict(zip(az, later[: len(az)]))
-    vb = dict(zip(by, later[len(az) :]))
-
-    ta = wide(*reduce_ring8(va, Z, a_up, a_down, low_half, high_half))
-    tb = wide(*reduce_ring4(vb, Y, b_up, b_down, low_half, high_half))
-
-    h = block_cols // 2
-    two = ta[2].astype(BF16)
-    ga = reduce_ring4({0: ta[0], 1: ta[1], -1: ta[3]}, Y, two[:h], two[h:], low_half, high_half)
-    four = tb[4].astype(BF16)
-    vz = {d: tb[d % NZ] for d in range(-3, 4)}
-    gb = reduce_ring8(vz, Z, four[:h], four[h:], low_half, high_half)
+    acts_peer = swapped(activations)
+    kvt_peer = swapped(kvt)
+
+    first = [group_a(4), group_b(2)]
+    rest = [group_a(3), group_b(1), group_a(2), group_a(1), KEPT_A, KEPT_B]
+    sizes = (block_rows, row_blocks, owner_table)
+    own = block_sums(first + rest, activations, kvt, *sizes)
+    a4, b2 = block_sums(first, acts_peer, kvt_peer, *sizes, before=own[:2])
+    a3, b1, a2, a1, a0, b0 = block_sums(rest, acts_peer, kvt_peer, *sizes, before=own[2:])
+
+    run = added_first(a3, directed(a4, Z))
+    run = added(a2, directed(run, Z))
+    run = added(a1, directed(run, Z))
+    run = directed(run, Z)
+    run = run.reshape(2, 2, 2, *run.shape[1:])
+    lo, hi = run[0], run[1]
+    core = lax.axis_index(CORE)
+    even_mine = jnp.where(core == 0, lo[0], hi[0])
+    even_far = jnp.where(core == 0, hi[0], lo[0])
+    odd_mine = lo[1]
+    odd_away = hi[1]
+    give = jnp.stack([odd_away[1], odd_away[0], even_far[1], even_mine[1]])
+    got = swapped(give)
+    keep = jnp.stack([odd_mine[0], odd_mine[1], even_far[0], even_mine[0]])
+    kept = wide(a0, keep, got)
+    near = added_first(kept[:2], directed(kept[2:3].astype(BF16), Y))
+    near = directed(near, Y)
+    ga = [kept[3], near[0], swapped(near[1])]
+
+    run = added_first(b1, directed(b2, Y))
+    run = directed(run, Y)
+    run = run.reshape(2, 4, 2, *run.shape[1:])
+    lo, hi = run[0], run[1]
+    mine = jnp.where(core == 0, lo[0], hi[0])
+    far = jnp.where(core == 0, hi[0], lo[0])
+    toward = [jnp.where(core == 0, lo[k], lo[4 - k]) for k in (3, 2, 1)]
+    away = [jnp.where(core == 0, hi[4 - k], hi[k]) for k in (3, 2, 1)]
+    give = jnp.stack([w[d] for w in away for d in (1, 0)] + [far[1], mine[1]])
+    keep = jnp.stack([w[d] for w in toward for d in (0, 1)] + [far[0], mine[0]])
+    got = swapped(give)
+    kept = wide(b0, keep, got)
+    near = added_first(kept[0:2], directed(kept[6:7].astype(BF16), Z))
+    near = added(kept[2:4], directed(near, Z))
+    near = added(kept[4:6], directed(near, Z))
+    near = directed(near, Z)
+    gb = [kept[7], near[0], swapped(near[1])]
     return ga, gb
 
 
@@ -298,7 +318,7 @@
     col_blocks = key_value_grads.shape[2] // cols_block
     inverse_tokens = 1.0 / (activations.shape[0] * lax.axis_size(DP))
 
-    ga, gb = own_gradient(activations, key_value_grads, owner_table, rows_block, cols_block)
+    ga, gb = own_gradient(activations, key_value_grads, owner_table, rows_block)
     left_new, right_new, directions = precondition(
         ga, gb, left_factors[0, 0], right_factors[0, 0], inverse_tokens
     )

time: 147 us -> 151 us (1.027)
  waiting for transfers between devices: 25.6 us -> 33.6 us
  local copies, waits for them, and re-layouts: 8.53 us -> 4.7 us
  starting transfers between devices: 56.7 us -> 54.3 us
  other arithmetic: 1.37 us -> 3.3 us
    ppermute x26 -> x18, waiting for transfers between devices: 15.1 us -> 23 us  [the longest x12 19.9 us: directed(): return lax.ppermute(x, (axis, CORE), pairs)]
    all_to_all x1, starting transfers between devices: 16.9 us -> 9.38 us  [routed(): lax.all_to_all(directions.reshape(slots, 8, width), DP, 0, 0, tiled=True)]
    ppermute x26 -> x18, starting transfers between devices: 39.8 us -> 44.9 us  [the longest x12 27.2 us: directed(): return lax.ppermute(x, (axis, CORE), pairs)]
    gather x5 -> x0, local copies, waits for them, and re-layouts: 4.23 us -> none  [the longest x2 1.44 us: listing(): jnp.take(line.reshape(-1), at)]
    convert_element_type x13 -> x8, other arithmetic: 0.56 us -> 2.41 us  [added(): return wide(*parts).astype(BF16)]
    unnamed x17 -> x19, local copies, waits for them, and re-layouts: 3.33 us -> 4.01 us
    pallas_call x2 -> x3, Pallas kernels: 8.71 us -> 8.52 us  [block_sums(): pl.pallas_call(body, out_shape=[jax.ShapeDtypeStruct((len(g), rows, half_...]
  transfers between devices with their start and end apart: 27 -> 19, of which waited for: 11 -> 9; matrix products, arithmetic and copies ran while one was open for 5% -> 3% of each run, Pallas kernels for 4% -> 4%
where the time goes in v1:
time: 151 us
  starting transfers between devices  54.3 us (36%)
  waiting for transfers between devices  33.6 us (22%)
  Pallas kernels  27 us (18%)
  blocking collectives  26.3 us (17%)
  local copies, waits for them, and re-layouts  4.7 us (3%)
  other arithmetic  3.3 us (2%)
    ppermute x12, starting transfers between devices, directed(): return lax.ppermute(x, (axis, CORE), pairs)  27.2 us
    all_to_all x1, blocking collectives, routed(): got = lax.all_to_all(copies, (*DP, 'tensor'), 0, 0, tiled=True)  26.3 us
    ppermute x12, waiting for transfers between devices, directed(): return lax.ppermute(x, (axis, CORE), pairs)  19.9 us
    ppermute x6, starting transfers between devices, swapped(): return lax.ppermute(x, CORE, [(0, 1), (1, 0)])  17.7 us
    pallas_call x1, Pallas kernels, precondition(): pl.pallas_call(body, out_shape=[jax.ShapeDtypeStruct(left.shape, F32), ja...  17 us
    all_to_all x1, waiting for transfers between devices, routed(): lax.all_to_all(directions.reshape(slots, 8, width), DP, 0, 0, tiled=True)  10.5 us
    all_to_all x1, starting transfers between devices, routed(): lax.all_to_all(directions.reshape(slots, 8, width), DP, 0, 0, tiled=True)  9.38 us
    pallas_call x3, Pallas kernels, block_sums(): pl.pallas_call(body, out_shape=[jax.ShapeDtypeStruct((len(g), rows, half_...  8.52 us
  transfers between devices with their start and end apart: 19, of which 9 were waited for; matrix products, arithmetic and copies ran while one was open for 3% of the time, Pallas kernels for 4%

profile of v1, /device:TPU:1, one launch (start us, length us, event | category | flops | bytes accessed | tf_op | source)
XLA Modules:
  0.0 150.5 jit_solution(1456762299184377600)
XLA Ops:
  0.6 3.3 %collective-permute-start = (bf16[256,8192]{1,0:T(8,128)(2,1)}, bf16[256,8192]{1,0:T(8,128)(2,1)}, u32[]{:S(2)}, u32[]{:S(2)}) collective-permute-start(bf16[256,8192]{1,0:T(8,128)(2,1)} %a_ref.1), channel_id=1, source_target_pairs={{0,4},{4,0},{1,5},{5,1},{2,6},{6,2},{3,7},{7,3},{8,12},{12,8},{9,1... | collective-permute-start | bytes 12582920 | tf_op jit(solution)/shard_map/ppermute | solution.py:29
  4.0 1.1 copy.10
  5.2 2.2 %copy-done = bf16[256,8192]{1,0:T(8,128)(2,1)S(1)} copy-done((bf16[256,8192]{1,0:T(8,128)(2,1)S(1)}, bf16[256,8192]{1,0:T(8,128)(2,1)}, u32[]{:S(2)}) %copy-start) | copy-done | bytes 4194328
  8.0 2.1 %block_sums.3 = (f32[4,128,256]{2,1,0:T(8,128)S(1)}, f32[8,128,256]{2,1,0:T(8,128)S(1)}, f32[8,128,256]{2,1,0:T(8,128)S(1)}, f32[16,128,256]{2,1,0:T(8,128)S(1)}...) custom-call(s32[64]{0:T(128)S(1)} %copy-done.3, ...), custom_call_target="tpu_custom_call" | custom-call | tf_op jit(solution)/shard_map/block_sums/pallas_call | solution.py:103
  10.1 1.0 collective-permute-done.1.k_ref
  11.1 2.7 %block_sums.5 = (bf16[4,128,256]{2,1,0:T(8,128)(2,1)S(1)}, bf16[8,128,256]{2,1,0:T(8,128)(2,1)S(1)}) custom-call(s32[64]{0:T(128)S(1)} %copy-done.3, bf16[256,8192]{1,0:T(8,128)(2,1)} %collective-permute-done.a_ref, bf16[512,256]{1,0:T(8,128)(2,1)S(1)} %collective-permute-done.1.k_ref, f32[4,128,256]{2,1,0:T(8,128)S(1)} %get-tuple-element.32.refs_0_, ...), custom_call_target="tpu_custom_call" | custom-call | tf_op jit(solution)/shard_map/block_sums/pallas_call | solution.py:103
  13.8 3.9 %collective-permute-start.2 = (bf16[4,128,256]{2,1,0:T(8,128)(2,1)S(1)}, bf16[4,128,256]{2,1,0:T(8,128)(2,1)S(1)}, u32[]{:S(2)}, u32[]{:S(2)}) collective-permute-start(bf16[4,128,256]{2,1,0:T(8,128)(2,1)S(1)} %get-tuple-element.34), channel_id=1, source_target_pairs={{0,32},{4,228},{32,64},{36,4},{64,96},{68,36},{96,128},{100,68},{1... | collective-permute-start | bytes 786440 | tf_op jit(solution)/shard_map/ppermute | solution.py:25
  17.7 2.7 %collective-permute-start.10 = (bf16[8,128,256]{2,1,0:T(8,128)(2,1)S(1)}, bf16[8,128,256]{2,1,0:T(8,128)(2,1)S(1)}, u32[]{:S(2)}, u32[]{:S(2)}) collective-permute-start(bf16[8,128,256]{2,1,0:T(8,128)(2,1)S(1)} %get-tuple-element.37), channel_id=1, source_target_pairs={{0,8},{4,28},{8,16},{12,4},{16,24},{20,12},{24,0},{28,20},{1,9},{5... | collective-permute-start | bytes 1572872 | tf_op jit(solution)/shard_map/ppermute | solution.py:25
  20.5 3.7 %block_sums.4 = (bf16[8,128,256]{2,1,0:T(8,128)(2,1)S(1)}, bf16[16,128,256]{2,1,0:T(8,128)(2,1)S(1)}, bf16[8,128,256]{2,1,0:T(8,128)(2,1)S(1)}, bf16[8,128,256]{...) custom-call(s32[64]{0:T(128)S(1)} %copy-done.3, ...), custom_call_target="tpu_custom_call" | custom-call | tf_op jit(solution)/shard_map/block_sums/pallas_call | solution.py:103
  25.2 1.4 collective-permute-done.10
  26.8 3.2 %collective-permute-start.11 = (bf16[16,128,256]{2,1,0:T(8,128)(2,1)S(1)}, bf16[16,128,256]{2,1,0:T(8,128)(2,1)S(1)}, u32[]{:S(2)}, u32[]{:S(2)}) collective-permute-start(bf16[16,128,256]{2,1,0:T(8,128)(2,1)S(1)} %pad_maximum_fusion), channel_id=1, source_target_pairs={{0,8},{4,28},{8,16},{12,4},{16,24},{20,12},{24,0},{28,20},{1,9},{5... | collective-permute-start | bytes 3145736 | tf_op jit(solution)/shard_map/ppermute | solution.py:25
  30.0 2.7 %collective-permute-done.3 = bf16[8,128,256]{2,1,0:T(8,128)(2,1)S(1)} collective-permute-done((bf16[8,128,256]{2,1,0:T(8,128)(2,1)S(1)}, bf16[8,128,256]{2,1,0:T(8,128)(2,1)S(1)}, u32[]{:S(2)}, u32[]{:S(2)}) %collective-permute-start.3) | collective-permute-done | bytes 524320 | tf_op jit(solution)/shard_map/ppermute | solution.py:25
  33.7 2.0 %collective-permute-start.4 = (bf16[8,128,256]{2,1,0:T(8,128)(2,1)}, bf16[8,128,256]{2,1,0:T(8,128)(2,1)}, u32[]{:S(2)}, u32[]{:S(2)}) collective-permute-start(bf16[8,128,256]{2,1,0:T(8,128)(2,1)} %add_convert_fusion.2), channel_id=1, source_target_pairs={{0,32},{4,228},{32,64},{36,4},{64,96},{68,36},{96,128},{100,68},{1... | collective-permute-start | bytes 1572872 | tf_op jit(solution)/shard_map/ppermute | solution.py:25
  35.7 6.7 %collective-permute-done.4 = bf16[8,128,256]{2,1,0:T(8,128)(2,1)} collective-permute-done((bf16[8,128,256]{2,1,0:T(8,128)(2,1)}, bf16[8,128,256]{2,1,0:T(8,128)(2,1)}, u32[]{:S(2)}, u32[]{:S(2)}) %collective-permute-start.4) | collective-permute-done | bytes 524320 | tf_op jit(solution)/shard_map/ppermute | solution.py:25
  42.3 1.2 add_convert_fusion.1
  43.5 2.9 %collective-permute-start.5 = (bf16[8,128,256]{2,1,0:T(8,128)(2,1)S(1)}, bf16[8,128,256]{2,1,0:T(8,128)(2,1)S(1)}, u32[]{:S(2)}, u32[]{:S(2)}) collective-permute-start(bf16[8,128,256]{2,1,0:T(8,128)(2,1)S(1)} %add_convert_fusion.1), channel_id=1, source_target_pairs={{0,32},{4,228},{32,64},{36,4},{64,96},{68,36},{96,128},{100,68},{1... | collective-permute-start | bytes 1572872 | tf_op jit(solution)/shard_map/ppermute | solution.py:25
  46.5 6.1 %collective-permute-done.5 = bf16[8,128,256]{2,1,0:T(8,128)(2,1)S(1)} collective-permute-done((bf16[8,128,256]{2,1,0:T(8,128)(2,1)S(1)}, bf16[8,128,256]{2,1,0:T(8,128)(2,1)S(1)}, u32[]{:S(2)}, u32[]{:S(2)}) %collective-permute-start.5) | collective-permute-done | bytes 524320 | tf_op jit(solution)/shard_map/ppermute | solution.py:25
  52.9 4.1 %collective-permute-start.12 = (bf16[8,128,256]{2,1,0:T(8,128)(2,1)S(1)}, bf16[8,128,256]{2,1,0:T(8,128)(2,1)S(1)}, u32[]{:S(2)}, u32[]{:S(2)}) collective-permute-start(bf16[8,128,256]{2,1,0:T(8,128)(2,1)S(1)} %get-tuple-element.66), channel_id=1, source_target_pairs={{0,4},{4,0},{1,5},{5,1},{2,6},{6,2},{3,7},{7,3},{8,12},{12,8},{9,1... | collective-permute-start | bytes 1572872 | tf_op jit(solution)/shard_map/ppermute | solution.py:29
  57.2 1.3 collective-permute-done.12
  59.2 3.0 %collective-permute-done.13 = bf16[1,128,256]{2,1,0:T(8,128)(2,1)S(1)} collective-permute-done((bf16[1,128,256]{2,1,0:T(8,128)(2,1)S(1)}, bf16[1,128,256]{2,1,0:T(8,128)(2,1)S(1)}, u32[]{:S(2)}, u32[]{:S(2)}) %collective-permute-start.13) | collective-permute-done | bytes 65568 | tf_op jit(solution)/shard_map/ppermute | solution.py:25
  62.2 1.3 collective-permute-start.14
  63.5 2.8 %collective-permute-start.7 = (bf16[1,128,256]{2,1,0:T(8,128)(2,1)S(1)}, bf16[1,128,256]{2,1,0:T(8,128)(2,1)S(1)}, u32[]{:S(2)}, u32[]{:S(2)}) collective-permute-start(bf16[1,128,256]{2,1,0:T(8,128)(2,1)S(1)} %get-tuple-element.61), channel_id=1, source_target_pairs={{0,8},{4,28},{8,16},{12,4},{16,24},{20,12},{24,0},{28,20},{1,9},{5... | collective-permute-start | bytes 196616 | tf_op jit(solution)/shard_map/ppermute | solution.py:25
  66.4 2.3 %collective-permute-start.15 = (bf16[2,128,256]{2,1,0:T(8,128)(2,1)S(1)}, bf16[2,128,256]{2,1,0:T(8,128)(2,1)S(1)}, u32[]{:S(2)}, u32[]{:S(2)}) collective-permute-start(bf16[2,128,256]{2,1,0:T(8,128)(2,1)S(1)} %fusion.4), channel_id=1, source_target_pairs={{0,32},{4,228},{32,64},{36,4},{64,96},{68,36},{96,128},{100,68},{1... | collective-permute-start | bytes 393224 | tf_op jit(solution)/shard_map/ppermute | solution.py:25
  68.7 2.8 %collective-permute-start.8 = (bf16[2,128,256]{2,1,0:T(8,128)(2,1)S(1)}, bf16[2,128,256]{2,1,0:T(8,128)(2,1)S(1)}, u32[]{:S(2)}, u32[]{:S(2)}) collective-permute-start(bf16[2,128,256]{2,1,0:T(8,128)(2,1)S(1)} %pad_maximum_fusion.3), channel_id=1, source_target_pairs={{0,8},{4,28},{8,16},{12,4},{16,24},{20,12},{24,0},{28,20},{1,9},{5... | collective-permute-start | bytes 393224 | tf_op jit(solution)/shard_map/ppermute | solution.py:25
  71.5 2.2 %collective-permute-start.16 = (bf16[2,128,256]{2,1,0:T(8,128)(2,1)S(1)}, bf16[2,128,256]{2,1,0:T(8,128)(2,1)S(1)}, u32[]{:S(2)}, u32[]{:S(2)}) collective-permute-start(bf16[2,128,256]{2,1,0:T(8,128)(2,1)S(1)} %fusion.5), channel_id=1, source_target_pairs={{0,32},{4,228},{32,64},{36,4},{64,96},{68,36},{96,128},{100,68},{1... | collective-permute-start | bytes 393224 | tf_op jit(solution)/shard_map/ppermute | solution.py:25
  73.8 4.0 %collective-permute-start.9 = (bf16[128,256]{1,0:T(8,128)(2,1)S(1)}, bf16[128,256]{1,0:T(8,128)(2,1)S(1)}, u32[]{:S(2)}, u32[]{:S(2)}) collective-permute-start(bf16[128,256]{1,0:T(8,128)(2,1)S(1)} %get-tuple-element.69), channel_id=1, source_target_pairs={{0,4},{4,0},{1,5},{5,1},{2,6},{6,2},{3,7},{7,3},{8,12},{12,8},{9,1... | collective-permute-start | bytes 196616 | tf_op jit(solution)/shard_map/ppermute | solution.py:29
  77.8 6.1 %collective-permute-start.17 = (bf16[128,256]{1,0:T(8,128)(2,1)S(1)}, bf16[128,256]{1,0:T(8,128)(2,1)S(1)}, u32[]{:S(2)}, u32[]{:S(2)}) collective-permute-start(bf16[128,256]{1,0:T(8,128)(2,1)S(1)} %get-tuple-element.63), channel_id=1, source_target_pairs={{0,4},{4,0},{1,5},{5,1},{2,6},{6,2},{3,7},{7,3},{8,12},{12,8},{9,1... | collective-permute-start | bytes 196616 | tf_op jit(solution)/shard_map/ppermute | solution.py:29
  84.8 17.0 %precondition.1 = (f32[512,512]{1,0:T(8,128)}, f32[128,128]{1,0:T(8,128)}, bf16[512,128]{1,0:T(8,128)(2,1)}) custom-call(f32[128,256]{1,0:T(8,128)S(1)} %get-tuple-element.55.refs_0_, bf16[128,256]{1,0:T(8,128)(2,1)S(1)} %get-tuple-element.70.refs_1_, bf16[128,256]{1,0:T(8,128)(2,1)S(1)} %collective-permute-done.9.refs_2_, ...), custom_call_target="tpu_custom_call" | custom-call | tf_op jit(solution)/shard_map/precondition/pallas_call | solution.py:203
  101.8 9.4 %all-to-all-start = ((bf16[64,8,128]{2,1,0:T(8,128)(2,1)}), bf16[64,8,128]{2,1,0:T(8,128)(2,1)S(1)}, u32[]{:S(2)}, u32[]{:S(2)}) async-start(bf16[64,8,128]{2,1,0:T(8,128)(2,1)} %bitcast.13), calls=%async_computation | async-start | bytes 262144 | tf_op jit(solution)/shard_map/all_to_all | solution.py:248
  111.8 10.5 %all-to-all-done = bf16[64,8,128]{2,1,0:T(8,128)(2,1)S(1)} async-done(((bf16[64,8,128]{2,1,0:T(8,128)(2,1)}), bf16[64,8,128]{2,1,0:T(8,128)(2,1)S(1)}, u32[]{:S(2)}, u32[]{:S(2)}) %all-to-all-start) | async-done | bytes 131104 | tf_op jit(solution)/shard_map/all_to_all | solution.py:248
  122.8 26.3 %all_to_all.10 = bf16[256,8,128]{2,1,0:T(8,128)(2,1)S(1)} all-to-all(bf16[256,8,128]{2,1,0:T(8,128)(2,1)S(1)} %bitcast.32), channel_id=1, replica_groups=mesh['dp_0'=8,'dp_1'=4,'dp_2'=2,'tensor'=4] {'dp_0','dp_1','dp_2','tensor'}, dimensions={0} | all-to-all | bytes 1048576 | tf_op jit(solution)/shard_map/all_to_all | solution.py:257
  149.1 1.5 placed.1
  (67 shorter events, 6.1 us)
Async XLA Ops:
  0.6 10.5 %collective-permute-start = (bf16[256,8192]{1,0:T(8,128)(2,1)}, bf16[256,8192]{1,0:T(8,128)(2,1)}, u32[]{:S(2)}, u32[]{:S(2)}) collective-permute-start(bf16[256,8192]{1,0:T(8,128)(2,1)} %a_ref.1), channel_id=1, source_target_pairs={{0,4},{4,0},{1,5},{5,1},{2,6},{6,2},{3,7},{7,3},{8,12},{12,8},{9,1... | collective-permute-start | bytes 12582920 | tf_op jit(solution)/shard_map/ppermute | solution.py:29
  5.1 6.1 %collective-permute-start.1 = (bf16[512,256]{1,0:T(8,128)(2,1)S(1)}, bf16[512,256]{1,0:T(8,128)(2,1)S(1)}, u32[]{:S(2)}, u32[]{:S(2)}) collective-permute-start(bf16[512,256]{1,0:T(8,128)(2,1)S(1)} %bitcast.28), channel_id=1, source_target_pairs={{0,4},{4,0},{1,5},{5,1},{2,6},{6,2},{3,7},{7,3},{8,12},{12,8},{9,1... | collective-permute-start | bytes 786440 | tf_op jit(solution)/shard_map/ppermute | solution.py:29
  5.2 2.2 %copy-start = (bf16[256,8192]{1,0:T(8,128)(2,1)S(1)}, bf16[256,8192]{1,0:T(8,128)(2,1)}, u32[]{:S(2)}) copy-start(bf16[256,8192]{1,0:T(8,128)(2,1)} %a_ref.1) | copy-start | bytes 12582916
  7.4 0.7 copy-start.3
  13.8 10.4 %collective-permute-start.2 = (bf16[4,128,256]{2,1,0:T(8,128)(2,1)S(1)}, bf16[4,128,256]{2,1,0:T(8,128)(2,1)S(1)}, u32[]{:S(2)}, u32[]{:S(2)}) collective-permute-start(bf16[4,128,256]{2,1,0:T(8,128)(2,1)S(1)} %get-tuple-element.34), channel_id=1, source_target_pairs={{0,32},{4,228},{32,64},{36,4},{64,96},{68,36},{96,128},{100,68},{1... | collective-permute-start | bytes 786440 | tf_op jit(solution)/shard_map/ppermute | solution.py:25
  17.7 8.9 %collective-permute-start.10 = (bf16[8,128,256]{2,1,0:T(8,128)(2,1)S(1)}, bf16[8,128,256]{2,1,0:T(8,128)(2,1)S(1)}, u32[]{:S(2)}, u32[]{:S(2)}) collective-permute-start(bf16[8,128,256]{2,1,0:T(8,128)(2,1)S(1)} %get-tuple-element.37), channel_id=1, source_target_pairs={{0,8},{4,28},{8,16},{12,4},{16,24},{20,12},{24,0},{28,20},{1,9},{5... | collective-permute-start | bytes 1572872 | tf_op jit(solution)/shard_map/ppermute | solution.py:25
  24.4 8.4 %collective-permute-start.3 = (bf16[8,128,256]{2,1,0:T(8,128)(2,1)S(1)}, bf16[8,128,256]{2,1,0:T(8,128)(2,1)S(1)}, u32[]{:S(2)}, u32[]{:S(2)}) collective-permute-start(bf16[8,128,256]{2,1,0:T(8,128)(2,1)S(1)} %pad_maximum_fusion.1), channel_id=1, source_target_pairs={{0,32},{4,228},{32,64},{36,4},{64,96},{68,36},{96,128},{100,68},{1... | collective-permute-start | bytes 1572872 | tf_op jit(solution)/shard_map/ppermute | solution.py:25
  26.8 19.6 %collective-permute-start.11 = (bf16[16,128,256]{2,1,0:T(8,128)(2,1)S(1)}, bf16[16,128,256]{2,1,0:T(8,128)(2,1)S(1)}, u32[]{:S(2)}, u32[]{:S(2)}) collective-permute-start(bf16[16,128,256]{2,1,0:T(8,128)(2,1)S(1)} %pad_maximum_fusion), channel_id=1, source_target_pairs={{0,8},{4,28},{8,16},{12,4},{16,24},{20,12},{24,0},{28,20},{1,9},{5... | collective-permute-start | bytes 3145736 | tf_op jit(solution)/shard_map/ppermute | solution.py:25
  33.7 8.6 %collective-permute-start.4 = (bf16[8,128,256]{2,1,0:T(8,128)(2,1)}, bf16[8,128,256]{2,1,0:T(8,128)(2,1)}, u32[]{:S(2)}, u32[]{:S(2)}) collective-permute-start(bf16[8,128,256]{2,1,0:T(8,128)(2,1)} %add_convert_fusion.2), channel_id=1, source_target_pairs={{0,32},{4,228},{32,64},{36,4},{64,96},{68,36},{96,128},{100,68},{1... | collective-permute-start | bytes 1572872 | tf_op jit(solution)/shard_map/ppermute | solution.py:25
  43.5 9.1 %collective-permute-start.5 = (bf16[8,128,256]{2,1,0:T(8,128)(2,1)S(1)}, bf16[8,128,256]{2,1,0:T(8,128)(2,1)S(1)}, u32[]{:S(2)}, u32[]{:S(2)}) collective-permute-start(bf16[8,128,256]{2,1,0:T(8,128)(2,1)S(1)} %add_convert_fusion.1), channel_id=1, source_target_pairs={{0,32},{4,228},{32,64},{36,4},{64,96},{68,36},{96,128},{100,68},{1... | collective-permute-start | bytes 1572872 | tf_op jit(solution)/shard_map/ppermute | solution.py:25
  52.9 5.6 %collective-permute-start.12 = (bf16[8,128,256]{2,1,0:T(8,128)(2,1)S(1)}, bf16[8,128,256]{2,1,0:T(8,128)(2,1)S(1)}, u32[]{:S(2)}, u32[]{:S(2)}) collective-permute-start(bf16[8,128,256]{2,1,0:T(8,128)(2,1)S(1)} %get-tuple-element.66), channel_id=1, source_target_pairs={{0,4},{4,0},{1,5},{5,1},{2,6},{6,2},{3,7},{7,3},{8,12},{12,8},{9,1... | collective-permute-start | bytes 1572872 | tf_op jit(solution)/shard_map/ppermute | solution.py:29
  57.1 1.9 %collective-permute-start.6 = (bf16[4,128,256]{2,1,0:T(8,128)(2,1)S(1)}, bf16[4,128,256]{2,1,0:T(8,128)(2,1)S(1)}, u32[]{:S(2)}, u32[]{:S(2)}) collective-permute-start(bf16[4,128,256]{2,1,0:T(8,128)(2,1)S(1)} %pad_maximum_fusion.2), channel_id=1, source_target_pairs={{0,4},{4,0},{1,5},{5,1},{2,6},{6,2},{3,7},{7,3},{8,12},{12,8},{9,1... | collective-permute-start | bytes 786440 | tf_op jit(solution)/shard_map/ppermute | solution.py:29
  58.6 26.2 %copy-start.1 = (f32[1,1,512,512]{3,2,1,0:T(8,128)S(1)}, f32[1,1,512,512]{3,2,1,0:T(8,128)}, u32[]{:S(2)}) copy-start(f32[1,1,512,512]{3,2,1,0:T(8,128)} %param.8) | copy-start | bytes 3145732
  58.6 26.2 %copy-start.2 = (f32[1,1,128,128]{3,2,1,0:T(8,128)S(1)}, f32[1,1,128,128]{3,2,1,0:T(8,128)}, u32[]{:S(2)}) copy-start(f32[1,1,128,128]{3,2,1,0:T(8,128)} %param.9) | copy-start | bytes 196612
  58.8 52.5 %copy-start.4 = (s32[64]{0:T(128)S(1)}, s32[64]{0:T(128)}, u32[]{:S(2)}) copy-start(s32[64]{0:T(128)} %owner_ref.5) | copy-start | bytes 772
  58.8 3.4 %collective-permute-start.13 = (bf16[1,128,256]{2,1,0:T(8,128)(2,1)S(1)}, bf16[1,128,256]{2,1,0:T(8,128)(2,1)S(1)}, u32[]{:S(2)}, u32[]{:S(2)}) collective-permute-start(bf16[1,128,256]{2,1,0:T(8,128)(2,1)S(1)} %get-tuple-element.52), channel_id=1, source_target_pairs={{0,32},{4,228},{32,64},{36,4},{64,96},{68,36},{96,128},{100,68},{1... | collective-permute-start | bytes 196616 | tf_op jit(solution)/shard_map/ppermute | solution.py:25
  62.2 4.1 %collective-permute-start.14 = (bf16[2,128,256]{2,1,0:T(8,128)(2,1)S(1)}, bf16[2,128,256]{2,1,0:T(8,128)(2,1)S(1)}, u32[]{:S(2)}, u32[]{:S(2)}) collective-permute-start(bf16[2,128,256]{2,1,0:T(8,128)(2,1)S(1)} %pad_maximum_fusion.4), channel_id=1, source_target_pairs={{0,32},{4,228},{32,64},{36,4},{64,96},{68,36},{96,128},{100,68},{1... | collective-permute-start | bytes 393224 | tf_op jit(solution)/shard_map/ppermute | solution.py:25
  63.5 5.1 %collective-permute-start.7 = (bf16[1,128,256]{2,1,0:T(8,128)(2,1)S(1)}, bf16[1,128,256]{2,1,0:T(8,128)(2,1)S(1)}, u32[]{:S(2)}, u32[]{:S(2)}) collective-permute-start(bf16[1,128,256]{2,1,0:T(8,128)(2,1)S(1)} %get-tuple-element.61), channel_id=1, source_target_pairs={{0,8},{4,28},{8,16},{12,4},{16,24},{20,12},{24,0},{28,20},{1,9},{5... | collective-permute-start | bytes 196616 | tf_op jit(solution)/shard_map/ppermute | solution.py:25
  66.4 5.1 %collective-permute-start.15 = (bf16[2,128,256]{2,1,0:T(8,128)(2,1)S(1)}, bf16[2,128,256]{2,1,0:T(8,128)(2,1)S(1)}, u32[]{:S(2)}, u32[]{:S(2)}) collective-permute-start(bf16[2,128,256]{2,1,0:T(8,128)(2,1)S(1)} %fusion.4), channel_id=1, source_target_pairs={{0,32},{4,228},{32,64},{36,4},{64,96},{68,36},{96,128},{100,68},{1... | collective-permute-start | bytes 393224 | tf_op jit(solution)/shard_map/ppermute | solution.py:25
  68.7 5.1 %collective-permute-start.8 = (bf16[2,128,256]{2,1,0:T(8,128)(2,1)S(1)}, bf16[2,128,256]{2,1,0:T(8,128)(2,1)S(1)}, u32[]{:S(2)}, u32[]{:S(2)}) collective-permute-start(bf16[2,128,256]{2,1,0:T(8,128)(2,1)S(1)} %pad_maximum_fusion.3), channel_id=1, source_target_pairs={{0,8},{4,28},{8,16},{12,4},{16,24},{20,12},{24,0},{28,20},{1,9},{5... | collective-permute-start | bytes 393224 | tf_op jit(solution)/shard_map/ppermute | solution.py:25
  71.5 6.2 %collective-permute-start.16 = (bf16[2,128,256]{2,1,0:T(8,128)(2,1)S(1)}, bf16[2,128,256]{2,1,0:T(8,128)(2,1)S(1)}, u32[]{:S(2)}, u32[]{:S(2)}) collective-permute-start(bf16[2,128,256]{2,1,0:T(8,128)(2,1)S(1)} %fusion.5), channel_id=1, source_target_pairs={{0,32},{4,228},{32,64},{36,4},{64,96},{68,36},{96,128},{100,68},{1... | collective-permute-start | bytes 393224 | tf_op jit(solution)/shard_map/ppermute | solution.py:25
  73.8 10.2 %collective-permute-start.9 = (bf16[128,256]{1,0:T(8,128)(2,1)S(1)}, bf16[128,256]{1,0:T(8,128)(2,1)S(1)}, u32[]{:S(2)}, u32[]{:S(2)}) collective-permute-start(bf16[128,256]{1,0:T(8,128)(2,1)S(1)} %get-tuple-element.69), channel_id=1, source_target_pairs={{0,4},{4,0},{1,5},{5,1},{2,6},{6,2},{3,7},{7,3},{8,12},{12,8},{9,1... | collective-permute-start | bytes 196616 | tf_op jit(solution)/shard_map/ppermute | solution.py:29
  77.8 7.0 %collective-permute-start.17 = (bf16[128,256]{1,0:T(8,128)(2,1)S(1)}, bf16[128,256]{1,0:T(8,128)(2,1)S(1)}, u32[]{:S(2)}, u32[]{:S(2)}) collective-permute-start(bf16[128,256]{1,0:T(8,128)(2,1)S(1)} %get-tuple-element.63), channel_id=1, source_target_pairs={{0,4},{4,0},{1,5},{5,1},{2,6},{6,2},{3,7},{7,3},{8,12},{12,8},{9,1... | collective-permute-start | bytes 196616 | tf_op jit(solution)/shard_map/ppermute | solution.py:29
  101.8 20.5 %all-to-all-start = ((bf16[64,8,128]{2,1,0:T(8,128)(2,1)}), bf16[64,8,128]{2,1,0:T(8,128)(2,1)S(1)}, u32[]{:S(2)}, u32[]{:S(2)}) async-start(bf16[64,8,128]{2,1,0:T(8,128)(2,1)} %bitcast.13), calls=%async_computation | async-start | bytes 262144 | tf_op jit(solution)/shard_map/all_to_all | solution.py:248

commit v2 on v1

--- a/solution.py
+++ b/solution.py
@@ -13,6 +13,7 @@
 Z, Y, CORE = DP
 F32 = jnp.float32
 BF16 = jnp.bfloat16
+VMEM_LIMIT = 24 * 1024 * 1024
 
 MOMENT_DECAY = 0.9
 RIDGE_SHARE = 0.0001
@@ -40,35 +41,45 @@
     return wide(*parts).astype(BF16)
 
 
-def added_first(base, part):
-    n = part.shape[0]
-    return jnp.concatenate([added(base[:n], part), base[n:].astype(BF16)], axis=0)
-
-
-def group_a(k):
-    if k == 4:
-        return [(0, ("fix", 4), ("turn", j), d) for j in range(2) for d in range(2)]
-    return [(0, ("sign", k), ("turn", j), d) for j in range(4) for d in range(2)]
-
-
-def group_b(k):
-    if k == 2:
-        return [(1, ("turn", j), ("fix", 2), d) for j in range(4) for d in range(2)]
-    return [(1, ("turn", j), ("sign", 1), d) for j in range(8) for d in range(2)]
-
-
-KEPT_A = [(0, ("fix", 0), ("sign", 1), d) for d in range(2)]
-KEPT_A += [(0, ("fix", 0), ("fix", dy), 0) for dy in (2, 0)]
-KEPT_B = [(1, ("sign", k), ("fix", 0), d) for k in (3, 2, 1) for d in range(2)]
-KEPT_B += [(1, ("fix", dz), ("fix", 0), 0) for dz in (4, 0)]
+def added_inside(base, part, start):
+    stop = start + part.shape[0]
+    ends = [base[:start].astype(BF16), added(base[start:stop], part), base[stop:].astype(BF16)]
+    return jnp.concatenate([e for e in ends if e.shape[0]], axis=0)
+
+
+def after(x, *others):
+    return lax.optimization_barrier((x, *others))[0]
+
+
+def give_and_keep(near_offsets, fixed):
+    back = [("sign", -k) for k in near_offsets]
+    ahead = [("sign", k) for k in near_offsets]
+    still = [("fix", k) for k in fixed]
+    give = [(o, 1) for o in back + still] + [(o, 0) for o in back]
+    keep = [(o, 0) for o in ahead + still] + [(o, 1) for o in ahead]
+    return give, keep
+
+
+GIVE_Y, KEEP_Y = give_and_keep((1,), (2, 0))
+GIVE_Z, KEEP_Z = give_and_keep((3, 2, 1), (4, 0))
+OWN_Y = [e for e in GIVE_Y + KEEP_Y if e[1] == 0]
+OWN_Z = [e for e in GIVE_Z + KEEP_Z if e[1] == 0]
+FIRST_OWN_Y = (GIVE_Y + KEEP_Y).index(OWN_Y[0])
+FIRST_OWN_Z = (GIVE_Z + KEEP_Z).index(OWN_Z[0])
+
+
+def group_a(dz, entries):
+    return [(0, dz, dy, flip) for dy, flip in entries]
+
+
+def group_b(dy, entries):
+    return [(1, dz, dy, flip) for dz, flip in entries]
 
 
 def offset(what, size, core):
     kind, k = what
     if kind == "sign":
-        return k + core * (size - 2 * k)
-    if kind == "turn":
-        return k + core * (size // 2)
+        return size + k - 2 * k * core
     return k
 
 
@@ -105,7 +116,7 @@
         out_shape=[jax.ShapeDtypeStruct((len(g), rows, half_cols), held) for g in groups],
         in_specs=[smem, vmem, vmem] + [vmem] * len(inputs),
         out_specs=[vmem for _ in groups],
-        compiler_params=pltpu.CompilerParams(vmem_limit_bytes=40 * 1024 * 1024),
+        compiler_params=pltpu.CompilerParams(vmem_limit_bytes=VMEM_LIMIT),
         name="block_sums",
     )(owner_table, acts, kvt, *inputs)
 
@@ -210,7 +221,7 @@
         in_specs=[vmem] * (n_a + n_b + 2),
         out_specs=[vmem] * 3,
         scratch_shapes=[pltpu.VMEM((order, width), F32)] * 2 + square(order) + square(width),
-        compiler_params=pltpu.CompilerParams(vmem_limit_bytes=48 * 1024 * 1024),
+        compiler_params=pltpu.CompilerParams(vmem_limit_bytes=VMEM_LIMIT),
         name="precondition",
     )(*parts_a, *parts_b, left, right)
 
@@ -265,49 +276,41 @@
     acts_peer = swapped(activations)
     kvt_peer = swapped(kvt)
 
-    first = [group_a(4), group_b(2)]
-    rest = [group_a(3), group_b(1), group_a(2), group_a(1), KEPT_A, KEPT_B]
+    all_y, all_z = GIVE_Y + KEEP_Y, GIVE_Z + KEEP_Z
+    first = [group_a(("fix", 4), OWN_Y), group_b(("fix", 2), OWN_Z)]
+    rest = [group_a(("sign", 3), all_y), group_b(("sign", 1), all_z)]
+    rest += [group_a(("sign", 2), all_y), group_a(("sign", 1), all_y)]
+    rest += [group_a(("fix", 0), KEEP_Y), group_b(("fix", 0), KEEP_Z)]
     sizes = (block_rows, row_blocks, owner_table)
     own = block_sums(first + rest, activations, kvt, *sizes)
     a4, b2 = block_sums(first, acts_peer, kvt_peer, *sizes, before=own[:2])
     a3, b1, a2, a1, a0, b0 = block_sums(rest, acts_peer, kvt_peer, *sizes, before=own[2:])
 
-    run = added_first(a3, directed(a4, Z))
-    run = added(a2, directed(run, Z))
-    run = added(a1, directed(run, Z))
-    run = directed(run, Z)
-    run = run.reshape(2, 2, 2, *run.shape[1:])
-    lo, hi = run[0], run[1]
-    core = lax.axis_index(CORE)
-    even_mine = jnp.where(core == 0, lo[0], hi[0])
-    even_far = jnp.where(core == 0, hi[0], lo[0])
-    odd_mine = lo[1]
-    odd_away = hi[1]
-    give = jnp.stack([odd_away[1], odd_away[0], even_far[1], even_mine[1]])
-    got = swapped(give)
-    keep = jnp.stack([odd_mine[0], odd_mine[1], even_far[0], even_mine[0]])
-    kept = wide(a0, keep, got)
-    near = added_first(kept[:2], directed(kept[2:3].astype(BF16), Y))
-    near = directed(near, Y)
-    ga = [kept[3], near[0], swapped(near[1])]
-
-    run = added_first(b1, directed(b2, Y))
-    run = directed(run, Y)
-    run = run.reshape(2, 4, 2, *run.shape[1:])
-    lo, hi = run[0], run[1]
-    mine = jnp.where(core == 0, lo[0], hi[0])
-    far = jnp.where(core == 0, hi[0], lo[0])
-    toward = [jnp.where(core == 0, lo[k], lo[4 - k]) for k in (3, 2, 1)]
-    away = [jnp.where(core == 0, hi[4 - k], hi[k]) for k in (3, 2, 1)]
-    give = jnp.stack([w[d] for w in away for d in (1, 0)] + [far[1], mine[1]])
-    keep = jnp.stack([w[d] for w in toward for d in (0, 1)] + [far[0], mine[0]])
-    got = swapped(give)
-    kept = wide(b0, keep, got)
-    near = added_first(kept[0:2], directed(kept[6:7].astype(BF16), Z))
-    near = added(kept[2:4], directed(near, Z))
-    near = added(kept[4:6], directed(near, Z))
-    near = directed(near, Z)
-    gb = [kept[7], near[0], swapped(near[1])]
+    a_run = added_inside(a3, directed(a4, Z), FIRST_OWN_Y)
+    b_run = added_inside(b1, directed(b2, Y), FIRST_OWN_Z)
+    a_run = added(a2, directed(a_run, Z))
+    a_run = added(a1, directed(a_run, Z))
+    b_run = directed(b_run, Y)
+    n = len(GIVE_Z)
+    b = wide(b0, b_run[n:], swapped(b_run[:n]))
+    b3, b2, b1, b4, b0 = (b[k] for k in range(5))
+    a_run = after(directed(a_run, Z), b)
+
+    b_near = after(directed(b4[None].astype(BF16), Z), a_run)
+    b_near = jnp.stack([added(b3, b_near[0]), b[5].astype(BF16)])
+
+    n = len(GIVE_Y)
+    a = wide(a0, a_run[n:], swapped(a_run[:n]))
+    b_near = after(directed(b_near, Z), a)
+    b_near = added(jnp.stack([b2, b[6]]), b_near)
+    a_near = directed(a[1:2].astype(BF16), Y)
+    a_near = jnp.stack([added(a[0], a_near[0]), a[3].astype(BF16)])
+    b_near = after(directed(b_near, Z), a_near)
+    b_near = added(jnp.stack([b1, b[7]]), b_near)
+    a_near = after(directed(a_near, Y), b_near)
+    b_near = directed(b_near, Z)
+    ga = [a[2], a_near[0], swapped(a_near[1])]
+    gb = [b0, b_near[0], swapped(b_near[1])]
     return ga, gb
 
 

time: 151 us -> 143 us (0.947)
  starting transfers between devices: 54.3 us -> 51.1 us
  waiting for transfers between devices: 33.6 us -> 30.7 us
  other arithmetic: 3.3 us -> 1.34 us
    ppermute x6, starting transfers between devices: 17.7 us -> 14.7 us  [swapped(): return lax.ppermute(x, CORE, [(0, 1), (1, 0)])]
    ppermute x12, waiting for transfers between devices: 19.9 us -> 17.7 us  [directed(): return lax.ppermute(x, (axis, CORE), pairs)]
    convert_element_type x8 -> x7, other arithmetic: 2.41 us -> 0.58 us  [added(): return wide(*parts).astype(BF16)]
    unnamed x19 -> x11, local copies, waits for them, and re-layouts: 4.01 us -> 3.95 us
  transfers between devices with their start and end apart: 19 -> 19, of which waited for: 9 -> 9; matrix products, arithmetic and copies ran while one was open for 3% -> 2% of each run, Pallas kernels for 4% -> 4%
where the time goes in v2:
time: 143 us; the launch traced here: 142 us
  starting transfers between devices  51.1 us (36%)
  waiting for transfers between devices  30.7 us (21%)
  Pallas kernels  27 us (19%)
  blocking collectives  26.3 us (18%)
  local copies, waits for them, and re-layouts  4.66 us (3%)
    ppermute x12, starting transfers between devices, directed(): return lax.ppermute(x, (axis, CORE), pairs)  27.2 us
    all_to_all x1, blocking collectives, routed(): got = lax.all_to_all(copies, (*DP, 'tensor'), 0, 0, tiled=True)  26.3 us
    ppermute x12, waiting for transfers between devices, directed(): return lax.ppermute(x, (axis, CORE), pairs)  17.7 us
    pallas_call x1, Pallas kernels, precondition(): pl.pallas_call(body, out_shape=[jax.ShapeDtypeStruct(left.shape, F32), ja...  17 us
    ppermute x6, starting transfers between devices, swapped(): return lax.ppermute(x, CORE, [(0, 1), (1, 0)])  14.7 us
    all_to_all x1, waiting for transfers between devices, routed(): lax.all_to_all(directions.reshape(slots, 8, width), DP, 0, 0, tiled=True)  10.5 us
    all_to_all x1, starting transfers between devices, routed(): lax.all_to_all(directions.reshape(slots, 8, width), DP, 0, 0, tiled=True)  9.11 us
    pallas_call x3, Pallas kernels, block_sums(): pl.pallas_call(body, out_shape=[jax.ShapeDtypeStruct((len(g), rows, half_...  8.5 us
  transfers between devices with their start and end apart: 19, of which 9 were waited for; matrix products, arithmetic and copies ran while one was open for 2% of the time, Pallas kernels for 4%

profile of v2, /device:TPU:1, one launch (start us, length us, event | category | flops | bytes accessed | tf_op | source)
XLA Modules:
  0.0 142.3 jit_solution(3710318390875976892)
XLA Ops:
  0.6 3.3 %collective-permute-start = (bf16[256,8192]{1,0:T(8,128)(2,1)}, bf16[256,8192]{1,0:T(8,128)(2,1)}, u32[]{:S(2)}, u32[]{:S(2)}) collective-permute-start(bf16[256,8192]{1,0:T(8,128)(2,1)} %a_ref.1), channel_id=1, source_target_pairs={{0,4},{4,0},{1,5},{5,1},{2,6},{6,2},{3,7},{7,3},{8,12},{12,8},{9,1... | collective-permute-start | bytes 12582920 | tf_op jit(solution)/shard_map/ppermute | solution.py:30
  4.0 1.1 copy.10
  5.2 2.2 %copy-done = bf16[256,8192]{1,0:T(8,128)(2,1)S(1)} copy-done((bf16[256,8192]{1,0:T(8,128)(2,1)S(1)}, bf16[256,8192]{1,0:T(8,128)(2,1)}, u32[]{:S(2)}) %copy-start) | copy-done | bytes 4194328
  8.0 2.1 %block_sums.3 = (f32[4,128,256]{2,1,0:T(8,128)S(1)}, f32[8,128,256]{2,1,0:T(8,128)S(1)}, f32[8,128,256]{2,1,0:T(8,128)S(1)}, f32[16,128,256]{2,1,0:T(8,128)S(1)}...) custom-call(s32[64]{0:T(128)S(1)} %copy-done.3, ...), custom_call_target="tpu_custom_call" | custom-call | tf_op jit(solution)/shard_map/block_sums/pallas_call | solution.py:114
  10.1 1.0 collective-permute-done.1.k_ref
  11.1 2.7 %block_sums.5 = (bf16[4,128,256]{2,1,0:T(8,128)(2,1)S(1)}, bf16[8,128,256]{2,1,0:T(8,128)(2,1)S(1)}) custom-call(s32[64]{0:T(128)S(1)} %copy-done.3, bf16[256,8192]{1,0:T(8,128)(2,1)} %collective-permute-done.a_ref, bf16[512,256]{1,0:T(8,128)(2,1)S(1)} %collective-permute-done.1.k_ref, f32[4,128,256]{2,1,0:T(8,128)S(1)} %get-tuple-element.37.refs_0_, ...), custom_call_target="tpu_custom_call" | custom-call | tf_op jit(solution)/shard_map/block_sums/pallas_call | solution.py:114
  13.8 3.9 %collective-permute-start.2 = (bf16[4,128,256]{2,1,0:T(8,128)(2,1)S(1)}, bf16[4,128,256]{2,1,0:T(8,128)(2,1)S(1)}, u32[]{:S(2)}, u32[]{:S(2)}) collective-permute-start(bf16[4,128,256]{2,1,0:T(8,128)(2,1)S(1)} %get-tuple-element.39), channel_id=1, source_target_pairs={{0,32},{4,228},{32,64},{36,4},{64,96},{68,36},{96,128},{100,68},{1... | collective-permute-start | bytes 786440 | tf_op jit(solution)/shard_map/ppermute | solution.py:26
  17.7 2.7 %collective-permute-start.6 = (bf16[8,128,256]{2,1,0:T(8,128)(2,1)S(1)}, bf16[8,128,256]{2,1,0:T(8,128)(2,1)S(1)}, u32[]{:S(2)}, u32[]{:S(2)}) collective-permute-start(bf16[8,128,256]{2,1,0:T(8,128)(2,1)S(1)} %get-tuple-element.42), channel_id=1, source_target_pairs={{0,8},{4,28},{8,16},{12,4},{16,24},{20,12},{24,0},{28,20},{1,9},{5... | collective-permute-start | bytes 1572872 | tf_op jit(solution)/shard_map/ppermute | solution.py:26
  20.4 3.7 %block_sums.4 = (bf16[8,128,256]{2,1,0:T(8,128)(2,1)S(1)}, bf16[16,128,256]{2,1,0:T(8,128)(2,1)S(1)}, bf16[8,128,256]{2,1,0:T(8,128)(2,1)S(1)}, bf16[8,128,256]{...) custom-call(s32[64]{0:T(128)S(1)} %copy-done.3, ...), custom_call_target="tpu_custom_call" | custom-call | tf_op jit(solution)/shard_map/block_sums/pallas_call | solution.py:114
  24.4 0.8 collective-permute-start.3
  25.3 1.3 collective-permute-done.6
  26.9 3.2 %collective-permute-start.7 = (bf16[16,128,256]{2,1,0:T(8,128)(2,1)S(1)}, bf16[16,128,256]{2,1,0:T(8,128)(2,1)S(1)}, u32[]{:S(2)}, u32[]{:S(2)}) collective-permute-start(bf16[16,128,256]{2,1,0:T(8,128)(2,1)S(1)} %pad_maximum_fusion), channel_id=1, source_target_pairs={{0,8},{4,28},{8,16},{12,4},{16,24},{20,12},{24,0},{28,20},{1,9},{5... | collective-permute-start | bytes 3145736 | tf_op jit(solution)/shard_map/ppermute | solution.py:26
  30.0 2.8 %collective-permute-done.3 = bf16[8,128,256]{2,1,0:T(8,128)(2,1)S(1)} collective-permute-done((bf16[8,128,256]{2,1,0:T(8,128)(2,1)S(1)}, bf16[8,128,256]{2,1,0:T(8,128)(2,1)S(1)}, u32[]{:S(2)}, u32[]{:S(2)}) %collective-permute-start.3) | collective-permute-done | bytes 524320 | tf_op jit(solution)/shard_map/ppermute | solution.py:26
  33.0 2.0 %collective-permute-start.4 = (bf16[8,128,256]{2,1,0:T(8,128)(2,1)S(1)}, bf16[8,128,256]{2,1,0:T(8,128)(2,1)S(1)}, u32[]{:S(2)}, u32[]{:S(2)}) collective-permute-start(bf16[8,128,256]{2,1,0:T(8,128)(2,1)S(1)} %add_convert_fusion.2), channel_id=1, source_target_pairs={{0,32},{4,228},{32,64},{36,4},{64,96},{68,36},{96,128},{100,68},{1... | collective-permute-start | bytes 1572872 | tf_op jit(solution)/shard_map/ppermute | solution.py:26
  35.0 6.8 %collective-permute-done.7 = bf16[16,128,256]{2,1,0:T(8,128)(2,1)S(1)} collective-permute-done((bf16[16,128,256]{2,1,0:T(8,128)(2,1)S(1)}, bf16[16,128,256]{2,1,0:T(8,128)(2,1)S(1)}, u32[]{:S(2)}, u32[]{:S(2)}) %collective-permute-start.7) | collective-permute-done | bytes 1048608 | tf_op jit(solution)/shard_map/ppermute | solution.py:26
  42.1 3.2 %collective-permute-start.5 = (bf16[8,128,256]{2,1,0:T(8,128)(2,1)S(1)}, bf16[8,128,256]{2,1,0:T(8,128)(2,1)S(1)}, u32[]{:S(2)}, u32[]{:S(2)}) collective-permute-start(bf16[8,128,256]{2,1,0:T(8,128)(2,1)S(1)} %add_convert_fusion.1), channel_id=1, source_target_pairs={{0,32},{4,228},{32,64},{36,4},{64,96},{68,36},{96,128},{100,68},{1... | collective-permute-start | bytes 1572872 | tf_op jit(solution)/shard_map/ppermute | solution.py:26
  45.5 1.7 %collective-permute-start.12 = (bf16[1,128,256]{2,1,0:T(8,128)(2,1)S(1)}, bf16[1,128,256]{2,1,0:T(8,128)(2,1)S(1)}, u32[]{:S(2)}, u32[]{:S(2)}) collective-permute-start(bf16[1,128,256]{2,1,0:T(8,128)(2,1)S(1)} %get-tuple-element.61), channel_id=1, source_target_pairs={{0,32},{4,228},{32,64},{36,4},{64,96},{68,36},{96,128},{100,68},{1... | collective-permute-start | bytes 196616 | tf_op jit(solution)/shard_map/ppermute | solution.py:26
  47.3 4.1 %collective-permute-done.5 = bf16[8,128,256]{2,1,0:T(8,128)(2,1)S(1)} collective-permute-done((bf16[8,128,256]{2,1,0:T(8,128)(2,1)S(1)}, bf16[8,128,256]{2,1,0:T(8,128)(2,1)S(1)}, u32[]{:S(2)}, u32[]{:S(2)}) %collective-permute-start.5) | collective-permute-done | bytes 524320 | tf_op jit(solution)/shard_map/ppermute | solution.py:26
  51.4 3.4 %collective-permute-start.9 = (bf16[4,128,256]{2,1,0:T(8,128)(2,1)S(1)}, bf16[4,128,256]{2,1,0:T(8,128)(2,1)S(1)}, u32[]{:S(2)}, u32[]{:S(2)}) collective-permute-start(bf16[4,128,256]{2,1,0:T(8,128)(2,1)S(1)} %slice.91), channel_id=1, source_target_pairs={{0,4},{4,0},{1,5},{5,1},{2,6},{6,2},{3,7},{7,3},{8,12},{12,8},{9,1... | collective-permute-start | bytes 786440 | tf_op jit(solution)/shard_map/ppermute | solution.py:30
  56.1 2.7 %collective-permute-done.13 = bf16[2,128,256]{2,1,0:T(8,128)(2,1)S(1)} collective-permute-done((bf16[2,128,256]{2,1,0:T(8,128)(2,1)S(1)}, bf16[2,128,256]{2,1,0:T(8,128)(2,1)S(1)}, u32[]{:S(2)}, u32[]{:S(2)}) %collective-permute-start.13) | collective-permute-done | bytes 131104 | tf_op jit(solution)/shard_map/ppermute | solution.py:26
  58.8 2.8 %collective-permute-start.10 = (bf16[1,128,256]{2,1,0:T(8,128)(2,1)S(1)}, bf16[1,128,256]{2,1,0:T(8,128)(2,1)S(1)}, u32[]{:S(2)}, u32[]{:S(2)}) collective-permute-start(bf16[1,128,256]{2,1,0:T(8,128)(2,1)S(1)} %get-tuple-element.65), channel_id=1, source_target_pairs={{0,8},{4,28},{8,16},{12,4},{16,24},{20,12},{24,0},{28,20},{1,9},{5... | collective-permute-start | bytes 196616 | tf_op jit(solution)/shard_map/ppermute | solution.py:26
  61.7 1.3 collective-permute-start.14
  63.1 3.1 %collective-permute-start.11 = (bf16[2,128,256]{2,1,0:T(8,128)(2,1)S(1)}, bf16[2,128,256]{2,1,0:T(8,128)(2,1)S(1)}, u32[]{:S(2)}, u32[]{:S(2)}) collective-permute-start(bf16[2,128,256]{2,1,0:T(8,128)(2,1)S(1)} %pad_maximum_fusion.2), channel_id=1, source_target_pairs={{0,8},{4,28},{8,16},{12,4},{16,24},{20,12},{24,0},{28,20},{1,9},{5... | collective-permute-start | bytes 393224 | tf_op jit(solution)/shard_map/ppermute | solution.py:26
  66.2 2.0 %collective-permute-start.16 = (bf16[2,128,256]{2,1,0:T(8,128)(2,1)S(1)}, bf16[2,128,256]{2,1,0:T(8,128)(2,1)S(1)}, u32[]{:S(2)}, u32[]{:S(2)}) collective-permute-start(bf16[2,128,256]{2,1,0:T(8,128)(2,1)S(1)} %fusion.4), channel_id=1, source_target_pairs={{0,32},{4,228},{32,64},{36,4},{64,96},{68,36},{96,128},{100,68},{1... | collective-permute-start | bytes 393224 | tf_op jit(solution)/shard_map/ppermute | solution.py:26
  68.2 5.4 %collective-permute-start.15 = (bf16[128,256]{1,0:T(8,128)(2,1)S(1)}, bf16[128,256]{1,0:T(8,128)(2,1)S(1)}, u32[]{:S(2)}, u32[]{:S(2)}) collective-permute-start(bf16[128,256]{1,0:T(8,128)(2,1)S(1)} %get-tuple-element.69), channel_id=1, source_target_pairs={{0,4},{4,0},{1,5},{5,1},{2,6},{6,2},{3,7},{7,3},{8,12},{12,8},{9,1... | collective-permute-start | bytes 196616 | tf_op jit(solution)/shard_map/ppermute | solution.py:30
  73.6 2.4 %collective-permute-start.17 = (bf16[128,256]{1,0:T(8,128)(2,1)S(1)}, bf16[128,256]{1,0:T(8,128)(2,1)S(1)}, u32[]{:S(2)}, u32[]{:S(2)}) collective-permute-start(bf16[128,256]{1,0:T(8,128)(2,1)S(1)} %get-tuple-element.67), channel_id=1, source_target_pairs={{0,4},{4,0},{1,5},{5,1},{2,6},{6,2},{3,7},{7,3},{8,12},{12,8},{9,1... | collective-permute-start | bytes 196616 | tf_op jit(solution)/shard_map/ppermute | solution.py:30
  76.0 0.8 collective-permute-done.17.refs_5_
  76.9 17.0 %precondition.1 = (f32[512,512]{1,0:T(8,128)}, f32[128,128]{1,0:T(8,128)}, bf16[512,128]{1,0:T(8,128)(2,1)}) custom-call(f32[128,256]{1,0:T(8,128)S(1)} %get-tuple-element.64.refs_0_, bf16[128,256]{1,0:T(8,128)(2,1)S(1)} %get-tuple-element.70.refs_1_, bf16[128,256]{1,0:T(8,128)(2,1)S(1)} %collective-permute-done.15.refs_2_, ...), custom_call_target="tpu_custom_call" | custom-call | tf_op jit(solution)/shard_map/precondition/pallas_call | solution.py:214
  93.9 9.1 %all-to-all-start = ((bf16[64,8,128]{2,1,0:T(8,128)(2,1)}), bf16[64,8,128]{2,1,0:T(8,128)(2,1)S(1)}, u32[]{:S(2)}, u32[]{:S(2)}) async-start(bf16[64,8,128]{2,1,0:T(8,128)(2,1)} %bitcast.13), calls=%async_computation | async-start | bytes 262144 | tf_op jit(solution)/shard_map/all_to_all | solution.py:259
  103.6 10.5 %all-to-all-done = bf16[64,8,128]{2,1,0:T(8,128)(2,1)S(1)} async-done(((bf16[64,8,128]{2,1,0:T(8,128)(2,1)}), bf16[64,8,128]{2,1,0:T(8,128)(2,1)S(1)}, u32[]{:S(2)}, u32[]{:S(2)}) %all-to-all-start) | async-done | bytes 131104 | tf_op jit(solution)/shard_map/all_to_all | solution.py:259
  114.6 26.3 %all_to_all.10 = bf16[256,8,128]{2,1,0:T(8,128)(2,1)S(1)} all-to-all(bf16[256,8,128]{2,1,0:T(8,128)(2,1)S(1)} %bitcast.32), channel_id=1, replica_groups=mesh['dp_0'=8,'dp_1'=4,'dp_2'=2,'tensor'=4] {'dp_0','dp_1','dp_2','tensor'}, dimensions={0} | all-to-all | bytes 1048576 | tf_op jit(solution)/shard_map/all_to_all | solution.py:268
  140.9 1.5 %placed.1 = bf16[2,128,1024]{2,1,0:T(8,128)(2,1)} custom-call(bf16[2048,128]{1,0:T(8,128)(2,1)S(1)} %bitcast.27), custom_call_target="tpu_custom_call" | custom-call | tf_op jit(solution)/shard_map/placed/pallas_call | solution.py:244
  (56 shorter events, 4.4 us)
Async XLA Ops:
  0.6 10.5 %collective-permute-start = (bf16[256,8192]{1,0:T(8,128)(2,1)}, bf16[256,8192]{1,0:T(8,128)(2,1)}, u32[]{:S(2)}, u32[]{:S(2)}) collective-permute-start(bf16[256,8192]{1,0:T(8,128)(2,1)} %a_ref.1), channel_id=1, source_target_pairs={{0,4},{4,0},{1,5},{5,1},{2,6},{6,2},{3,7},{7,3},{8,12},{12,8},{9,1... | collective-permute-start | bytes 12582920 | tf_op jit(solution)/shard_map/ppermute | solution.py:30
  5.1 6.1 %collective-permute-start.1 = (bf16[512,256]{1,0:T(8,128)(2,1)S(1)}, bf16[512,256]{1,0:T(8,128)(2,1)S(1)}, u32[]{:S(2)}, u32[]{:S(2)}) collective-permute-start(bf16[512,256]{1,0:T(8,128)(2,1)S(1)} %bitcast.28), channel_id=1, source_target_pairs={{0,4},{4,0},{1,5},{5,1},{2,6},{6,2},{3,7},{7,3},{8,12},{12,8},{9,1... | collective-permute-start | bytes 786440 | tf_op jit(solution)/shard_map/ppermute | solution.py:30
  5.2 2.2 %copy-start = (bf16[256,8192]{1,0:T(8,128)(2,1)S(1)}, bf16[256,8192]{1,0:T(8,128)(2,1)}, u32[]{:S(2)}) copy-start(bf16[256,8192]{1,0:T(8,128)(2,1)} %a_ref.1) | copy-start | bytes 12582916
  7.4 0.7 copy-start.3
  13.8 10.5 %collective-permute-start.2 = (bf16[4,128,256]{2,1,0:T(8,128)(2,1)S(1)}, bf16[4,128,256]{2,1,0:T(8,128)(2,1)S(1)}, u32[]{:S(2)}, u32[]{:S(2)}) collective-permute-start(bf16[4,128,256]{2,1,0:T(8,128)(2,1)S(1)} %get-tuple-element.39), channel_id=1, source_target_pairs={{0,32},{4,228},{32,64},{36,4},{64,96},{68,36},{96,128},{100,68},{1... | collective-permute-start | bytes 786440 | tf_op jit(solution)/shard_map/ppermute | solution.py:26
  17.7 8.9 %collective-permute-start.6 = (bf16[8,128,256]{2,1,0:T(8,128)(2,1)S(1)}, bf16[8,128,256]{2,1,0:T(8,128)(2,1)S(1)}, u32[]{:S(2)}, u32[]{:S(2)}) collective-permute-start(bf16[8,128,256]{2,1,0:T(8,128)(2,1)S(1)} %get-tuple-element.42), channel_id=1, source_target_pairs={{0,8},{4,28},{8,16},{12,4},{16,24},{20,12},{24,0},{28,20},{1,9},{5... | collective-permute-start | bytes 1572872 | tf_op jit(solution)/shard_map/ppermute | solution.py:26
  24.4 8.4 %collective-permute-start.3 = (bf16[8,128,256]{2,1,0:T(8,128)(2,1)S(1)}, bf16[8,128,256]{2,1,0:T(8,128)(2,1)S(1)}, u32[]{:S(2)}, u32[]{:S(2)}) collective-permute-start(bf16[8,128,256]{2,1,0:T(8,128)(2,1)S(1)} %pad_maximum_fusion.1), channel_id=1, source_target_pairs={{0,32},{4,228},{32,64},{36,4},{64,96},{68,36},{96,128},{100,68},{1... | collective-permute-start | bytes 1572872 | tf_op jit(solution)/shard_map/ppermute | solution.py:26
  26.9 14.9 %collective-permute-start.7 = (bf16[16,128,256]{2,1,0:T(8,128)(2,1)S(1)}, bf16[16,128,256]{2,1,0:T(8,128)(2,1)S(1)}, u32[]{:S(2)}, u32[]{:S(2)}) collective-permute-start(bf16[16,128,256]{2,1,0:T(8,128)(2,1)S(1)} %pad_maximum_fusion), channel_id=1, source_target_pairs={{0,8},{4,28},{8,16},{12,4},{16,24},{20,12},{24,0},{28,20},{1,9},{5... | collective-permute-start | bytes 3145736 | tf_op jit(solution)/shard_map/ppermute | solution.py:26
  33.0 8.9 %collective-permute-start.4 = (bf16[8,128,256]{2,1,0:T(8,128)(2,1)S(1)}, bf16[8,128,256]{2,1,0:T(8,128)(2,1)S(1)}, u32[]{:S(2)}, u32[]{:S(2)}) collective-permute-start(bf16[8,128,256]{2,1,0:T(8,128)(2,1)S(1)} %add_convert_fusion.2), channel_id=1, source_target_pairs={{0,32},{4,228},{32,64},{36,4},{64,96},{68,36},{96,128},{100,68},{1... | collective-permute-start | bytes 1572872 | tf_op jit(solution)/shard_map/ppermute | solution.py:26
  41.8 3.4 %collective-permute-start.8 = (bf16[8,128,256]{2,1,0:T(8,128)(2,1)S(1)}, bf16[8,128,256]{2,1,0:T(8,128)(2,1)S(1)}, u32[]{:S(2)}, u32[]{:S(2)}) collective-permute-start(bf16[8,128,256]{2,1,0:T(8,128)(2,1)S(1)} %slice.109), channel_id=1, source_target_pairs={{0,4},{4,0},{1,5},{5,1},{2,6},{6,2},{3,7},{7,3},{8,12},{12,8},{9,1... | collective-permute-start | bytes 1572872 | tf_op jit(solution)/shard_map/ppermute | solution.py:30
  42.1 9.3 %collective-permute-start.5 = (bf16[8,128,256]{2,1,0:T(8,128)(2,1)S(1)}, bf16[8,128,256]{2,1,0:T(8,128)(2,1)S(1)}, u32[]{:S(2)}, u32[]{:S(2)}) collective-permute-start(bf16[8,128,256]{2,1,0:T(8,128)(2,1)S(1)} %add_convert_fusion.1), channel_id=1, source_target_pairs={{0,32},{4,228},{32,64},{36,4},{64,96},{68,36},{96,128},{100,68},{1... | collective-permute-start | bytes 1572872 | tf_op jit(solution)/shard_map/ppermute | solution.py:26
  45.5 31.4 %copy-start.1 = (f32[1,1,512,512]{3,2,1,0:T(8,128)S(1)}, f32[1,1,512,512]{3,2,1,0:T(8,128)}, u32[]{:S(2)}) copy-start(f32[1,1,512,512]{3,2,1,0:T(8,128)} %param.8) | copy-start | bytes 3145732
  45.5 31.4 %copy-start.2 = (f32[1,1,128,128]{3,2,1,0:T(8,128)S(1)}, f32[1,1,128,128]{3,2,1,0:T(8,128)}, u32[]{:S(2)}) copy-start(f32[1,1,128,128]{3,2,1,0:T(8,128)} %param.9) | copy-start | bytes 196612
  45.5 9.3 %collective-permute-start.12 = (bf16[1,128,256]{2,1,0:T(8,128)(2,1)S(1)}, bf16[1,128,256]{2,1,0:T(8,128)(2,1)S(1)}, u32[]{:S(2)}, u32[]{:S(2)}) collective-permute-start(bf16[1,128,256]{2,1,0:T(8,128)(2,1)S(1)} %get-tuple-element.61), channel_id=1, source_target_pairs={{0,32},{4,228},{32,64},{36,4},{64,96},{68,36},{96,128},{100,68},{1... | collective-permute-start | bytes 196616 | tf_op jit(solution)/shard_map/ppermute | solution.py:26
  51.4 51.6 %copy-start.4 = (s32[64]{0:T(128)S(1)}, s32[64]{0:T(128)}, u32[]{:S(2)}) copy-start(s32[64]{0:T(128)} %owner_ref.5) | copy-start | bytes 772
  51.4 4.6 %collective-permute-start.9 = (bf16[4,128,256]{2,1,0:T(8,128)(2,1)S(1)}, bf16[4,128,256]{2,1,0:T(8,128)(2,1)S(1)}, u32[]{:S(2)}, u32[]{:S(2)}) collective-permute-start(bf16[4,128,256]{2,1,0:T(8,128)(2,1)S(1)} %slice.91), channel_id=1, source_target_pairs={{0,4},{4,0},{1,5},{5,1},{2,6},{6,2},{3,7},{7,3},{8,12},{12,8},{9,1... | collective-permute-start | bytes 786440 | tf_op jit(solution)/shard_map/ppermute | solution.py:30
  54.9 3.9 %collective-permute-start.13 = (bf16[2,128,256]{2,1,0:T(8,128)(2,1)S(1)}, bf16[2,128,256]{2,1,0:T(8,128)(2,1)S(1)}, u32[]{:S(2)}, u32[]{:S(2)}) collective-permute-start(bf16[2,128,256]{2,1,0:T(8,128)(2,1)S(1)} %pad_maximum_fusion.3), channel_id=1, source_target_pairs={{0,32},{4,228},{32,64},{36,4},{64,96},{68,36},{96,128},{100,68},{1... | collective-permute-start | bytes 393224 | tf_op jit(solution)/shard_map/ppermute | solution.py:26
  58.8 4.2 %collective-permute-start.10 = (bf16[1,128,256]{2,1,0:T(8,128)(2,1)S(1)}, bf16[1,128,256]{2,1,0:T(8,128)(2,1)S(1)}, u32[]{:S(2)}, u32[]{:S(2)}) collective-permute-start(bf16[1,128,256]{2,1,0:T(8,128)(2,1)S(1)} %get-tuple-element.65), channel_id=1, source_target_pairs={{0,8},{4,28},{8,16},{12,4},{16,24},{20,12},{24,0},{28,20},{1,9},{5... | collective-permute-start | bytes 196616 | tf_op jit(solution)/shard_map/ppermute | solution.py:26
  61.7 4.4 %collective-permute-start.14 = (bf16[2,128,256]{2,1,0:T(8,128)(2,1)S(1)}, bf16[2,128,256]{2,1,0:T(8,128)(2,1)S(1)}, u32[]{:S(2)}, u32[]{:S(2)}) collective-permute-start(bf16[2,128,256]{2,1,0:T(8,128)(2,1)S(1)} %fusion.5), channel_id=1, source_target_pairs={{0,32},{4,228},{32,64},{36,4},{64,96},{68,36},{96,128},{100,68},{1... | collective-permute-start | bytes 393224 | tf_op jit(solution)/shard_map/ppermute | solution.py:26
  63.1 5.1 %collective-permute-start.11 = (bf16[2,128,256]{2,1,0:T(8,128)(2,1)S(1)}, bf16[2,128,256]{2,1,0:T(8,128)(2,1)S(1)}, u32[]{:S(2)}, u32[]{:S(2)}) collective-permute-start(bf16[2,128,256]{2,1,0:T(8,128)(2,1)S(1)} %pad_maximum_fusion.2), channel_id=1, source_target_pairs={{0,8},{4,28},{8,16},{12,4},{16,24},{20,12},{24,0},{28,20},{1,9},{5... | collective-permute-start | bytes 393224 | tf_op jit(solution)/shard_map/ppermute | solution.py:26
  66.2 7.4 %collective-permute-start.16 = (bf16[2,128,256]{2,1,0:T(8,128)(2,1)S(1)}, bf16[2,128,256]{2,1,0:T(8,128)(2,1)S(1)}, u32[]{:S(2)}, u32[]{:S(2)}) collective-permute-start(bf16[2,128,256]{2,1,0:T(8,128)(2,1)S(1)} %fusion.4), channel_id=1, source_target_pairs={{0,32},{4,228},{32,64},{36,4},{64,96},{68,36},{96,128},{100,68},{1... | collective-permute-start | bytes 393224 | tf_op jit(solution)/shard_map/ppermute | solution.py:26
  68.2 7.9 %collective-permute-start.15 = (bf16[128,256]{1,0:T(8,128)(2,1)S(1)}, bf16[128,256]{1,0:T(8,128)(2,1)S(1)}, u32[]{:S(2)}, u32[]{:S(2)}) collective-permute-start(bf16[128,256]{1,0:T(8,128)(2,1)S(1)} %get-tuple-element.69), channel_id=1, source_target_pairs={{0,4},{4,0},{1,5},{5,1},{2,6},{6,2},{3,7},{7,3},{8,12},{12,8},{9,1... | collective-permute-start | bytes 196616 | tf_op jit(solution)/shard_map/ppermute | solution.py:30
  73.6 3.3 %collective-permute-start.17 = (bf16[128,256]{1,0:T(8,128)(2,1)S(1)}, bf16[128,256]{1,0:T(8,128)(2,1)S(1)}, u32[]{:S(2)}, u32[]{:S(2)}) collective-permute-start(bf16[128,256]{1,0:T(8,128)(2,1)S(1)} %get-tuple-element.67), channel_id=1, source_target_pairs={{0,4},{4,0},{1,5},{5,1},{2,6},{6,2},{3,7},{7,3},{8,12},{12,8},{9,1... | collective-permute-start | bytes 196616 | tf_op jit(solution)/shard_map/ppermute | solution.py:30
  93.9 20.2 %all-to-all-start = ((bf16[64,8,128]{2,1,0:T(8,128)(2,1)}), bf16[64,8,128]{2,1,0:T(8,128)(2,1)S(1)}, u32[]{:S(2)}, u32[]{:S(2)}) async-start(bf16[64,8,128]{2,1,0:T(8,128)(2,1)} %bitcast.13), calls=%async_computation | async-start | bytes 262144 | tf_op jit(solution)/shard_map/all_to_all | solution.py:259

commit v3 on v2

--- a/solution.py
+++ b/solution.py
@@ -17,11 +17,11 @@
 
 MOMENT_DECAY = 0.9
 RIDGE_SHARE = 0.0001
-def directed(x, axis):
+def directed(x, axis, hops=1):
     size = lax.axis_size(axis)
     pairs = []
     for i in range(size):
-        for core, step in enumerate((1, -1)):
+        for core, step in enumerate((hops, -hops)):
             pairs.append((i * 2 + core, (i + step) % size * 2 + core))
     return lax.ppermute(x, (axis, CORE), pairs)
 
@@ -289,28 +289,29 @@
     a_run = added_inside(a3, directed(a4, Z), FIRST_OWN_Y)
     b_run = added_inside(b1, directed(b2, Y), FIRST_OWN_Z)
     a_run = added(a2, directed(a_run, Z))
+    b_run = directed(b_run, Y)
     a_run = added(a1, directed(a_run, Z))
-    b_run = directed(b_run, Y)
     n = len(GIVE_Z)
     b = wide(b0, b_run[n:], swapped(b_run[:n]))
-    b3, b2, b1, b4, b0 = (b[k] for k in range(5))
+    b_far = jnp.stack([b[3], b[0], b[5]]).astype(BF16)
+    b_far = directed(b_far, Z, 2)
+    b_two = jnp.stack([added(b[1], b_far[0]), b[6].astype(BF16)])
+    b_one = jnp.stack([added(b[2], b_far[1]), added(b[7], b_far[2])])
+
     a_run = after(directed(a_run, Z), b)
-
-    b_near = after(directed(b4[None].astype(BF16), Z), a_run)
-    b_near = jnp.stack([added(b3, b_near[0]), b[5].astype(BF16)])
-
     n = len(GIVE_Y)
     a = wide(a0, a_run[n:], swapped(a_run[:n]))
-    b_near = after(directed(b_near, Z), a)
-    b_near = added(jnp.stack([b2, b[6]]), b_near)
-    a_near = directed(a[1:2].astype(BF16), Y)
-    a_near = jnp.stack([added(a[0], a_near[0]), a[3].astype(BF16)])
-    b_near = after(directed(b_near, Z), a_near)
-    b_near = added(jnp.stack([b1, b[7]]), b_near)
-    a_near = after(directed(a_near, Y), b_near)
-    b_near = directed(b_near, Z)
-    ga = [a[2], a_near[0], swapped(a_near[1])]
-    gb = [b0, b_near[0], swapped(b_near[1])]
+    a_two = a[1:2].astype(BF16)
+    a_one = jnp.stack([a[0], a[3]]).astype(BF16)
+    b_two = after(directed(b_two, Z, 2), a_two, a_one)
+    b_one = after(directed(b_one, Z), a_two, a_one)
+    a_two = directed(a_two, Y, 2)
+    a_one = directed(a_one, Y)
+    b_give = added(b_two[1], b_one[1])
+    b_got = swapped(b_give)
+    a_got = swapped(a_one[1])
+    ga = [a[2], a_two[0], a_one[0], a_got]
+    gb = [b[4], b_two[0], b_one[0], b_got]
     return ga, gb
 
 

time: 143 us -> 135 us (0.944)
  starting transfers between devices: 51.1 us -> 43.6 us
    ppermute x6, starting transfers between devices: 14.7 us -> 10.5 us  [swapped(): return lax.ppermute(x, CORE, [(0, 1), (1, 0)])]
    ppermute x12 -> x11, starting transfers between devices: 27.2 us -> 23.3 us  [directed(): return lax.ppermute(x, (axis, CORE), pairs)]
    ppermute x12 -> x11, waiting for transfers between devices: 17.7 us -> 18.2 us  [directed(): return lax.ppermute(x, (axis, CORE), pairs)]
  transfers between devices with their start and end apart: 19 -> 18, of which waited for: 9 -> 10; matrix products, arithmetic and copies ran while one was open for 2% -> 2% of each run, Pallas kernels for 4% -> 4%
where the time goes in v3:
time: 135 us
  starting transfers between devices  43.6 us (32%)
  waiting for transfers between devices  30.9 us (23%)
  Pallas kernels  27 us (20%)
  blocking collectives  26.3 us (19%)
  local copies, waits for them, and re-layouts  4.68 us (3%)
    all_to_all x1, blocking collectives, routed(): got = lax.all_to_all(copies, (*DP, 'tensor'), 0, 0, tiled=True)  26.3 us
    ppermute x11, starting transfers between devices, directed(): return lax.ppermute(x, (axis, CORE), pairs)  23.3 us
    ppermute x11, waiting for transfers between devices, directed(): return lax.ppermute(x, (axis, CORE), pairs)  18.2 us
    pallas_call x1, Pallas kernels, precondition(): pl.pallas_call(body, out_shape=[jax.ShapeDtypeStruct(left.shape, F32), ja...  17 us
    all_to_all x1, waiting for transfers between devices, routed(): lax.all_to_all(directions.reshape(slots, 8, width), DP, 0, 0, tiled=True)  10.5 us
    ppermute x6, starting transfers between devices, swapped(): return lax.ppermute(x, CORE, [(0, 1), (1, 0)])  10.5 us
    all_to_all x1, starting transfers between devices, routed(): lax.all_to_all(directions.reshape(slots, 8, width), DP, 0, 0, tiled=True)  9.75 us
    pallas_call x3, Pallas kernels, block_sums(): pl.pallas_call(body, out_shape=[jax.ShapeDtypeStruct((len(g), rows, half_...  8.51 us
  transfers between devices with their start and end apart: 18, of which 10 were waited for; matrix products, arithmetic and copies ran while one was open for 2% of the time, Pallas kernels for 4%

profile of v3, /device:TPU:1, one launch (start us, length us, event | category | flops | bytes accessed | tf_op | source)
XLA Modules:
  0.0 135.0 jit_solution(9048346721310753871)
XLA Ops:
  0.6 3.3 %collective-permute-start = (bf16[256,8192]{1,0:T(8,128)(2,1)}, bf16[256,8192]{1,0:T(8,128)(2,1)}, u32[]{:S(2)}, u32[]{:S(2)}) collective-permute-start(bf16[256,8192]{1,0:T(8,128)(2,1)} %a_ref.1), channel_id=1, source_target_pairs={{0,4},{4,0},{1,5},{5,1},{2,6},{6,2},{3,7},{7,3},{8,12},{12,8},{9,1... | collective-permute-start | bytes 12582920 | tf_op jit(solution)/shard_map/ppermute | solution.py:30
  4.0 1.1 copy.10
  5.2 2.2 %copy-done = bf16[256,8192]{1,0:T(8,128)(2,1)S(1)} copy-done((bf16[256,8192]{1,0:T(8,128)(2,1)S(1)}, bf16[256,8192]{1,0:T(8,128)(2,1)}, u32[]{:S(2)}) %copy-start) | copy-done | bytes 4194328
  7.4 0.7 copy-done.3
  8.0 2.1 %block_sums.3 = (f32[4,128,256]{2,1,0:T(8,128)S(1)}, f32[8,128,256]{2,1,0:T(8,128)S(1)}, f32[8,128,256]{2,1,0:T(8,128)S(1)}, f32[16,128,256]{2,1,0:T(8,128)S(1)}...) custom-call(s32[64]{0:T(128)S(1)} %copy-done.3, ...), custom_call_target="tpu_custom_call" | custom-call | tf_op jit(solution)/shard_map/block_sums/pallas_call | solution.py:114
  10.1 1.0 collective-permute-done.1.k_ref
  11.1 2.7 %block_sums.5 = (bf16[4,128,256]{2,1,0:T(8,128)(2,1)S(1)}, bf16[8,128,256]{2,1,0:T(8,128)(2,1)S(1)}) custom-call(s32[64]{0:T(128)S(1)} %copy-done.3, bf16[256,8192]{1,0:T(8,128)(2,1)} %collective-permute-done.a_ref, bf16[512,256]{1,0:T(8,128)(2,1)S(1)} %collective-permute-done.1.k_ref, f32[4,128,256]{2,1,0:T(8,128)S(1)} %get-tuple-element.35.refs_0_, ...), custom_call_target="tpu_custom_call" | custom-call | tf_op jit(solution)/shard_map/block_sums/pallas_call | solution.py:114
  13.8 3.9 %collective-permute-start.2 = (bf16[4,128,256]{2,1,0:T(8,128)(2,1)S(1)}, bf16[4,128,256]{2,1,0:T(8,128)(2,1)S(1)}, u32[]{:S(2)}, u32[]{:S(2)}) collective-permute-start(bf16[4,128,256]{2,1,0:T(8,128)(2,1)S(1)} %get-tuple-element.37), channel_id=1, source_target_pairs={{0,32},{4,228},{32,64},{36,4},{64,96},{68,36},{96,128},{100,68},{1... | collective-permute-start | bytes 786440 | tf_op jit(solution)/shard_map/ppermute | solution.py:26
  17.7 2.7 %collective-permute-start.6 = (bf16[8,128,256]{2,1,0:T(8,128)(2,1)S(1)}, bf16[8,128,256]{2,1,0:T(8,128)(2,1)S(1)}, u32[]{:S(2)}, u32[]{:S(2)}) collective-permute-start(bf16[8,128,256]{2,1,0:T(8,128)(2,1)S(1)} %get-tuple-element.40), channel_id=1, source_target_pairs={{0,8},{4,28},{8,16},{12,4},{16,24},{20,12},{24,0},{28,20},{1,9},{5... | collective-permute-start | bytes 1572872 | tf_op jit(solution)/shard_map/ppermute | solution.py:26
  20.4 3.7 %block_sums.4 = (bf16[8,128,256]{2,1,0:T(8,128)(2,1)S(1)}, bf16[16,128,256]{2,1,0:T(8,128)(2,1)S(1)}, bf16[8,128,256]{2,1,0:T(8,128)(2,1)S(1)}, bf16[8,128,256]{...) custom-call(s32[64]{0:T(128)S(1)} %copy-done.3, ...), custom_call_target="tpu_custom_call" | custom-call | tf_op jit(solution)/shard_map/block_sums/pallas_call | solution.py:114
  24.4 0.8 collective-permute-start.3
  25.2 1.3 collective-permute-done.6
  26.8 3.2 %collective-permute-start.7 = (bf16[16,128,256]{2,1,0:T(8,128)(2,1)S(1)}, bf16[16,128,256]{2,1,0:T(8,128)(2,1)S(1)}, u32[]{:S(2)}, u32[]{:S(2)}) collective-permute-start(bf16[16,128,256]{2,1,0:T(8,128)(2,1)S(1)} %pad_maximum_fusion), channel_id=1, source_target_pairs={{0,8},{4,28},{8,16},{12,4},{16,24},{20,12},{24,0},{28,20},{1,9},{5... | collective-permute-start | bytes 3145736 | tf_op jit(solution)/shard_map/ppermute | solution.py:26
  30.0 2.8 %collective-permute-done.3 = bf16[8,128,256]{2,1,0:T(8,128)(2,1)S(1)} collective-permute-done((bf16[8,128,256]{2,1,0:T(8,128)(2,1)S(1)}, bf16[8,128,256]{2,1,0:T(8,128)(2,1)S(1)}, u32[]{:S(2)}, u32[]{:S(2)}) %collective-permute-start.3) | collective-permute-done | bytes 524320 | tf_op jit(solution)/shard_map/ppermute | solution.py:26
  33.0 2.0 %collective-permute-start.4 = (bf16[8,128,256]{2,1,0:T(8,128)(2,1)S(1)}, bf16[8,128,256]{2,1,0:T(8,128)(2,1)S(1)}, u32[]{:S(2)}, u32[]{:S(2)}) collective-permute-start(bf16[8,128,256]{2,1,0:T(8,128)(2,1)S(1)} %add_convert_fusion.2), channel_id=1, source_target_pairs={{0,32},{4,228},{32,64},{36,4},{64,96},{68,36},{96,128},{100,68},{1... | collective-permute-start | bytes 1572872 | tf_op jit(solution)/shard_map/ppermute | solution.py:26
  35.0 6.8 %collective-permute-done.7 = bf16[16,128,256]{2,1,0:T(8,128)(2,1)S(1)} collective-permute-done((bf16[16,128,256]{2,1,0:T(8,128)(2,1)S(1)}, bf16[16,128,256]{2,1,0:T(8,128)(2,1)S(1)}, u32[]{:S(2)}, u32[]{:S(2)}) %collective-permute-start.7) | collective-permute-done | bytes 1048608 | tf_op jit(solution)/shard_map/ppermute | solution.py:26
  42.1 3.2 %collective-permute-start.5 = (bf16[8,128,256]{2,1,0:T(8,128)(2,1)S(1)}, bf16[8,128,256]{2,1,0:T(8,128)(2,1)S(1)}, u32[]{:S(2)}, u32[]{:S(2)}) collective-permute-start(bf16[8,128,256]{2,1,0:T(8,128)(2,1)S(1)} %add_convert_fusion.1), channel_id=1, source_target_pairs={{0,32},{4,228},{32,64},{36,4},{64,96},{68,36},{96,128},{100,68},{1... | collective-permute-start | bytes 1572872 | tf_op jit(solution)/shard_map/ppermute | solution.py:26
  45.6 2.8 %collective-permute-start.13 = (bf16[3,128,256]{2,1,0:T(8,128)(2,1)S(1)}, bf16[3,128,256]{2,1,0:T(8,128)(2,1)S(1)}, u32[]{:S(2)}, u32[]{:S(2)}) collective-permute-start(bf16[3,128,256]{2,1,0:T(8,128)(2,1)S(1)} %pad_maximum_fusion.2), channel_id=1, source_target_pairs={{0,64},{4,196},{32,96},{36,228},{64,128},{68,4},{96,160},{100,36},... | collective-permute-start | bytes 589832 | tf_op jit(solution)/shard_map/ppermute | solution.py:26
  48.5 4.0 %collective-permute-done.5 = bf16[8,128,256]{2,1,0:T(8,128)(2,1)S(1)} collective-permute-done((bf16[8,128,256]{2,1,0:T(8,128)(2,1)S(1)}, bf16[8,128,256]{2,1,0:T(8,128)(2,1)S(1)}, u32[]{:S(2)}, u32[]{:S(2)}) %collective-permute-start.5) | collective-permute-done | bytes 524320 | tf_op jit(solution)/shard_map/ppermute | solution.py:26
  52.5 3.8 %collective-permute-start.9 = (bf16[4,128,256]{2,1,0:T(8,128)(2,1)S(1)}, bf16[4,128,256]{2,1,0:T(8,128)(2,1)S(1)}, u32[]{:S(2)}, u32[]{:S(2)}) collective-permute-start(bf16[4,128,256]{2,1,0:T(8,128)(2,1)S(1)} %slice.109), channel_id=1, source_target_pairs={{0,4},{4,0},{1,5},{5,1},{2,6},{6,2},{3,7},{7,3},{8,12},{12,8},{9,1... | collective-permute-start | bytes 786440 | tf_op jit(solution)/shard_map/ppermute | solution.py:30
  56.4 3.4 %collective-permute-start.14 = (bf16[2,128,256]{2,1,0:T(8,128)(2,1)S(1)}, bf16[2,128,256]{2,1,0:T(8,128)(2,1)S(1)}, u32[]{:S(2)}, u32[]{:S(2)}) collective-permute-start(bf16[2,128,256]{2,1,0:T(8,128)(2,1)S(1)} %pad_maximum_fusion.4), channel_id=1, source_target_pairs={{0,64},{4,196},{32,96},{36,228},{64,128},{68,4},{96,160},{100,36},... | collective-permute-start | bytes 393224 | tf_op jit(solution)/shard_map/ppermute | solution.py:26
  60.1 0.8 collective-permute-start.11
  61.3 2.2 %collective-permute-done.14 = bf16[2,128,256]{2,1,0:T(8,128)(2,1)S(1)} collective-permute-done((bf16[2,128,256]{2,1,0:T(8,128)(2,1)S(1)}, bf16[2,128,256]{2,1,0:T(8,128)(2,1)S(1)}, u32[]{:S(2)}, u32[]{:S(2)}) %collective-permute-start.14) | collective-permute-done | bytes 131104 | tf_op jit(solution)/shard_map/ppermute | solution.py:26
  63.4 1.1 collective-permute-done.15
  64.6 3.0 %collective-permute-start.16 = (bf16[128,256]{1,0:T(8,128)(2,1)S(1)}, bf16[128,256]{1,0:T(8,128)(2,1)S(1)}, u32[]{:S(2)}, u32[]{:S(2)}) collective-permute-start(bf16[128,256]{1,0:T(8,128)(2,1)S(1)} %fusion.8), channel_id=1, source_target_pairs={{0,4},{4,0},{1,5},{5,1},{2,6},{6,2},{3,7},{7,3},{8,12},{12,8},{9,1... | collective-permute-start | bytes 196616 | tf_op jit(solution)/shard_map/ppermute | solution.py:30
  67.8 0.7 collective-permute-done.16.refs_7_
  68.5 0.5 collective-permute-done.12.refs_3_
  68.9 17.0 %precondition.1 = (f32[512,512]{1,0:T(8,128)}, f32[128,128]{1,0:T(8,128)}, bf16[512,128]{1,0:T(8,128)(2,1)}) custom-call(f32[128,256]{1,0:T(8,128)S(1)} %slice_bitcast_fusion.1.refs_0_, bf16[128,256]{1,0:T(8,128)(2,1)S(1)} %bitcast.35, bf16[128,256]{1,0:T(8,128)(2,1)S(1)} %get-tuple-element.63.refs_2_, bf16[128,256]{1,0:T(8,128)(2,1)S(1)} %collective-permute-done.12.refs_3_, ...), custom_call_target="tpu_custom_call" | custom-call | tf_op jit(solution)/shard_map/precondition/pallas_call | solution.py:214
  86.0 9.8 %all-to-all-start = ((bf16[64,8,128]{2,1,0:T(8,128)(2,1)}), bf16[64,8,128]{2,1,0:T(8,128)(2,1)S(1)}, u32[]{:S(2)}, u32[]{:S(2)}) async-start(bf16[64,8,128]{2,1,0:T(8,128)(2,1)} %bitcast.15), calls=%async_computation | async-start | bytes 262144 | tf_op jit(solution)/shard_map/all_to_all | solution.py:259
  96.3 10.5 %all-to-all-done = bf16[64,8,128]{2,1,0:T(8,128)(2,1)S(1)} async-done(((bf16[64,8,128]{2,1,0:T(8,128)(2,1)}), bf16[64,8,128]{2,1,0:T(8,128)(2,1)S(1)}, u32[]{:S(2)}, u32[]{:S(2)}) %all-to-all-start) | async-done | bytes 131104 | tf_op jit(solution)/shard_map/all_to_all | solution.py:259
  107.3 26.3 %all_to_all.10 = bf16[256,8,128]{2,1,0:T(8,128)(2,1)S(1)} all-to-all(bf16[256,8,128]{2,1,0:T(8,128)(2,1)S(1)} %bitcast.36), channel_id=1, replica_groups=mesh['dp_0'=8,'dp_1'=4,'dp_2'=2,'tensor'=4] {'dp_0','dp_1','dp_2','tensor'}, dimensions={0} | all-to-all | bytes 1048576 | tf_op jit(solution)/shard_map/all_to_all | solution.py:268
  133.6 1.5 %placed.1 = bf16[2,128,1024]{2,1,0:T(8,128)(2,1)} custom-call(bf16[2048,128]{1,0:T(8,128)(2,1)S(1)} %bitcast.30), custom_call_target="tpu_custom_call" | custom-call | tf_op jit(solution)/shard_map/placed/pallas_call | solution.py:244
  (55 shorter events, 3.2 us)
Async XLA Ops:
  0.6 10.5 %collective-permute-start = (bf16[256,8192]{1,0:T(8,128)(2,1)}, bf16[256,8192]{1,0:T(8,128)(2,1)}, u32[]{:S(2)}, u32[]{:S(2)}) collective-permute-start(bf16[256,8192]{1,0:T(8,128)(2,1)} %a_ref.1), channel_id=1, source_target_pairs={{0,4},{4,0},{1,5},{5,1},{2,6},{6,2},{3,7},{7,3},{8,12},{12,8},{9,1... | collective-permute-start | bytes 12582920 | tf_op jit(solution)/shard_map/ppermute | solution.py:30
  5.1 6.1 %collective-permute-start.1 = (bf16[512,256]{1,0:T(8,128)(2,1)S(1)}, bf16[512,256]{1,0:T(8,128)(2,1)S(1)}, u32[]{:S(2)}, u32[]{:S(2)}) collective-permute-start(bf16[512,256]{1,0:T(8,128)(2,1)S(1)} %bitcast.32), channel_id=1, source_target_pairs={{0,4},{4,0},{1,5},{5,1},{2,6},{6,2},{3,7},{7,3},{8,12},{12,8},{9,1... | collective-permute-start | bytes 786440 | tf_op jit(solution)/shard_map/ppermute | solution.py:30
  5.2 2.2 %copy-start = (bf16[256,8192]{1,0:T(8,128)(2,1)S(1)}, bf16[256,8192]{1,0:T(8,128)(2,1)}, u32[]{:S(2)}) copy-start(bf16[256,8192]{1,0:T(8,128)(2,1)} %a_ref.1) | copy-start | bytes 12582916
  7.4 0.7 copy-start.3
  13.8 10.5 %collective-permute-start.2 = (bf16[4,128,256]{2,1,0:T(8,128)(2,1)S(1)}, bf16[4,128,256]{2,1,0:T(8,128)(2,1)S(1)}, u32[]{:S(2)}, u32[]{:S(2)}) collective-permute-start(bf16[4,128,256]{2,1,0:T(8,128)(2,1)S(1)} %get-tuple-element.37), channel_id=1, source_target_pairs={{0,32},{4,228},{32,64},{36,4},{64,96},{68,36},{96,128},{100,68},{1... | collective-permute-start | bytes 786440 | tf_op jit(solution)/shard_map/ppermute | solution.py:26
  17.7 8.8 %collective-permute-start.6 = (bf16[8,128,256]{2,1,0:T(8,128)(2,1)S(1)}, bf16[8,128,256]{2,1,0:T(8,128)(2,1)S(1)}, u32[]{:S(2)}, u32[]{:S(2)}) collective-permute-start(bf16[8,128,256]{2,1,0:T(8,128)(2,1)S(1)} %get-tuple-element.40), channel_id=1, source_target_pairs={{0,8},{4,28},{8,16},{12,4},{16,24},{20,12},{24,0},{28,20},{1,9},{5... | collective-permute-start | bytes 1572872 | tf_op jit(solution)/shard_map/ppermute | solution.py:26
  24.4 8.4 %collective-permute-start.3 = (bf16[8,128,256]{2,1,0:T(8,128)(2,1)S(1)}, bf16[8,128,256]{2,1,0:T(8,128)(2,1)S(1)}, u32[]{:S(2)}, u32[]{:S(2)}) collective-permute-start(bf16[8,128,256]{2,1,0:T(8,128)(2,1)S(1)} %pad_maximum_fusion.1), channel_id=1, source_target_pairs={{0,32},{4,228},{32,64},{36,4},{64,96},{68,36},{96,128},{100,68},{1... | collective-permute-start | bytes 1572872 | tf_op jit(solution)/shard_map/ppermute | solution.py:26
  26.8 14.9 %collective-permute-start.7 = (bf16[16,128,256]{2,1,0:T(8,128)(2,1)S(1)}, bf16[16,128,256]{2,1,0:T(8,128)(2,1)S(1)}, u32[]{:S(2)}, u32[]{:S(2)}) collective-permute-start(bf16[16,128,256]{2,1,0:T(8,128)(2,1)S(1)} %pad_maximum_fusion), channel_id=1, source_target_pairs={{0,8},{4,28},{8,16},{12,4},{16,24},{20,12},{24,0},{28,20},{1,9},{5... | collective-permute-start | bytes 3145736 | tf_op jit(solution)/shard_map/ppermute | solution.py:26
  33.0 9.0 %collective-permute-start.4 = (bf16[8,128,256]{2,1,0:T(8,128)(2,1)S(1)}, bf16[8,128,256]{2,1,0:T(8,128)(2,1)S(1)}, u32[]{:S(2)}, u32[]{:S(2)}) collective-permute-start(bf16[8,128,256]{2,1,0:T(8,128)(2,1)S(1)} %add_convert_fusion.2), channel_id=1, source_target_pairs={{0,32},{4,228},{32,64},{36,4},{64,96},{68,36},{96,128},{100,68},{1... | collective-permute-start | bytes 1572872 | tf_op jit(solution)/shard_map/ppermute | solution.py:26
  41.8 3.5 %collective-permute-start.8 = (bf16[8,128,256]{2,1,0:T(8,128)(2,1)S(1)}, bf16[8,128,256]{2,1,0:T(8,128)(2,1)S(1)}, u32[]{:S(2)}, u32[]{:S(2)}) collective-permute-start(bf16[8,128,256]{2,1,0:T(8,128)(2,1)S(1)} %slice.132), channel_id=1, source_target_pairs={{0,4},{4,0},{1,5},{5,1},{2,6},{6,2},{3,7},{7,3},{8,12},{12,8},{9,1... | collective-permute-start | bytes 1572872 | tf_op jit(solution)/shard_map/ppermute | solution.py:30
  42.1 10.4 %collective-permute-start.5 = (bf16[8,128,256]{2,1,0:T(8,128)(2,1)S(1)}, bf16[8,128,256]{2,1,0:T(8,128)(2,1)S(1)}, u32[]{:S(2)}, u32[]{:S(2)}) collective-permute-start(bf16[8,128,256]{2,1,0:T(8,128)(2,1)S(1)} %add_convert_fusion.1), channel_id=1, source_target_pairs={{0,32},{4,228},{32,64},{36,4},{64,96},{68,36},{96,128},{100,68},{1... | collective-permute-start | bytes 1572872 | tf_op jit(solution)/shard_map/ppermute | solution.py:26
  45.3 23.6 %copy-start.1 = (f32[1,1,512,512]{3,2,1,0:T(8,128)S(1)}, f32[1,1,512,512]{3,2,1,0:T(8,128)}, u32[]{:S(2)}) copy-start(f32[1,1,512,512]{3,2,1,0:T(8,128)} %param.8) | copy-start | bytes 3145732
  45.3 23.6 %copy-start.2 = (f32[1,1,128,128]{3,2,1,0:T(8,128)S(1)}, f32[1,1,128,128]{3,2,1,0:T(8,128)}, u32[]{:S(2)}) copy-start(f32[1,1,128,128]{3,2,1,0:T(8,128)} %param.9) | copy-start | bytes 196612
  45.5 50.2 %copy-start.4 = (s32[64]{0:T(128)S(1)}, s32[64]{0:T(128)}, u32[]{:S(2)}) copy-start(s32[64]{0:T(128)} %owner_ref.5) | copy-start | bytes 772
  45.6 10.7 %collective-permute-start.13 = (bf16[3,128,256]{2,1,0:T(8,128)(2,1)S(1)}, bf16[3,128,256]{2,1,0:T(8,128)(2,1)S(1)}, u32[]{:S(2)}, u32[]{:S(2)}) collective-permute-start(bf16[3,128,256]{2,1,0:T(8,128)(2,1)S(1)} %pad_maximum_fusion.2), channel_id=1, source_target_pairs={{0,64},{4,196},{32,96},{36,228},{64,128},{68,4},{96,160},{100,36},... | collective-permute-start | bytes 589832 | tf_op jit(solution)/shard_map/ppermute | solution.py:26
  52.5 7.4 %collective-permute-start.9 = (bf16[4,128,256]{2,1,0:T(8,128)(2,1)S(1)}, bf16[4,128,256]{2,1,0:T(8,128)(2,1)S(1)}, u32[]{:S(2)}, u32[]{:S(2)}) collective-permute-start(bf16[4,128,256]{2,1,0:T(8,128)(2,1)S(1)} %slice.109), channel_id=1, source_target_pairs={{0,4},{4,0},{1,5},{5,1},{2,6},{6,2},{3,7},{7,3},{8,12},{12,8},{9,1... | collective-permute-start | bytes 786440 | tf_op jit(solution)/shard_map/ppermute | solution.py:30
  56.4 7.0 %collective-permute-start.14 = (bf16[2,128,256]{2,1,0:T(8,128)(2,1)S(1)}, bf16[2,128,256]{2,1,0:T(8,128)(2,1)S(1)}, u32[]{:S(2)}, u32[]{:S(2)}) collective-permute-start(bf16[2,128,256]{2,1,0:T(8,128)(2,1)S(1)} %pad_maximum_fusion.4), channel_id=1, source_target_pairs={{0,64},{4,196},{32,96},{36,228},{64,128},{68,4},{96,160},{100,36},... | collective-permute-start | bytes 393224 | tf_op jit(solution)/shard_map/ppermute | solution.py:26
  59.9 4.7 %collective-permute-start.15 = (bf16[2,128,256]{2,1,0:T(8,128)(2,1)S(1)}, bf16[2,128,256]{2,1,0:T(8,128)(2,1)S(1)}, u32[]{:S(2)}, u32[]{:S(2)}) collective-permute-start(bf16[2,128,256]{2,1,0:T(8,128)(2,1)S(1)} %pad_maximum_fusion.5), channel_id=1, source_target_pairs={{0,32},{4,228},{32,64},{36,4},{64,96},{68,36},{96,128},{100,68},{1... | collective-permute-start | bytes 393224 | tf_op jit(solution)/shard_map/ppermute | solution.py:26
  60.1 7.4 %collective-permute-start.11 = (bf16[2,128,256]{2,1,0:T(8,128)(2,1)S(1)}, bf16[2,128,256]{2,1,0:T(8,128)(2,1)S(1)}, u32[]{:S(2)}, u32[]{:S(2)}) collective-permute-start(bf16[2,128,256]{2,1,0:T(8,128)(2,1)S(1)} %pad_maximum_fusion.3), channel_id=1, source_target_pairs={{0,8},{4,28},{8,16},{12,4},{16,24},{20,12},{24,0},{28,20},{1,9},{5... | collective-permute-start | bytes 393224 | tf_op jit(solution)/shard_map/ppermute | solution.py:26
  61.0 6.8 %collective-permute-start.10 = (bf16[1,128,256]{2,1,0:T(8,128)(2,1)S(1)}, bf16[1,128,256]{2,1,0:T(8,128)(2,1)S(1)}, u32[]{:S(2)}, u32[]{:S(2)}) collective-permute-start(bf16[1,128,256]{2,1,0:T(8,128)(2,1)S(1)} %get-tuple-element.61), channel_id=1, source_target_pairs={{0,16},{4,20},{8,24},{12,28},{16,0},{20,4},{24,8},{28,12},{1,17},{... | collective-permute-start | bytes 196616 | tf_op jit(solution)/shard_map/ppermute | solution.py:26
  64.6 3.9 %collective-permute-start.16 = (bf16[128,256]{1,0:T(8,128)(2,1)S(1)}, bf16[128,256]{1,0:T(8,128)(2,1)S(1)}, u32[]{:S(2)}, u32[]{:S(2)}) collective-permute-start(bf16[128,256]{1,0:T(8,128)(2,1)S(1)} %fusion.8), channel_id=1, source_target_pairs={{0,4},{4,0},{1,5},{5,1},{2,6},{6,2},{3,7},{7,3},{8,12},{12,8},{9,1... | collective-permute-start | bytes 196616 | tf_op jit(solution)/shard_map/ppermute | solution.py:30
  67.6 1.3 collective-permute-start.12
  86.0 20.9 %all-to-all-start = ((bf16[64,8,128]{2,1,0:T(8,128)(2,1)}), bf16[64,8,128]{2,1,0:T(8,128)(2,1)S(1)}, u32[]{:S(2)}, u32[]{:S(2)}) async-start(bf16[64,8,128]{2,1,0:T(8,128)(2,1)} %bitcast.15), calls=%async_computation | async-start | bytes 262144 | tf_op jit(solution)/shard_map/all_to_all | solution.py:259

commit v4 on v3

--- a/solution.py
+++ b/solution.py
@@ -141,7 +141,11 @@
 
 
 def exact(a, b):
-    return jnp.dot(a, b, precision=lax.Precision.HIGHEST, preferred_element_type=F32)
+    ah = a.astype(BF16)
+    al = (a - ah.astype(F32)).astype(BF16)
+    bh = b.astype(BF16)
+    bl = (b - bh.astype(F32)).astype(BF16)
+    return coarse(ah, bh) + (coarse(ah, bl) + coarse(al, bh))
 
 
 def start_root(matrix, f_ref, m_ref, x_ref):
@@ -155,16 +159,7 @@
     first = jnp.sqrt(jnp.sqrt(scaling)).astype(BF16).astype(F32)
     f_ref[...] = factor
     m_ref[...] = powered.astype(BF16)
-    x_ref[...] = (first * factor.astype(F32)).astype(BF16)
-
-
-def advance_power(f_ref, m_ref, eye):
-    factor = f_ref[...]
-    squared = coarse(factor, factor).astype(BF16)
-    fourth = coarse(squared, squared).astype(BF16)
-    powered = coarse(fourth, m_ref[...])
-    f_ref[...] = narrow_factor(powered, eye)
-    m_ref[...] = powered.astype(BF16)
+    x_ref[...] = jnp.where(eye, first, 0.0).astype(BF16)
 
 
 def precondition(parts_a, parts_b, left, right, inverse_tokens):
@@ -187,16 +182,21 @@
         right_out[...] = right_new
         start_root(right_new, fr, mr, xr)
 
-        def step(_, carry):
-            advance_power(fl, ml, spread_eye(order))
-            advance_power(fr, mr, spread_eye(width))
-            xl[...] = coarse(xl[...], fl[...]).astype(BF16)
-            xr[...] = coarse(xr[...], fr[...]).astype(BF16)
-            return carry
-
-        lax.fori_loop(0, ITERS - 2, step, 0)
-        advance_power(fl, ml, spread_eye(order))
-        advance_power(fr, mr, spread_eye(width))
+        eye_l, eye_r = spread_eye(order), spread_eye(width)
+        for _ in range(ITERS - 1):
+            factor_l, factor_r = fl[...], fr[...]
+            squared_l = coarse(factor_l, factor_l).astype(BF16)
+            squared_r = coarse(factor_r, factor_r).astype(BF16)
+            xl[...] = coarse(xl[...], factor_l).astype(BF16)
+            fourth_l = coarse(squared_l, squared_l).astype(BF16)
+            fourth_r = coarse(squared_r, squared_r).astype(BF16)
+            xr[...] = coarse(xr[...], factor_r).astype(BF16)
+            powered_l = coarse(fourth_l, ml[...])
+            powered_r = coarse(fourth_r, mr[...])
+            fl[...] = narrow_factor(powered_l, eye_l)
+            fr[...] = narrow_factor(powered_r, eye_r)
+            ml[...] = powered_l.astype(BF16)
+            mr[...] = powered_r.astype(BF16)
         left_root = coarse(xl[...], fl[...])
         right_root = coarse(xr[...], fr[...])
         pre = exact(exact(left_root, g_ref[...]), right_root)

time: 135 us -> 131 us (0.970)
  Pallas kernels: 27 us -> 22.3 us
    pallas_call x1, Pallas kernels: 17 us -> 12.3 us  [precondition(): pl.pallas_call(body, out_shape=[jax.ShapeDtypeStruct(left.shape, F32), ja...]
where the time goes in v4:
time: 131 us; the launch traced here: 130 us
  starting transfers between devices  43.6 us (33%)
  waiting for transfers between devices  30.8 us (24%)
  blocking collectives  26.3 us (20%)
  Pallas kernels  22.3 us (17%)
  local copies, waits for them, and re-layouts  4.68 us (4%)
  other arithmetic  1.32 us (1%)
    all_to_all x1, blocking collectives, routed(): got = lax.all_to_all(copies, (*DP, 'tensor'), 0, 0, tiled=True)  26.3 us
    ppermute x11, starting transfers between devices, directed(): return lax.ppermute(x, (axis, CORE), pairs)  23.3 us
    ppermute x11, waiting for transfers between devices, directed(): return lax.ppermute(x, (axis, CORE), pairs)  18.1 us
    pallas_call x1, Pallas kernels, precondition(): pl.pallas_call(body, out_shape=[jax.ShapeDtypeStruct(left.shape, F32), ja...  12.3 us
    ppermute x6, starting transfers between devices, swapped(): return lax.ppermute(x, CORE, [(0, 1), (1, 0)])  10.5 us
    all_to_all x1, waiting for transfers between devices, routed(): lax.all_to_all(directions.reshape(slots, 8, width), DP, 0, 0, tiled=True)  10.5 us
    all_to_all x1, starting transfers between devices, routed(): lax.all_to_all(directions.reshape(slots, 8, width), DP, 0, 0, tiled=True)  9.76 us
    pallas_call x3, Pallas kernels, block_sums(): pl.pallas_call(body, out_shape=[jax.ShapeDtypeStruct((len(g), rows, half_...  8.51 us
  transfers between devices with their start and end apart: 18, of which 10 were waited for; matrix products, arithmetic and copies ran while one was open for 2% of the time, Pallas kernels for 4%

profile of v4, /device:TPU:1, one launch (start us, length us, event | category | flops | bytes accessed | tf_op | source)
XLA Modules:
  0.0 130.3 jit_solution(3823595426810631578)
XLA Ops:
  0.6 3.3 %collective-permute-start = (bf16[256,8192]{1,0:T(8,128)(2,1)}, bf16[256,8192]{1,0:T(8,128)(2,1)}, u32[]{:S(2)}, u32[]{:S(2)}) collective-permute-start(bf16[256,8192]{1,0:T(8,128)(2,1)} %a_ref.1), channel_id=1, source_target_pairs={{0,4},{4,0},{1,5},{5,1},{2,6},{6,2},{3,7},{7,3},{8,12},{12,8},{9,1... | collective-permute-start | bytes 12582920 | tf_op jit(solution)/shard_map/ppermute | solution.py:30
  4.0 1.1 copy.10
  5.2 2.2 %copy-done = bf16[256,8192]{1,0:T(8,128)(2,1)S(1)} copy-done((bf16[256,8192]{1,0:T(8,128)(2,1)S(1)}, bf16[256,8192]{1,0:T(8,128)(2,1)}, u32[]{:S(2)}) %copy-start) | copy-done | bytes 4194328
  7.4 0.7 copy-done.3
  8.0 2.1 %block_sums.3 = (f32[4,128,256]{2,1,0:T(8,128)S(1)}, f32[8,128,256]{2,1,0:T(8,128)S(1)}, f32[8,128,256]{2,1,0:T(8,128)S(1)}, f32[16,128,256]{2,1,0:T(8,128)S(1)}...) custom-call(s32[64]{0:T(128)S(1)} %copy-done.3, ...), custom_call_target="tpu_custom_call" | custom-call | tf_op jit(solution)/shard_map/block_sums/pallas_call | solution.py:114
  10.1 1.0 collective-permute-done.1.k_ref
  11.1 2.7 %block_sums.5 = (bf16[4,128,256]{2,1,0:T(8,128)(2,1)S(1)}, bf16[8,128,256]{2,1,0:T(8,128)(2,1)S(1)}) custom-call(s32[64]{0:T(128)S(1)} %copy-done.3, bf16[256,8192]{1,0:T(8,128)(2,1)} %collective-permute-done.a_ref, bf16[512,256]{1,0:T(8,128)(2,1)S(1)} %collective-permute-done.1.k_ref, f32[4,128,256]{2,1,0:T(8,128)S(1)} %get-tuple-element.35.refs_0_, ...), custom_call_target="tpu_custom_call" | custom-call | tf_op jit(solution)/shard_map/block_sums/pallas_call | solution.py:114
  13.8 3.9 %collective-permute-start.2 = (bf16[4,128,256]{2,1,0:T(8,128)(2,1)S(1)}, bf16[4,128,256]{2,1,0:T(8,128)(2,1)S(1)}, u32[]{:S(2)}, u32[]{:S(2)}) collective-permute-start(bf16[4,128,256]{2,1,0:T(8,128)(2,1)S(1)} %get-tuple-element.37), channel_id=1, source_target_pairs={{0,32},{4,228},{32,64},{36,4},{64,96},{68,36},{96,128},{100,68},{1... | collective-permute-start | bytes 786440 | tf_op jit(solution)/shard_map/ppermute | solution.py:26
  17.7 2.7 %collective-permute-start.6 = (bf16[8,128,256]{2,1,0:T(8,128)(2,1)S(1)}, bf16[8,128,256]{2,1,0:T(8,128)(2,1)S(1)}, u32[]{:S(2)}, u32[]{:S(2)}) collective-permute-start(bf16[8,128,256]{2,1,0:T(8,128)(2,1)S(1)} %get-tuple-element.40), channel_id=1, source_target_pairs={{0,8},{4,28},{8,16},{12,4},{16,24},{20,12},{24,0},{28,20},{1,9},{5... | collective-permute-start | bytes 1572872 | tf_op jit(solution)/shard_map/ppermute | solution.py:26
  20.4 3.7 %block_sums.4 = (bf16[8,128,256]{2,1,0:T(8,128)(2,1)S(1)}, bf16[16,128,256]{2,1,0:T(8,128)(2,1)S(1)}, bf16[8,128,256]{2,1,0:T(8,128)(2,1)S(1)}, bf16[8,128,256]{...) custom-call(s32[64]{0:T(128)S(1)} %copy-done.3, ...), custom_call_target="tpu_custom_call" | custom-call | tf_op jit(solution)/shard_map/block_sums/pallas_call | solution.py:114
  24.5 0.8 collective-permute-start.3
  25.3 1.3 collective-permute-done.6
  26.9 3.2 %collective-permute-start.7 = (bf16[16,128,256]{2,1,0:T(8,128)(2,1)S(1)}, bf16[16,128,256]{2,1,0:T(8,128)(2,1)S(1)}, u32[]{:S(2)}, u32[]{:S(2)}) collective-permute-start(bf16[16,128,256]{2,1,0:T(8,128)(2,1)S(1)} %pad_maximum_fusion), channel_id=1, source_target_pairs={{0,8},{4,28},{8,16},{12,4},{16,24},{20,12},{24,0},{28,20},{1,9},{5... | collective-permute-start | bytes 3145736 | tf_op jit(solution)/shard_map/ppermute | solution.py:26
  30.0 2.8 %collective-permute-done.3 = bf16[8,128,256]{2,1,0:T(8,128)(2,1)S(1)} collective-permute-done((bf16[8,128,256]{2,1,0:T(8,128)(2,1)S(1)}, bf16[8,128,256]{2,1,0:T(8,128)(2,1)S(1)}, u32[]{:S(2)}, u32[]{:S(2)}) %collective-permute-start.3) | collective-permute-done | bytes 524320 | tf_op jit(solution)/shard_map/ppermute | solution.py:26
  33.0 2.0 %collective-permute-start.4 = (bf16[8,128,256]{2,1,0:T(8,128)(2,1)S(1)}, bf16[8,128,256]{2,1,0:T(8,128)(2,1)S(1)}, u32[]{:S(2)}, u32[]{:S(2)}) collective-permute-start(bf16[8,128,256]{2,1,0:T(8,128)(2,1)S(1)} %add_convert_fusion.2), channel_id=1, source_target_pairs={{0,32},{4,228},{32,64},{36,4},{64,96},{68,36},{96,128},{100,68},{1... | collective-permute-start | bytes 1572872 | tf_op jit(solution)/shard_map/ppermute | solution.py:26
  35.0 6.8 %collective-permute-done.7 = bf16[16,128,256]{2,1,0:T(8,128)(2,1)S(1)} collective-permute-done((bf16[16,128,256]{2,1,0:T(8,128)(2,1)S(1)}, bf16[16,128,256]{2,1,0:T(8,128)(2,1)S(1)}, u32[]{:S(2)}, u32[]{:S(2)}) %collective-permute-start.7) | collective-permute-done | bytes 1048608 | tf_op jit(solution)/shard_map/ppermute | solution.py:26
  42.1 3.2 %collective-permute-start.5 = (bf16[8,128,256]{2,1,0:T(8,128)(2,1)S(1)}, bf16[8,128,256]{2,1,0:T(8,128)(2,1)S(1)}, u32[]{:S(2)}, u32[]{:S(2)}) collective-permute-start(bf16[8,128,256]{2,1,0:T(8,128)(2,1)S(1)} %add_convert_fusion.1), channel_id=1, source_target_pairs={{0,32},{4,228},{32,64},{36,4},{64,96},{68,36},{96,128},{100,68},{1... | collective-permute-start | bytes 1572872 | tf_op jit(solution)/shard_map/ppermute | solution.py:26
  45.6 2.8 %collective-permute-start.13 = (bf16[3,128,256]{2,1,0:T(8,128)(2,1)S(1)}, bf16[3,128,256]{2,1,0:T(8,128)(2,1)S(1)}, u32[]{:S(2)}, u32[]{:S(2)}) collective-permute-start(bf16[3,128,256]{2,1,0:T(8,128)(2,1)S(1)} %pad_maximum_fusion.2), channel_id=1, source_target_pairs={{0,64},{4,196},{32,96},{36,228},{64,128},{68,4},{96,160},{100,36},... | collective-permute-start | bytes 589832 | tf_op jit(solution)/shard_map/ppermute | solution.py:26
  48.4 4.0 %collective-permute-done.5 = bf16[8,128,256]{2,1,0:T(8,128)(2,1)S(1)} collective-permute-done((bf16[8,128,256]{2,1,0:T(8,128)(2,1)S(1)}, bf16[8,128,256]{2,1,0:T(8,128)(2,1)S(1)}, u32[]{:S(2)}, u32[]{:S(2)}) %collective-permute-start.5) | collective-permute-done | bytes 524320 | tf_op jit(solution)/shard_map/ppermute | solution.py:26
  52.5 3.8 %collective-permute-start.9 = (bf16[4,128,256]{2,1,0:T(8,128)(2,1)S(1)}, bf16[4,128,256]{2,1,0:T(8,128)(2,1)S(1)}, u32[]{:S(2)}, u32[]{:S(2)}) collective-permute-start(bf16[4,128,256]{2,1,0:T(8,128)(2,1)S(1)} %slice.109), channel_id=1, source_target_pairs={{0,4},{4,0},{1,5},{5,1},{2,6},{6,2},{3,7},{7,3},{8,12},{12,8},{9,1... | collective-permute-start | bytes 786440 | tf_op jit(solution)/shard_map/ppermute | solution.py:30
  56.4 3.4 %collective-permute-start.14 = (bf16[2,128,256]{2,1,0:T(8,128)(2,1)S(1)}, bf16[2,128,256]{2,1,0:T(8,128)(2,1)S(1)}, u32[]{:S(2)}, u32[]{:S(2)}) collective-permute-start(bf16[2,128,256]{2,1,0:T(8,128)(2,1)S(1)} %pad_maximum_fusion.4), channel_id=1, source_target_pairs={{0,64},{4,196},{32,96},{36,228},{64,128},{68,4},{96,160},{100,36},... | collective-permute-start | bytes 393224 | tf_op jit(solution)/shard_map/ppermute | solution.py:26
  60.1 0.8 collective-permute-start.11
  61.3 2.2 %collective-permute-done.14 = bf16[2,128,256]{2,1,0:T(8,128)(2,1)S(1)} collective-permute-done((bf16[2,128,256]{2,1,0:T(8,128)(2,1)S(1)}, bf16[2,128,256]{2,1,0:T(8,128)(2,1)S(1)}, u32[]{:S(2)}, u32[]{:S(2)}) %collective-permute-start.14) | collective-permute-done | bytes 131104 | tf_op jit(solution)/shard_map/ppermute | solution.py:26
  63.4 1.1 collective-permute-done.15
  64.6 3.0 %collective-permute-start.16 = (bf16[128,256]{1,0:T(8,128)(2,1)S(1)}, bf16[128,256]{1,0:T(8,128)(2,1)S(1)}, u32[]{:S(2)}, u32[]{:S(2)}) collective-permute-start(bf16[128,256]{1,0:T(8,128)(2,1)S(1)} %fusion.8), channel_id=1, source_target_pairs={{0,4},{4,0},{1,5},{5,1},{2,6},{6,2},{3,7},{7,3},{8,12},{12,8},{9,1... | collective-permute-start | bytes 196616 | tf_op jit(solution)/shard_map/ppermute | solution.py:30
  67.8 0.7 collective-permute-done.16.refs_7_
  68.4 0.5 collective-permute-done.12.refs_3_
  68.9 12.3 %precondition.1 = (f32[512,512]{1,0:T(8,128)}, f32[128,128]{1,0:T(8,128)}, bf16[512,128]{1,0:T(8,128)(2,1)}) custom-call(f32[128,256]{1,0:T(8,128)S(1)} %slice_bitcast_fusion.1.refs_0_, bf16[128,256]{1,0:T(8,128)(2,1)S(1)} %bitcast.35, bf16[128,256]{1,0:T(8,128)(2,1)S(1)} %get-tuple-element.63.refs_2_, bf16[128,256]{1,0:T(8,128)(2,1)S(1)} %collective-permute-done.12.refs_3_, ...), custom_call_target="tpu_custom_call" | custom-call | tf_op jit(solution)/shard_map/precondition/pallas_call | solution.py:214
  81.2 9.8 %all-to-all-start = ((bf16[64,8,128]{2,1,0:T(8,128)(2,1)}), bf16[64,8,128]{2,1,0:T(8,128)(2,1)S(1)}, u32[]{:S(2)}, u32[]{:S(2)}) async-start(bf16[64,8,128]{2,1,0:T(8,128)(2,1)} %bitcast.15), calls=%async_computation | async-start | bytes 262144 | tf_op jit(solution)/shard_map/all_to_all | solution.py:259
  91.6 10.5 %all-to-all-done = bf16[64,8,128]{2,1,0:T(8,128)(2,1)S(1)} async-done(((bf16[64,8,128]{2,1,0:T(8,128)(2,1)}), bf16[64,8,128]{2,1,0:T(8,128)(2,1)S(1)}, u32[]{:S(2)}, u32[]{:S(2)}) %all-to-all-start) | async-done | bytes 131104 | tf_op jit(solution)/shard_map/all_to_all | solution.py:259
  102.6 26.3 %all_to_all.10 = bf16[256,8,128]{2,1,0:T(8,128)(2,1)S(1)} all-to-all(bf16[256,8,128]{2,1,0:T(8,128)(2,1)S(1)} %bitcast.36), channel_id=1, replica_groups=mesh['dp_0'=8,'dp_1'=4,'dp_2'=2,'tensor'=4] {'dp_0','dp_1','dp_2','tensor'}, dimensions={0} | all-to-all | bytes 1048576 | tf_op jit(solution)/shard_map/all_to_all | solution.py:268
  128.9 1.5 %placed.1 = bf16[2,128,1024]{2,1,0:T(8,128)(2,1)} custom-call(bf16[2048,128]{1,0:T(8,128)(2,1)S(1)} %bitcast.30), custom_call_target="tpu_custom_call" | custom-call | tf_op jit(solution)/shard_map/placed/pallas_call | solution.py:244
  (55 shorter events, 3.2 us)
Async XLA Ops:
  0.6 10.5 %collective-permute-start = (bf16[256,8192]{1,0:T(8,128)(2,1)}, bf16[256,8192]{1,0:T(8,128)(2,1)}, u32[]{:S(2)}, u32[]{:S(2)}) collective-permute-start(bf16[256,8192]{1,0:T(8,128)(2,1)} %a_ref.1), channel_id=1, source_target_pairs={{0,4},{4,0},{1,5},{5,1},{2,6},{6,2},{3,7},{7,3},{8,12},{12,8},{9,1... | collective-permute-start | bytes 12582920 | tf_op jit(solution)/shard_map/ppermute | solution.py:30
  5.1 6.1 %collective-permute-start.1 = (bf16[512,256]{1,0:T(8,128)(2,1)S(1)}, bf16[512,256]{1,0:T(8,128)(2,1)S(1)}, u32[]{:S(2)}, u32[]{:S(2)}) collective-permute-start(bf16[512,256]{1,0:T(8,128)(2,1)S(1)} %bitcast.32), channel_id=1, source_target_pairs={{0,4},{4,0},{1,5},{5,1},{2,6},{6,2},{3,7},{7,3},{8,12},{12,8},{9,1... | collective-permute-start | bytes 786440 | tf_op jit(solution)/shard_map/ppermute | solution.py:30
  5.2 2.2 %copy-start = (bf16[256,8192]{1,0:T(8,128)(2,1)S(1)}, bf16[256,8192]{1,0:T(8,128)(2,1)}, u32[]{:S(2)}) copy-start(bf16[256,8192]{1,0:T(8,128)(2,1)} %a_ref.1) | copy-start | bytes 12582916
  7.4 0.7 copy-start.3
  13.8 10.5 %collective-permute-start.2 = (bf16[4,128,256]{2,1,0:T(8,128)(2,1)S(1)}, bf16[4,128,256]{2,1,0:T(8,128)(2,1)S(1)}, u32[]{:S(2)}, u32[]{:S(2)}) collective-permute-start(bf16[4,128,256]{2,1,0:T(8,128)(2,1)S(1)} %get-tuple-element.37), channel_id=1, source_target_pairs={{0,32},{4,228},{32,64},{36,4},{64,96},{68,36},{96,128},{100,68},{1... | collective-permute-start | bytes 786440 | tf_op jit(solution)/shard_map/ppermute | solution.py:26
  17.7 8.9 %collective-permute-start.6 = (bf16[8,128,256]{2,1,0:T(8,128)(2,1)S(1)}, bf16[8,128,256]{2,1,0:T(8,128)(2,1)S(1)}, u32[]{:S(2)}, u32[]{:S(2)}) collective-permute-start(bf16[8,128,256]{2,1,0:T(8,128)(2,1)S(1)} %get-tuple-element.40), channel_id=1, source_target_pairs={{0,8},{4,28},{8,16},{12,4},{16,24},{20,12},{24,0},{28,20},{1,9},{5... | collective-permute-start | bytes 1572872 | tf_op jit(solution)/shard_map/ppermute | solution.py:26
  24.5 8.4 %collective-permute-start.3 = (bf16[8,128,256]{2,1,0:T(8,128)(2,1)S(1)}, bf16[8,128,256]{2,1,0:T(8,128)(2,1)S(1)}, u32[]{:S(2)}, u32[]{:S(2)}) collective-permute-start(bf16[8,128,256]{2,1,0:T(8,128)(2,1)S(1)} %pad_maximum_fusion.1), channel_id=1, source_target_pairs={{0,32},{4,228},{32,64},{36,4},{64,96},{68,36},{96,128},{100,68},{1... | collective-permute-start | bytes 1572872 | tf_op jit(solution)/shard_map/ppermute | solution.py:26
  26.9 14.9 %collective-permute-start.7 = (bf16[16,128,256]{2,1,0:T(8,128)(2,1)S(1)}, bf16[16,128,256]{2,1,0:T(8,128)(2,1)S(1)}, u32[]{:S(2)}, u32[]{:S(2)}) collective-permute-start(bf16[16,128,256]{2,1,0:T(8,128)(2,1)S(1)} %pad_maximum_fusion), channel_id=1, source_target_pairs={{0,8},{4,28},{8,16},{12,4},{16,24},{20,12},{24,0},{28,20},{1,9},{5... | collective-permute-start | bytes 3145736 | tf_op jit(solution)/shard_map/ppermute | solution.py:26
  33.0 8.9 %collective-permute-start.4 = (bf16[8,128,256]{2,1,0:T(8,128)(2,1)S(1)}, bf16[8,128,256]{2,1,0:T(8,128)(2,1)S(1)}, u32[]{:S(2)}, u32[]{:S(2)}) collective-permute-start(bf16[8,128,256]{2,1,0:T(8,128)(2,1)S(1)} %add_convert_fusion.2), channel_id=1, source_target_pairs={{0,32},{4,228},{32,64},{36,4},{64,96},{68,36},{96,128},{100,68},{1... | collective-permute-start | bytes 1572872 | tf_op jit(solution)/shard_map/ppermute | solution.py:26
  41.8 3.5 %collective-permute-start.8 = (bf16[8,128,256]{2,1,0:T(8,128)(2,1)S(1)}, bf16[8,128,256]{2,1,0:T(8,128)(2,1)S(1)}, u32[]{:S(2)}, u32[]{:S(2)}) collective-permute-start(bf16[8,128,256]{2,1,0:T(8,128)(2,1)S(1)} %slice.132), channel_id=1, source_target_pairs={{0,4},{4,0},{1,5},{5,1},{2,6},{6,2},{3,7},{7,3},{8,12},{12,8},{9,1... | collective-permute-start | bytes 1572872 | tf_op jit(solution)/shard_map/ppermute | solution.py:30
  42.1 10.3 %collective-permute-start.5 = (bf16[8,128,256]{2,1,0:T(8,128)(2,1)S(1)}, bf16[8,128,256]{2,1,0:T(8,128)(2,1)S(1)}, u32[]{:S(2)}, u32[]{:S(2)}) collective-permute-start(bf16[8,128,256]{2,1,0:T(8,128)(2,1)S(1)} %add_convert_fusion.1), channel_id=1, source_target_pairs={{0,32},{4,228},{32,64},{36,4},{64,96},{68,36},{96,128},{100,68},{1... | collective-permute-start | bytes 1572872 | tf_op jit(solution)/shard_map/ppermute | solution.py:26
  45.3 23.6 %copy-start.1 = (f32[1,1,512,512]{3,2,1,0:T(8,128)S(1)}, f32[1,1,512,512]{3,2,1,0:T(8,128)}, u32[]{:S(2)}) copy-start(f32[1,1,512,512]{3,2,1,0:T(8,128)} %param.8) | copy-start | bytes 3145732
  45.3 23.6 %copy-start.2 = (f32[1,1,128,128]{3,2,1,0:T(8,128)S(1)}, f32[1,1,128,128]{3,2,1,0:T(8,128)}, u32[]{:S(2)}) copy-start(f32[1,1,128,128]{3,2,1,0:T(8,128)} %param.9) | copy-start | bytes 196612
  45.5 45.5 %copy-start.4 = (s32[64]{0:T(128)S(1)}, s32[64]{0:T(128)}, u32[]{:S(2)}) copy-start(s32[64]{0:T(128)} %owner_ref.5) | copy-start | bytes 772
  45.6 10.7 %collective-permute-start.13 = (bf16[3,128,256]{2,1,0:T(8,128)(2,1)S(1)}, bf16[3,128,256]{2,1,0:T(8,128)(2,1)S(1)}, u32[]{:S(2)}, u32[]{:S(2)}) collective-permute-start(bf16[3,128,256]{2,1,0:T(8,128)(2,1)S(1)} %pad_maximum_fusion.2), channel_id=1, source_target_pairs={{0,64},{4,196},{32,96},{36,228},{64,128},{68,4},{96,160},{100,36},... | collective-permute-start | bytes 589832 | tf_op jit(solution)/shard_map/ppermute | solution.py:26
  52.5 7.5 %collective-permute-start.9 = (bf16[4,128,256]{2,1,0:T(8,128)(2,1)S(1)}, bf16[4,128,256]{2,1,0:T(8,128)(2,1)S(1)}, u32[]{:S(2)}, u32[]{:S(2)}) collective-permute-start(bf16[4,128,256]{2,1,0:T(8,128)(2,1)S(1)} %slice.109), channel_id=1, source_target_pairs={{0,4},{4,0},{1,5},{5,1},{2,6},{6,2},{3,7},{7,3},{8,12},{12,8},{9,1... | collective-permute-start | bytes 786440 | tf_op jit(solution)/shard_map/ppermute | solution.py:30
  56.4 7.0 %collective-permute-start.14 = (bf16[2,128,256]{2,1,0:T(8,128)(2,1)S(1)}, bf16[2,128,256]{2,1,0:T(8,128)(2,1)S(1)}, u32[]{:S(2)}, u32[]{:S(2)}) collective-permute-start(bf16[2,128,256]{2,1,0:T(8,128)(2,1)S(1)} %pad_maximum_fusion.4), channel_id=1, source_target_pairs={{0,64},{4,196},{32,96},{36,228},{64,128},{68,4},{96,160},{100,36},... | collective-permute-start | bytes 393224 | tf_op jit(solution)/shard_map/ppermute | solution.py:26
  59.8 4.7 %collective-permute-start.15 = (bf16[2,128,256]{2,1,0:T(8,128)(2,1)S(1)}, bf16[2,128,256]{2,1,0:T(8,128)(2,1)S(1)}, u32[]{:S(2)}, u32[]{:S(2)}) collective-permute-start(bf16[2,128,256]{2,1,0:T(8,128)(2,1)S(1)} %pad_maximum_fusion.5), channel_id=1, source_target_pairs={{0,32},{4,228},{32,64},{36,4},{64,96},{68,36},{96,128},{100,68},{1... | collective-permute-start | bytes 393224 | tf_op jit(solution)/shard_map/ppermute | solution.py:26
  60.1 7.4 %collective-permute-start.11 = (bf16[2,128,256]{2,1,0:T(8,128)(2,1)S(1)}, bf16[2,128,256]{2,1,0:T(8,128)(2,1)S(1)}, u32[]{:S(2)}, u32[]{:S(2)}) collective-permute-start(bf16[2,128,256]{2,1,0:T(8,128)(2,1)S(1)} %pad_maximum_fusion.3), channel_id=1, source_target_pairs={{0,8},{4,28},{8,16},{12,4},{16,24},{20,12},{24,0},{28,20},{1,9},{5... | collective-permute-start | bytes 393224 | tf_op jit(solution)/shard_map/ppermute | solution.py:26
  60.9 6.8 %collective-permute-start.10 = (bf16[1,128,256]{2,1,0:T(8,128)(2,1)S(1)}, bf16[1,128,256]{2,1,0:T(8,128)(2,1)S(1)}, u32[]{:S(2)}, u32[]{:S(2)}) collective-permute-start(bf16[1,128,256]{2,1,0:T(8,128)(2,1)S(1)} %get-tuple-element.61), channel_id=1, source_target_pairs={{0,16},{4,20},{8,24},{12,28},{16,0},{20,4},{24,8},{28,12},{1,17},{... | collective-permute-start | bytes 196616 | tf_op jit(solution)/shard_map/ppermute | solution.py:26
  64.6 3.9 %collective-permute-start.16 = (bf16[128,256]{1,0:T(8,128)(2,1)S(1)}, bf16[128,256]{1,0:T(8,128)(2,1)S(1)}, u32[]{:S(2)}, u32[]{:S(2)}) collective-permute-start(bf16[128,256]{1,0:T(8,128)(2,1)S(1)} %fusion.8), channel_id=1, source_target_pairs={{0,4},{4,0},{1,5},{5,1},{2,6},{6,2},{3,7},{7,3},{8,12},{12,8},{9,1... | collective-permute-start | bytes 196616 | tf_op jit(solution)/shard_map/ppermute | solution.py:30
  67.6 1.3 %collective-permute-start.12 = (bf16[128,256]{1,0:T(8,128)(2,1)S(1)}, bf16[128,256]{1,0:T(8,128)(2,1)S(1)}, u32[]{:S(2)}, u32[]{:S(2)}) collective-permute-start(bf16[128,256]{1,0:T(8,128)(2,1)S(1)} %get-tuple-element.62), channel_id=1, source_target_pairs={{0,4},{4,0},{1,5},{5,1},{2,6},{6,2},{3,7},{7,3},{8,12},{12,8},{9,1... | collective-permute-start | bytes 196616 | tf_op jit(solution)/shard_map/ppermute | solution.py:30
  81.2 20.9 %all-to-all-start = ((bf16[64,8,128]{2,1,0:T(8,128)(2,1)}), bf16[64,8,128]{2,1,0:T(8,128)(2,1)S(1)}, u32[]{:S(2)}, u32[]{:S(2)}) async-start(bf16[64,8,128]{2,1,0:T(8,128)(2,1)} %bitcast.15), calls=%async_computation | async-start | bytes 262144 | tf_op jit(solution)/shard_map/all_to_all | solution.py:259

commit v5 on v4

--- a/solution.py
+++ b/solution.py
@@ -62,10 +62,14 @@
 
 GIVE_Y, KEEP_Y = give_and_keep((1,), (2, 0))
 GIVE_Z, KEEP_Z = give_and_keep((3, 2, 1), (4, 0))
-OWN_Y = [e for e in GIVE_Y + KEEP_Y if e[1] == 0]
-OWN_Z = [e for e in GIVE_Z + KEEP_Z if e[1] == 0]
-FIRST_OWN_Y = (GIVE_Y + KEEP_Y).index(OWN_Y[0])
-FIRST_OWN_Z = (GIVE_Z + KEEP_Z).index(OWN_Z[0])
+
+
+def own(entries):
+    return [e for e in entries if e[1] == 0]
+
+
+def own_at(entries):
+    return entries.index(own(entries)[0])
 
 
 def group_a(dz, entries):
@@ -111,12 +115,18 @@
     vmem = pl.BlockSpec(memory_space=pltpu.VMEM)
     smem = pl.BlockSpec(memory_space=pltpu.SMEM)
     inputs = [] if before is None else list(before)
+    count = sum(len(g) for g in groups)
+    moved = acts.size * 2 + kvt.size * 2 + count * rows * half_cols * (4 if before is None else 6)
+    cost = pl.CostEstimate(
+        flops=2 * count * rows * half_cols * acts.shape[0], transcendentals=0, bytes_accessed=moved
+    )
     return pl.pallas_call(
         body,
         out_shape=[jax.ShapeDtypeStruct((len(g), rows, half_cols), held) for g in groups],
         in_specs=[smem, vmem, vmem] + [vmem] * len(inputs),
         out_specs=[vmem for _ in groups],
         compiler_params=pltpu.CompilerParams(vmem_limit_bytes=VMEM_LIMIT),
+        cost_estimate=cost,
         name="block_sums",
     )(owner_table, acts, kvt, *inputs)
 
@@ -276,35 +286,41 @@
     acts_peer = swapped(activations)
     kvt_peer = swapped(kvt)
 
-    all_y, all_z = GIVE_Y + KEEP_Y, GIVE_Z + KEEP_Z
-    first = [group_a(("fix", 4), OWN_Y), group_b(("fix", 2), OWN_Z)]
-    rest = [group_a(("sign", 3), all_y), group_b(("sign", 1), all_z)]
-    rest += [group_a(("sign", 2), all_y), group_a(("sign", 1), all_y)]
+    four, two = ("fix", 4), ("fix", 2)
+    first = [group_a(four, own(GIVE_Y + KEEP_Y)), group_b(two, own(GIVE_Z + KEEP_Z))]
+    rest = [group_a(("sign", k), e) for k in (3, 2, 1) for e in (GIVE_Y, KEEP_Y)]
+    rest += [group_b(("sign", 1), e) for e in (GIVE_Z, KEEP_Z)]
     rest += [group_a(("fix", 0), KEEP_Y), group_b(("fix", 0), KEEP_Z)]
     sizes = (block_rows, row_blocks, owner_table)
-    own = block_sums(first + rest, activations, kvt, *sizes)
-    a4, b2 = block_sums(first, acts_peer, kvt_peer, *sizes, before=own[:2])
-    a3, b1, a2, a1, a0, b0 = block_sums(rest, acts_peer, kvt_peer, *sizes, before=own[2:])
-
-    a_run = added_inside(a3, directed(a4, Z), FIRST_OWN_Y)
-    b_run = added_inside(b1, directed(b2, Y), FIRST_OWN_Z)
-    a_run = added(a2, directed(a_run, Z))
-    b_run = directed(b_run, Y)
-    a_run = added(a1, directed(a_run, Z))
-    n = len(GIVE_Z)
-    b = wide(b0, b_run[n:], swapped(b_run[:n]))
-    b_far = jnp.stack([b[3], b[0], b[5]]).astype(BF16)
-    b_far = directed(b_far, Z, 2)
+    sums = block_sums(first + rest, activations, kvt, *sizes)
+    a4, b2 = block_sums(first, acts_peer, kvt_peer, *sizes, before=sums[:2])
+    later = block_sums(rest, acts_peer, kvt_peer, *sizes, before=sums[2:])
+    a3g, a3k, a2g, a2k, a1g, a1k, b1g, b1k, a0, b0 = later
+
+    n_a, n_b = len(own(GIVE_Y)), len(own(GIVE_Z))
+    b2 = directed(b2, Y)
+    bg = added_inside(b1g, b2[:n_b], own_at(GIVE_Z))
+    bk = added_inside(b1k, b2[n_b:], own_at(KEEP_Z))
+    a4 = after(directed(a4, Z), bk)
+    ag = added_inside(a3g, a4[:n_a], own_at(GIVE_Y))
+    ak = added_inside(a3k, a4[n_a:], own_at(KEEP_Y))
+    ag = added(a2g, after(directed(ag, Z), ak))
+    bg = after(directed(bg, Y), ag)
+    ak = added(a2k, after(directed(ak, Z), bg))
+    ag = added(a1g, after(directed(ag, Z), ak))
+    bk = after(directed(bk, Y), ag)
+    b = wide(b0, bk, after(swapped(bg), bk))
+    ak = added(a1k, after(directed(ak, Z), b))
+    ag = after(directed(ag, Z), ak)
+    b_far = after(directed(jnp.stack([b[3], b[0], b[5]]).astype(BF16), Z, 2), ag)
     b_two = jnp.stack([added(b[1], b_far[0]), b[6].astype(BF16)])
     b_one = jnp.stack([added(b[2], b_far[1]), added(b[7], b_far[2])])
-
-    a_run = after(directed(a_run, Z), b)
-    n = len(GIVE_Y)
-    a = wide(a0, a_run[n:], swapped(a_run[:n]))
+    ak = after(directed(ak, Z), b_two)
+    a = wide(a0, ak, after(swapped(ag), ak))
     a_two = a[1:2].astype(BF16)
     a_one = jnp.stack([a[0], a[3]]).astype(BF16)
-    b_two = after(directed(b_two, Z, 2), a_two, a_one)
-    b_one = after(directed(b_one, Z), a_two, a_one)
+    b_two = directed(b_two, Z, 2)
+    b_one = directed(b_one, Z)
     a_two = directed(a_two, Y, 2)
     a_one = directed(a_one, Y)
     b_give = added(b_two[1], b_one[1])

time: 131 us -> 129 us (0.985)
  waiting for transfers between devices: 30.8 us -> 25.1 us
  starting transfers between devices: 43.6 us -> 47.7 us
    ppermute x11 -> x15, starting transfers between devices: 23.3 us -> 30.5 us  [directed(): return lax.ppermute(x, (axis, CORE), pairs)]
    ppermute x11 -> x15, waiting for transfers between devices: 18.1 us -> 12.6 us  [directed(): return lax.ppermute(x, (axis, CORE), pairs)]
    all_to_all x1, starting transfers between devices: 9.76 us -> 7.6 us  [routed(): lax.all_to_all(directions.reshape(slots, 8, width), DP, 0, 0, tiled=True)]
    unnamed x11 -> x9, local copies, waits for them, and re-layouts: 3.95 us -> 3.95 us
  transfers between devices with their start and end apart: 18 -> 22, of which waited for: 10 -> 10; matrix products, arithmetic and copies ran while one was open for 2% -> 2% of each run, Pallas kernels for 4% -> 5%
where the time goes in v5:
time: 129 us
  starting transfers between devices  47.7 us (37%)
  blocking collectives  26.3 us (20%)
  waiting for transfers between devices  25.1 us (19%)
  Pallas kernels  22.3 us (17%)
  local copies, waits for them, and re-layouts  4.62 us (4%)
    ppermute x15, starting transfers between devices, directed(): return lax.ppermute(x, (axis, CORE), pairs)  30.5 us
    all_to_all x1, blocking collectives, routed(): got = lax.all_to_all(copies, (*DP, 'tensor'), 0, 0, tiled=True)  26.3 us
    ppermute x15, waiting for transfers between devices, directed(): return lax.ppermute(x, (axis, CORE), pairs)  12.6 us
    pallas_call x1, Pallas kernels, precondition(): pl.pallas_call(body, out_shape=[jax.ShapeDtypeStruct(left.shape, F32), ja...  12.3 us
    all_to_all x1, waiting for transfers between devices, routed(): lax.all_to_all(directions.reshape(slots, 8, width), DP, 0, 0, tiled=True)  10.5 us
    ppermute x6, starting transfers between devices, swapped(): return lax.ppermute(x, CORE, [(0, 1), (1, 0)])  9.61 us
    pallas_call x3, Pallas kernels, block_sums(): pl.pallas_call(body, out_shape=[jax.ShapeDtypeStruct((len(g), rows, half_...  8.51 us
    all_to_all x1, starting transfers between devices, routed(): lax.all_to_all(directions.reshape(slots, 8, width), DP, 0, 0, tiled=True)  7.6 us
  transfers between devices with their start and end apart: 22, of which 10 were waited for; matrix products, arithmetic and copies ran while one was open for 2% of the time, Pallas kernels for 5%

profile of v5, /device:TPU:1, one launch (start us, length us, event | category | flops | bytes accessed | tf_op | source)
XLA Modules:
  0.0 128.5 jit_solution(16509394082443659588)
XLA Ops:
  0.6 3.3 %collective-permute-start = (bf16[256,8192]{1,0:T(8,128)(2,1)}, bf16[256,8192]{1,0:T(8,128)(2,1)}, u32[]{:S(2)}, u32[]{:S(2)}) collective-permute-start(bf16[256,8192]{1,0:T(8,128)(2,1)} %a_ref.1), channel_id=1, source_target_pairs={{0,4},{4,0},{1,5},{5,1},{2,6},{6,2},{3,7},{7,3},{8,12},{12,8},{9,1... | collective-permute-start | bytes 12582920 | tf_op jit(solution)/shard_map/ppermute | solution.py:30
  4.0 1.1 copy.10
  5.2 2.2 %copy-done = bf16[256,8192]{1,0:T(8,128)(2,1)S(1)} copy-done((bf16[256,8192]{1,0:T(8,128)(2,1)S(1)}, bf16[256,8192]{1,0:T(8,128)(2,1)}, u32[]{:S(2)}) %copy-start) | copy-done | bytes 4194328
  8.0 2.1 %block_sums.3 = (f32[4,128,256]{2,1,0:T(8,128)S(1)}, f32[8,128,256]{2,1,0:T(8,128)S(1)}, f32[4,128,256]{2,1,0:T(8,128)S(1)}, f32[4,128,256]{2,1,0:T(8,128)S(1)},...) custom-call(s32[64]{0:T(128)S(1)} %copy-done.3, ...), custom_call_target="tpu_custom_call" | custom-call | flops 1073741824 | bytes 12845056 | tf_op jit(solution)/shard_map/block_sums/pallas_call | solution.py:123
  10.1 1.0 collective-permute-done.1.k_ref
  11.1 2.7 %block_sums.5 = (bf16[4,128,256]{2,1,0:T(8,128)(2,1)S(1)}, bf16[8,128,256]{2,1,0:T(8,128)(2,1)S(1)}) custom-call(s32[64]{0:T(128)S(1)} %copy-done.3, bf16[256,8192]{1,0:T(8,128)(2,1)} %collective-permute-done.a_ref, bf16[512,256]{1,0:T(8,128)(2,1)S(1)} %collective-permute-done.1.k_ref, f32[4,128,256]{2,1,0:T(8,128)S(1)} %get-tuple-element.56.refs_0_, ...), custom_call_target="tpu_custom_call" | custom-call | flops 201326592 | bytes 6815744 | tf_op jit(solution)/shard_map/block_sums/pallas_call | solution.py:123
  13.8 1.1 collective-permute-start.3
  14.9 5.6 %collective-permute-start.2 = (bf16[4,128,256]{2,1,0:T(8,128)(2,1)S(1)}, bf16[4,128,256]{2,1,0:T(8,128)(2,1)S(1)}, u32[]{:S(2)}, u32[]{:S(2)}) collective-permute-start(bf16[4,128,256]{2,1,0:T(8,128)(2,1)S(1)} %get-tuple-element.58), channel_id=1, source_target_pairs={{0,32},{4,228},{32,64},{36,4},{64,96},{68,36},{96,128},{100,68},{1... | collective-permute-start | bytes 786440 | tf_op jit(solution)/shard_map/ppermute | solution.py:26
  20.4 3.8 %block_sums.4 = (bf16[4,128,256]{2,1,0:T(8,128)(2,1)S(1)}, bf16[4,128,256]{2,1,0:T(8,128)(2,1)S(1)}, bf16[4,128,256]{2,1,0:T(8,128)(2,1)S(1)}, bf16[4,128,256]{2...) custom-call(s32[64]{0:T(128)S(1)} %copy-done.3, ...), custom_call_target="tpu_custom_call" | custom-call | flops 872415232 | bytes 14680064 | tf_op jit(solution)/shard_map/block_sums/pallas_call | solution.py:123
  25.1 5.0 %collective-permute-start.6 = (bf16[4,128,256]{2,1,0:T(8,128)(2,1)S(1)}, bf16[4,128,256]{2,1,0:T(8,128)(2,1)S(1)}, u32[]{:S(2)}, u32[]{:S(2)}) collective-permute-start(bf16[4,128,256]{2,1,0:T(8,128)(2,1)S(1)} %pad_maximum_fusion.3), channel_id=1, source_target_pairs={{0,32},{4,228},{32,64},{36,4},{64,96},{68,36},{96,128},{100,68},{1... | collective-permute-start | bytes 786440 | tf_op jit(solution)/shard_map/ppermute | solution.py:26
  31.1 2.2 %collective-permute-done.6 = bf16[4,128,256]{2,1,0:T(8,128)(2,1)S(1)} collective-permute-done((bf16[4,128,256]{2,1,0:T(8,128)(2,1)S(1)}, bf16[4,128,256]{2,1,0:T(8,128)(2,1)S(1)}, u32[]{:S(2)}, u32[]{:S(2)}) %collective-permute-start.6) | collective-permute-done | bytes 262176 | tf_op jit(solution)/shard_map/ppermute | solution.py:26
  33.4 3.5 %collective-permute-start.9 = (bf16[4,128,256]{2,1,0:T(8,128)(2,1)S(1)}, bf16[4,128,256]{2,1,0:T(8,128)(2,1)S(1)}, u32[]{:S(2)}, u32[]{:S(2)}) collective-permute-start(bf16[4,128,256]{2,1,0:T(8,128)(2,1)S(1)} %add_convert_fusion.4), channel_id=1, source_target_pairs={{0,32},{4,228},{32,64},{36,4},{64,96},{68,36},{96,128},{100,68},{1... | collective-permute-start | bytes 786440 | tf_op jit(solution)/shard_map/ppermute | solution.py:26
  36.9 1.6 %collective-permute-done.5 = bf16[8,128,256]{2,1,0:T(8,128)(2,1)S(1)} collective-permute-done((bf16[8,128,256]{2,1,0:T(8,128)(2,1)S(1)}, bf16[8,128,256]{2,1,0:T(8,128)(2,1)S(1)}, u32[]{:S(2)}, u32[]{:S(2)}) %collective-permute-start.5) | collective-permute-done | bytes 524320 | tf_op jit(solution)/shard_map/ppermute | solution.py:26
  38.5 2.3 %collective-permute-start.10 = (bf16[8,128,256]{2,1,0:T(8,128)(2,1)S(1)}, bf16[8,128,256]{2,1,0:T(8,128)(2,1)S(1)}, u32[]{:S(2)}, u32[]{:S(2)}) collective-permute-start(bf16[8,128,256]{2,1,0:T(8,128)(2,1)S(1)} %collective-permute-done.5), channel_id=1, source_target_pairs={{0,4},{4,0},{1,5},{5,1},{2,6},{6,2},{3,7},{7,3},{8,12},{12,8},{9,1... | collective-permute-start | bytes 1572872 | tf_op jit(solution)/shard_map/ppermute | solution.py:30
  41.0 3.9 %collective-permute-start.7 = (bf16[4,128,256]{2,1,0:T(8,128)(2,1)S(1)}, bf16[4,128,256]{2,1,0:T(8,128)(2,1)S(1)}, u32[]{:S(2)}, u32[]{:S(2)}) collective-permute-start(bf16[4,128,256]{2,1,0:T(8,128)(2,1)S(1)} %add_convert_fusion.3), channel_id=1, source_target_pairs={{0,32},{4,228},{32,64},{36,4},{64,96},{68,36},{96,128},{100,68},{1... | collective-permute-start | bytes 786440 | tf_op jit(solution)/shard_map/ppermute | solution.py:26
  45.0 1.0 collective-permute-start.13
  46.3 1.9 %collective-permute-done.7 = bf16[4,128,256]{2,1,0:T(8,128)(2,1)S(1)} collective-permute-done((bf16[4,128,256]{2,1,0:T(8,128)(2,1)S(1)}, bf16[4,128,256]{2,1,0:T(8,128)(2,1)S(1)}, u32[]{:S(2)}, u32[]{:S(2)}) %collective-permute-start.7) | collective-permute-done | bytes 262176 | tf_op jit(solution)/shard_map/ppermute | solution.py:26
  48.3 2.6 %collective-permute-start.12 = (bf16[3,128,256]{2,1,0:T(8,128)(2,1)S(1)}, bf16[3,128,256]{2,1,0:T(8,128)(2,1)S(1)}, u32[]{:S(2)}, u32[]{:S(2)}) collective-permute-start(bf16[3,128,256]{2,1,0:T(8,128)(2,1)S(1)} %pad_maximum_fusion.4), channel_id=1, source_target_pairs={{0,64},{4,196},{32,96},{36,228},{64,128},{68,4},{96,160},{100,36},... | collective-permute-start | bytes 589832 | tf_op jit(solution)/shard_map/ppermute | solution.py:26
  51.0 0.8 collective-permute-start.11
  52.4 3.2 %collective-permute-done.12 = bf16[3,128,256]{2,1,0:T(8,128)(2,1)S(1)} collective-permute-done((bf16[3,128,256]{2,1,0:T(8,128)(2,1)S(1)}, bf16[3,128,256]{2,1,0:T(8,128)(2,1)S(1)}, u32[]{:S(2)}, u32[]{:S(2)}) %collective-permute-start.12) | collective-permute-done | bytes 196640 | tf_op jit(solution)/shard_map/ppermute | solution.py:26
  55.7 2.1 %collective-permute-start.18 = (bf16[2,128,256]{2,1,0:T(8,128)(2,1)S(1)}, bf16[2,128,256]{2,1,0:T(8,128)(2,1)S(1)}, u32[]{:S(2)}, u32[]{:S(2)}) collective-permute-start(bf16[2,128,256]{2,1,0:T(8,128)(2,1)S(1)} %pad_maximum_fusion.5), channel_id=1, source_target_pairs={{0,64},{4,196},{32,96},{36,228},{64,128},{68,4},{96,160},{100,36},... | collective-permute-start | bytes 393224 | tf_op jit(solution)/shard_map/ppermute | solution.py:26
  57.8 2.1 %collective-permute-start.19 = (bf16[2,128,256]{2,1,0:T(8,128)(2,1)S(1)}, bf16[2,128,256]{2,1,0:T(8,128)(2,1)S(1)}, u32[]{:S(2)}, u32[]{:S(2)}) collective-permute-start(bf16[2,128,256]{2,1,0:T(8,128)(2,1)S(1)} %pad_maximum_fusion.7), channel_id=1, source_target_pairs={{0,32},{4,228},{32,64},{36,4},{64,96},{68,36},{96,128},{100,68},{1... | collective-permute-start | bytes 393224 | tf_op jit(solution)/shard_map/ppermute | solution.py:26
  59.9 1.5 %collective-permute-done.11 = bf16[4,128,256]{2,1,0:T(8,128)(2,1)S(1)} collective-permute-done((bf16[4,128,256]{2,1,0:T(8,128)(2,1)S(1)}, bf16[4,128,256]{2,1,0:T(8,128)(2,1)S(1)}, u32[]{:S(2)}, u32[]{:S(2)}) %collective-permute-start.11) | collective-permute-done | bytes 262176 | tf_op jit(solution)/shard_map/ppermute | solution.py:26
  62.1 0.9 collective-permute-start.16
  63.0 2.1 %collective-permute-done.19 = bf16[2,128,256]{2,1,0:T(8,128)(2,1)S(1)} collective-permute-done((bf16[2,128,256]{2,1,0:T(8,128)(2,1)S(1)}, bf16[2,128,256]{2,1,0:T(8,128)(2,1)S(1)}, u32[]{:S(2)}, u32[]{:S(2)}) %collective-permute-start.19) | collective-permute-done | bytes 131104 | tf_op jit(solution)/shard_map/ppermute | solution.py:26
  65.1 2.4 %collective-permute-start.20 = (bf16[128,256]{1,0:T(8,128)(2,1)S(1)}, bf16[128,256]{1,0:T(8,128)(2,1)S(1)}, u32[]{:S(2)}, u32[]{:S(2)}) collective-permute-start(bf16[128,256]{1,0:T(8,128)(2,1)S(1)} %fusion.8), channel_id=1, source_target_pairs={{0,4},{4,0},{1,5},{5,1},{2,6},{6,2},{3,7},{7,3},{8,12},{12,8},{9,1... | collective-permute-start | bytes 196616 | tf_op jit(solution)/shard_map/ppermute | solution.py:30
  68.4 0.8 collective-permute-done.17.refs_3_
  69.3 12.3 %precondition.1 = (f32[512,512]{1,0:T(8,128)}, f32[128,128]{1,0:T(8,128)}, bf16[512,128]{1,0:T(8,128)(2,1)}) custom-call(f32[128,256]{1,0:T(8,128)S(1)} %slice_bitcast_fusion.1.refs_0_, bf16[128,256]{1,0:T(8,128)(2,1)S(1)} %bitcast.35, bf16[128,256]{1,0:T(8,128)(2,1)S(1)} %get-tuple-element.97.refs_2_, bf16[128,256]{1,0:T(8,128)(2,1)S(1)} %collective-permute-done.17.refs_3_, ...), custom_call_target="tpu_custom_call" | custom-call | tf_op jit(solution)/shard_map/precondition/pallas_call | solution.py:224
  81.6 7.6 %all-to-all-start = ((bf16[64,8,128]{2,1,0:T(8,128)(2,1)}), bf16[64,8,128]{2,1,0:T(8,128)(2,1)S(1)}, u32[]{:S(2)}, u32[]{:S(2)}) async-start(bf16[64,8,128]{2,1,0:T(8,128)(2,1)} %bitcast.15), calls=%async_computation | async-start | bytes 262144 | tf_op jit(solution)/shard_map/all_to_all | solution.py:269
  89.8 10.5 %all-to-all-done = bf16[64,8,128]{2,1,0:T(8,128)(2,1)S(1)} async-done(((bf16[64,8,128]{2,1,0:T(8,128)(2,1)}), bf16[64,8,128]{2,1,0:T(8,128)(2,1)S(1)}, u32[]{:S(2)}, u32[]{:S(2)}) %all-to-all-start) | async-done | bytes 131104 | tf_op jit(solution)/shard_map/all_to_all | solution.py:269
  100.8 26.3 %all_to_all.10 = bf16[256,8,128]{2,1,0:T(8,128)(2,1)S(1)} all-to-all(bf16[256,8,128]{2,1,0:T(8,128)(2,1)S(1)} %bitcast.36), channel_id=1, replica_groups=mesh['dp_0'=8,'dp_1'=4,'dp_2'=2,'tensor'=4] {'dp_0','dp_1','dp_2','tensor'}, dimensions={0} | all-to-all | bytes 1048576 | tf_op jit(solution)/shard_map/all_to_all | solution.py:278
  127.1 1.5 %placed.1 = bf16[2,128,1024]{2,1,0:T(8,128)(2,1)} custom-call(bf16[2048,128]{1,0:T(8,128)(2,1)S(1)} %bitcast.30), custom_call_target="tpu_custom_call" | custom-call | tf_op jit(solution)/shard_map/placed/pallas_call | solution.py:254
  (66 shorter events, 6.6 us)
Async XLA Ops:
  0.6 10.5 %collective-permute-start = (bf16[256,8192]{1,0:T(8,128)(2,1)}, bf16[256,8192]{1,0:T(8,128)(2,1)}, u32[]{:S(2)}, u32[]{:S(2)}) collective-permute-start(bf16[256,8192]{1,0:T(8,128)(2,1)} %a_ref.1), channel_id=1, source_target_pairs={{0,4},{4,0},{1,5},{5,1},{2,6},{6,2},{3,7},{7,3},{8,12},{12,8},{9,1... | collective-permute-start | bytes 12582920 | tf_op jit(solution)/shard_map/ppermute | solution.py:30
  5.1 6.1 %collective-permute-start.1 = (bf16[512,256]{1,0:T(8,128)(2,1)S(1)}, bf16[512,256]{1,0:T(8,128)(2,1)S(1)}, u32[]{:S(2)}, u32[]{:S(2)}) collective-permute-start(bf16[512,256]{1,0:T(8,128)(2,1)S(1)} %bitcast.32), channel_id=1, source_target_pairs={{0,4},{4,0},{1,5},{5,1},{2,6},{6,2},{3,7},{7,3},{8,12},{12,8},{9,1... | collective-permute-start | bytes 786440 | tf_op jit(solution)/shard_map/ppermute | solution.py:30
  5.2 2.2 %copy-start = (bf16[256,8192]{1,0:T(8,128)(2,1)S(1)}, bf16[256,8192]{1,0:T(8,128)(2,1)}, u32[]{:S(2)}) copy-start(bf16[256,8192]{1,0:T(8,128)(2,1)} %a_ref.1) | copy-start | bytes 12582916
  7.4 0.7 copy-start.3
  13.8 10.5 %collective-permute-start.3 = (bf16[8,128,256]{2,1,0:T(8,128)(2,1)S(1)}, bf16[8,128,256]{2,1,0:T(8,128)(2,1)S(1)}, u32[]{:S(2)}, u32[]{:S(2)}) collective-permute-start(bf16[8,128,256]{2,1,0:T(8,128)(2,1)S(1)} %get-tuple-element.60), channel_id=1, source_target_pairs={{0,8},{4,28},{8,16},{12,4},{16,24},{20,12},{24,0},{28,20},{1,9},{5... | collective-permute-start | bytes 1572872 | tf_op jit(solution)/shard_map/ppermute | solution.py:26
  14.9 10.2 %collective-permute-start.2 = (bf16[4,128,256]{2,1,0:T(8,128)(2,1)S(1)}, bf16[4,128,256]{2,1,0:T(8,128)(2,1)S(1)}, u32[]{:S(2)}, u32[]{:S(2)}) collective-permute-start(bf16[4,128,256]{2,1,0:T(8,128)(2,1)S(1)} %get-tuple-element.58), channel_id=1, source_target_pairs={{0,32},{4,228},{32,64},{36,4},{64,96},{68,36},{96,128},{100,68},{1... | collective-permute-start | bytes 786440 | tf_op jit(solution)/shard_map/ppermute | solution.py:26
  24.5 21.6 %collective-permute-start.8 = (bf16[8,128,256]{2,1,0:T(8,128)(2,1)S(1)}, bf16[8,128,256]{2,1,0:T(8,128)(2,1)S(1)}, u32[]{:S(2)}, u32[]{:S(2)}) collective-permute-start(bf16[8,128,256]{2,1,0:T(8,128)(2,1)S(1)} %pad_maximum_fusion), channel_id=1, source_target_pairs={{0,8},{4,28},{8,16},{12,4},{16,24},{20,12},{24,0},{28,20},{1,9},{5... | collective-permute-start | bytes 1572872 | tf_op jit(solution)/shard_map/ppermute | solution.py:26
  25.1 8.3 %collective-permute-start.6 = (bf16[4,128,256]{2,1,0:T(8,128)(2,1)S(1)}, bf16[4,128,256]{2,1,0:T(8,128)(2,1)S(1)}, u32[]{:S(2)}, u32[]{:S(2)}) collective-permute-start(bf16[4,128,256]{2,1,0:T(8,128)(2,1)S(1)} %pad_maximum_fusion.3), channel_id=1, source_target_pairs={{0,32},{4,228},{32,64},{36,4},{64,96},{68,36},{96,128},{100,68},{1... | collective-permute-start | bytes 786440 | tf_op jit(solution)/shard_map/ppermute | solution.py:26
  30.1 8.4 %collective-permute-start.5 = (bf16[8,128,256]{2,1,0:T(8,128)(2,1)S(1)}, bf16[8,128,256]{2,1,0:T(8,128)(2,1)S(1)}, u32[]{:S(2)}, u32[]{:S(2)}) collective-permute-start(bf16[8,128,256]{2,1,0:T(8,128)(2,1)S(1)} %pad_maximum_fusion.1), channel_id=1, source_target_pairs={{0,8},{4,28},{8,16},{12,4},{16,24},{20,12},{24,0},{28,20},{1,9},{5... | collective-permute-start | bytes 1572872 | tf_op jit(solution)/shard_map/ppermute | solution.py:26
  30.3 10.6 %collective-permute-start.4 = (bf16[4,128,256]{2,1,0:T(8,128)(2,1)S(1)}, bf16[4,128,256]{2,1,0:T(8,128)(2,1)S(1)}, u32[]{:S(2)}, u32[]{:S(2)}) collective-permute-start(bf16[4,128,256]{2,1,0:T(8,128)(2,1)S(1)} %pad_maximum_fusion.2), channel_id=1, source_target_pairs={{0,32},{4,228},{32,64},{36,4},{64,96},{68,36},{96,128},{100,68},{1... | collective-permute-start | bytes 786440 | tf_op jit(solution)/shard_map/ppermute | solution.py:26
  33.4 11.5 %collective-permute-start.9 = (bf16[4,128,256]{2,1,0:T(8,128)(2,1)S(1)}, bf16[4,128,256]{2,1,0:T(8,128)(2,1)S(1)}, u32[]{:S(2)}, u32[]{:S(2)}) collective-permute-start(bf16[4,128,256]{2,1,0:T(8,128)(2,1)S(1)} %add_convert_fusion.4), channel_id=1, source_target_pairs={{0,32},{4,228},{32,64},{36,4},{64,96},{68,36},{96,128},{100,68},{1... | collective-permute-start | bytes 786440 | tf_op jit(solution)/shard_map/ppermute | solution.py:26
  38.5 7.5 %collective-permute-start.10 = (bf16[8,128,256]{2,1,0:T(8,128)(2,1)S(1)}, bf16[8,128,256]{2,1,0:T(8,128)(2,1)S(1)}, u32[]{:S(2)}, u32[]{:S(2)}) collective-permute-start(bf16[8,128,256]{2,1,0:T(8,128)(2,1)S(1)} %collective-permute-done.5), channel_id=1, source_target_pairs={{0,4},{4,0},{1,5},{5,1},{2,6},{6,2},{3,7},{7,3},{8,12},{12,8},{9,1... | collective-permute-start | bytes 1572872 | tf_op jit(solution)/shard_map/ppermute | solution.py:30
  41.0 7.2 %collective-permute-start.7 = (bf16[4,128,256]{2,1,0:T(8,128)(2,1)S(1)}, bf16[4,128,256]{2,1,0:T(8,128)(2,1)S(1)}, u32[]{:S(2)}, u32[]{:S(2)}) collective-permute-start(bf16[4,128,256]{2,1,0:T(8,128)(2,1)S(1)} %add_convert_fusion.3), channel_id=1, source_target_pairs={{0,32},{4,228},{32,64},{36,4},{64,96},{68,36},{96,128},{100,68},{1... | collective-permute-start | bytes 786440 | tf_op jit(solution)/shard_map/ppermute | solution.py:26
  45.0 6.8 %collective-permute-start.13 = (bf16[4,128,256]{2,1,0:T(8,128)(2,1)S(1)}, bf16[4,128,256]{2,1,0:T(8,128)(2,1)S(1)}, u32[]{:S(2)}, u32[]{:S(2)}) collective-permute-start(bf16[4,128,256]{2,1,0:T(8,128)(2,1)S(1)} %add_convert_fusion.2), channel_id=1, source_target_pairs={{0,32},{4,228},{32,64},{36,4},{64,96},{68,36},{96,128},{100,68},{1... | collective-permute-start | bytes 786440 | tf_op jit(solution)/shard_map/ppermute | solution.py:26
  46.0 23.3 %copy-start.1 = (f32[1,1,512,512]{3,2,1,0:T(8,128)S(1)}, f32[1,1,512,512]{3,2,1,0:T(8,128)}, u32[]{:S(2)}) copy-start(f32[1,1,512,512]{3,2,1,0:T(8,128)} %param.8) | copy-start | bytes 3145732
  46.0 23.3 %copy-start.2 = (f32[1,1,128,128]{3,2,1,0:T(8,128)S(1)}, f32[1,1,128,128]{3,2,1,0:T(8,128)}, u32[]{:S(2)}) copy-start(f32[1,1,128,128]{3,2,1,0:T(8,128)} %param.9) | copy-start | bytes 196612
  48.3 7.4 %collective-permute-start.12 = (bf16[3,128,256]{2,1,0:T(8,128)(2,1)S(1)}, bf16[3,128,256]{2,1,0:T(8,128)(2,1)S(1)}, u32[]{:S(2)}, u32[]{:S(2)}) collective-permute-start(bf16[3,128,256]{2,1,0:T(8,128)(2,1)S(1)} %pad_maximum_fusion.4), channel_id=1, source_target_pairs={{0,64},{4,196},{32,96},{36,228},{64,128},{68,4},{96,160},{100,36},... | collective-permute-start | bytes 589832 | tf_op jit(solution)/shard_map/ppermute | solution.py:26
  51.0 10.4 %collective-permute-start.11 = (bf16[4,128,256]{2,1,0:T(8,128)(2,1)S(1)}, bf16[4,128,256]{2,1,0:T(8,128)(2,1)S(1)}, u32[]{:S(2)}, u32[]{:S(2)}) collective-permute-start(bf16[4,128,256]{2,1,0:T(8,128)(2,1)S(1)} %add_convert_fusion.1), channel_id=1, source_target_pairs={{0,32},{4,228},{32,64},{36,4},{64,96},{68,36},{96,128},{100,68},{1... | collective-permute-start | bytes 786440 | tf_op jit(solution)/shard_map/ppermute | solution.py:26
  51.8 9.6 %collective-permute-start.14 = (bf16[4,128,256]{2,1,0:T(8,128)(2,1)S(1)}, bf16[4,128,256]{2,1,0:T(8,128)(2,1)S(1)}, u32[]{:S(2)}, u32[]{:S(2)}) collective-permute-start(bf16[4,128,256]{2,1,0:T(8,128)(2,1)S(1)} %collective-permute-done.13), channel_id=1, source_target_pairs={{0,4},{4,0},{1,5},{5,1},{2,6},{6,2},{3,7},{7,3},{8,12},{12,8},{9,1... | collective-permute-start | bytes 786440 | tf_op jit(solution)/shard_map/ppermute | solution.py:30
  55.7 7.3 %collective-permute-start.18 = (bf16[2,128,256]{2,1,0:T(8,128)(2,1)S(1)}, bf16[2,128,256]{2,1,0:T(8,128)(2,1)S(1)}, u32[]{:S(2)}, u32[]{:S(2)}) collective-permute-start(bf16[2,128,256]{2,1,0:T(8,128)(2,1)S(1)} %pad_maximum_fusion.5), channel_id=1, source_target_pairs={{0,64},{4,196},{32,96},{36,228},{64,128},{68,4},{96,160},{100,36},... | collective-permute-start | bytes 393224 | tf_op jit(solution)/shard_map/ppermute | solution.py:26
  57.8 7.2 %collective-permute-start.19 = (bf16[2,128,256]{2,1,0:T(8,128)(2,1)S(1)}, bf16[2,128,256]{2,1,0:T(8,128)(2,1)S(1)}, u32[]{:S(2)}, u32[]{:S(2)}) collective-permute-start(bf16[2,128,256]{2,1,0:T(8,128)(2,1)S(1)} %pad_maximum_fusion.7), channel_id=1, source_target_pairs={{0,32},{4,228},{32,64},{36,4},{64,96},{68,36},{96,128},{100,68},{1... | collective-permute-start | bytes 393224 | tf_op jit(solution)/shard_map/ppermute | solution.py:26
  61.5 6.9 %collective-permute-start.15 = (bf16[1,128,256]{2,1,0:T(8,128)(2,1)S(1)}, bf16[1,128,256]{2,1,0:T(8,128)(2,1)S(1)}, u32[]{:S(2)}, u32[]{:S(2)}) collective-permute-start(bf16[1,128,256]{2,1,0:T(8,128)(2,1)S(1)} %get-tuple-element.95), channel_id=1, source_target_pairs={{0,16},{4,20},{8,24},{12,28},{16,0},{20,4},{24,8},{28,12},{1,17},{... | collective-permute-start | bytes 196616 | tf_op jit(solution)/shard_map/ppermute | solution.py:26
  62.1 5.4 %collective-permute-start.16 = (bf16[2,128,256]{2,1,0:T(8,128)(2,1)S(1)}, bf16[2,128,256]{2,1,0:T(8,128)(2,1)S(1)}, u32[]{:S(2)}, u32[]{:S(2)}) collective-permute-start(bf16[2,128,256]{2,1,0:T(8,128)(2,1)S(1)} %pad_maximum_fusion.6), channel_id=1, source_target_pairs={{0,8},{4,28},{8,16},{12,4},{16,24},{20,12},{24,0},{28,20},{1,9},{5... | collective-permute-start | bytes 393224 | tf_op jit(solution)/shard_map/ppermute | solution.py:26
  65.1 3.4 %collective-permute-start.20 = (bf16[128,256]{1,0:T(8,128)(2,1)S(1)}, bf16[128,256]{1,0:T(8,128)(2,1)S(1)}, u32[]{:S(2)}, u32[]{:S(2)}) collective-permute-start(bf16[128,256]{1,0:T(8,128)(2,1)S(1)} %fusion.8), channel_id=1, source_target_pairs={{0,4},{4,0},{1,5},{5,1},{2,6},{6,2},{3,7},{7,3},{8,12},{12,8},{9,1... | collective-permute-start | bytes 196616 | tf_op jit(solution)/shard_map/ppermute | solution.py:30
  67.6 1.7 %collective-permute-start.17 = (bf16[128,256]{1,0:T(8,128)(2,1)S(1)}, bf16[128,256]{1,0:T(8,128)(2,1)S(1)}, u32[]{:S(2)}, u32[]{:S(2)}) collective-permute-start(bf16[128,256]{1,0:T(8,128)(2,1)S(1)} %get-tuple-element.96), channel_id=1, source_target_pairs={{0,4},{4,0},{1,5},{5,1},{2,6},{6,2},{3,7},{7,3},{8,12},{12,8},{9,1... | collective-permute-start | bytes 196616 | tf_op jit(solution)/shard_map/ppermute | solution.py:30
  81.6 18.7 %all-to-all-start = ((bf16[64,8,128]{2,1,0:T(8,128)(2,1)}), bf16[64,8,128]{2,1,0:T(8,128)(2,1)S(1)}, u32[]{:S(2)}, u32[]{:S(2)}) async-start(bf16[64,8,128]{2,1,0:T(8,128)(2,1)} %bitcast.15), calls=%async_computation | async-start | bytes 262144 | tf_op jit(solution)/shard_map/all_to_all | solution.py:269

commit v6 on v4

--- a/solution.py
+++ b/solution.py
@@ -26,6 +26,11 @@
     return lax.ppermute(x, (axis, CORE), pairs)
 
 
+def shifted(x, axis, step):
+    size = lax.axis_size(axis)
+    return lax.ppermute(x, axis, [(i, (i + step) % size) for i in range(size)])
+
+
 def swapped(x):
     return lax.ppermute(x, CORE, [(0, 1), (1, 0)])
 
@@ -62,10 +67,14 @@
 
 GIVE_Y, KEEP_Y = give_and_keep((1,), (2, 0))
 GIVE_Z, KEEP_Z = give_and_keep((3, 2, 1), (4, 0))
-OWN_Y = [e for e in GIVE_Y + KEEP_Y if e[1] == 0]
-OWN_Z = [e for e in GIVE_Z + KEEP_Z if e[1] == 0]
-FIRST_OWN_Y = (GIVE_Y + KEEP_Y).index(OWN_Y[0])
-FIRST_OWN_Z = (GIVE_Z + KEEP_Z).index(OWN_Z[0])
+
+
+def own(entries):
+    return [e for e in entries if e[1] == 0]
+
+
+def own_at(entries):
+    return entries.index(own(entries)[0])
 
 
 def group_a(dz, entries):
@@ -95,7 +104,7 @@
         z, y, core = (lax.axis_index(a) for a in DP)
         for g, group in enumerate(groups):
             for n, (half, dz, dy, flip) in enumerate(group):
-                to_z = (z + offset(dz, NZ, core)) % NZ
+                to_z = dz[1] if dz[0] == "at" else (z + offset(dz, NZ, core)) % NZ
                 to_y = (y + offset(dy, NY, core)) % NY
                 to_core = core if flip == 0 else 1 - core
                 block = owner_ref[(to_z * NY + to_y) * 2 + to_core]
@@ -111,12 +120,18 @@
     vmem = pl.BlockSpec(memory_space=pltpu.VMEM)
     smem = pl.BlockSpec(memory_space=pltpu.SMEM)
     inputs = [] if before is None else list(before)
+    count = sum(len(g) for g in groups)
+    moved = acts.size * 2 + kvt.size * 2 + count * rows * half_cols * (4 if before is None else 6)
+    cost = pl.CostEstimate(
+        flops=2 * count * rows * half_cols * acts.shape[0], transcendentals=0, bytes_accessed=moved
+    )
     return pl.pallas_call(
         body,
         out_shape=[jax.ShapeDtypeStruct((len(g), rows, half_cols), held) for g in groups],
         in_specs=[smem, vmem, vmem] + [vmem] * len(inputs),
         out_specs=[vmem for _ in groups],
         compiler_params=pltpu.CompilerParams(vmem_limit_bytes=VMEM_LIMIT),
+        cost_estimate=cost,
         name="block_sums",
     )(owner_table, acts, kvt, *inputs)
 
@@ -276,41 +291,30 @@
     acts_peer = swapped(activations)
     kvt_peer = swapped(kvt)
 
-    all_y, all_z = GIVE_Y + KEEP_Y, GIVE_Z + KEEP_Z
-    first = [group_a(("fix", 4), OWN_Y), group_b(("fix", 2), OWN_Z)]
-    rest = [group_a(("sign", 3), all_y), group_b(("sign", 1), all_z)]
-    rest += [group_a(("sign", 2), all_y), group_a(("sign", 1), all_y)]
-    rest += [group_a(("fix", 0), KEEP_Y), group_b(("fix", 0), KEEP_Z)]
+    two = ("fix", 2)
+    every = [(0, ("at", dz), ("fix", dy), 0) for dz in range(NZ) for dy in range(NY)]
+    first = [every, group_b(two, own(GIVE_Z + KEEP_Z))]
+    rest = [group_b(("sign", 1), GIVE_Z + KEEP_Z), group_b(("fix", 0), KEEP_Z)]
     sizes = (block_rows, row_blocks, owner_table)
-    own = block_sums(first + rest, activations, kvt, *sizes)
-    a4, b2 = block_sums(first, acts_peer, kvt_peer, *sizes, before=own[:2])
-    a3, b1, a2, a1, a0, b0 = block_sums(rest, acts_peer, kvt_peer, *sizes, before=own[2:])
-
-    a_run = added_inside(a3, directed(a4, Z), FIRST_OWN_Y)
-    b_run = added_inside(b1, directed(b2, Y), FIRST_OWN_Z)
-    a_run = added(a2, directed(a_run, Z))
+    sums = block_sums(first + rest, activations, kvt, *sizes)
+    a_all, b2 = block_sums(first, acts_peer, kvt_peer, *sizes, before=sums[:2])
+    b1, b0 = block_sums(rest, acts_peer, kvt_peer, *sizes, before=sums[2:])
+
+    a = lax.psum_scatter(a_all, Z, scatter_dimension=0, tiled=True)
+    b_run = added_inside(b1, directed(b2, Y), own_at(GIVE_Z + KEEP_Z))
     b_run = directed(b_run, Y)
-    a_run = added(a1, directed(a_run, Z))
     n = len(GIVE_Z)
     b = wide(b0, b_run[n:], swapped(b_run[:n]))
     b_far = jnp.stack([b[3], b[0], b[5]]).astype(BF16)
     b_far = directed(b_far, Z, 2)
     b_two = jnp.stack([added(b[1], b_far[0]), b[6].astype(BF16)])
     b_one = jnp.stack([added(b[2], b_far[1]), added(b[7], b_far[2])])
-
-    a_run = after(directed(a_run, Z), b)
-    n = len(GIVE_Y)
-    a = wide(a0, a_run[n:], swapped(a_run[:n]))
-    a_two = a[1:2].astype(BF16)
-    a_one = jnp.stack([a[0], a[3]]).astype(BF16)
-    b_two = after(directed(b_two, Z, 2), a_two, a_one)
-    b_one = after(directed(b_one, Z), a_two, a_one)
-    a_two = directed(a_two, Y, 2)
-    a_one = directed(a_one, Y)
-    b_give = added(b_two[1], b_one[1])
-    b_got = swapped(b_give)
-    a_got = swapped(a_one[1])
-    ga = [a[2], a_two[0], a_one[0], a_got]
+    a = after(a, b_two)
+    parts = [a[k] for k in range(4)]
+    b_two = after(directed(b_two, Z, 2), *parts)
+    b_one = after(directed(b_one, Z), *parts)
+    ga = [parts[0]] + [shifted(parts[k], Y, k) for k in (2, 1, 3)]
+    b_got = swapped(added(b_two[1], b_one[1]))
     gb = [b[4], b_two[0], b_one[0], b_got]
     return ga, gb
 

time: 131 us -> 147 us (1.12)
  between operations: 0.93 us -> 14.3 us
  starting transfers between devices: 43.6 us -> 36.5 us
  waiting for transfers between devices: 30.8 us -> 37.2 us
  local copies, waits for them, and re-layouts: 4.68 us -> 7.33 us
    ppermute x11 -> x5, starting transfers between devices: 23.3 us -> 11.4 us  [directed(): return lax.ppermute(x, (axis, CORE), pairs)]
    ppermute x11 -> x5, waiting for transfers between devices: 18.1 us -> 24.1 us  [directed(): return lax.ppermute(x, (axis, CORE), pairs)]
    ppermute x0 -> x3, starting transfers between devices: none -> 4.3 us  [shifted(): return lax.ppermute(x, axis, [(i, (i + step) % size) for i in range(size)])]
    unnamed x11 -> x17, local copies, waits for them, and re-layouts: 3.95 us -> 5.72 us
    ppermute x6 -> x4, starting transfers between devices: 10.5 us -> 11.8 us  [swapped(): return lax.ppermute(x, CORE, [(0, 1), (1, 0)])]
  transfers between devices with their start and end apart: 18 -> 14, of which waited for: 10 -> 6; matrix products, arithmetic and copies ran while one was open for 2% -> 2% of each run, Pallas kernels for 4% -> 3%
where the time goes in v6:
time: 147 us
  waiting for transfers between devices  37.2 us (25%)
  starting transfers between devices  36.5 us (25%)
  blocking collectives  27.1 us (18%)
  Pallas kernels  23.7 us (16%)
  between operations  14.3 us (10%)
  local copies, waits for them, and re-layouts  7.33 us (5%)
    all_to_all x1, blocking collectives, routed(): got = lax.all_to_all(copies, (*DP, 'tensor'), 0, 0, tiled=True)  27.1 us
    ppermute x5, waiting for transfers between devices, directed(): return lax.ppermute(x, (axis, CORE), pairs)  24.1 us
    pallas_call x1, Pallas kernels, precondition(): pl.pallas_call(body, out_shape=[jax.ShapeDtypeStruct(left.shape, F32), ja...  12.3 us
    ppermute x4, starting transfers between devices, swapped(): return lax.ppermute(x, CORE, [(0, 1), (1, 0)])  11.8 us
    ppermute x5, starting transfers between devices, directed(): return lax.ppermute(x, (axis, CORE), pairs)  11.4 us
    all_to_all x1, waiting for transfers between devices, routed(): lax.all_to_all(directions.reshape(slots, 8, width), DP, 0, 0, tiled=True)  10.5 us
    pallas_call x3, Pallas kernels, block_sums(): pl.pallas_call(body, out_shape=[jax.ShapeDtypeStruct((len(g), rows, half_...  9.86 us
    all_to_all x1, starting transfers between devices, routed(): lax.all_to_all(directions.reshape(slots, 8, width), DP, 0, 0, tiled=True)  8.9 us
  transfers between devices with their start and end apart: 14, of which 6 were waited for; matrix products, arithmetic and copies ran while one was open for 2% of the time, Pallas kernels for 3%

profile of v6, /device:TPU:1, one launch (start us, length us, event | category | flops | bytes accessed | tf_op | source)
XLA Modules:
  0.0 147.1 jit_solution(5898697797661413121)
XLA Ops:
  7.2 3.3 %collective-permute-start = (bf16[256,8192]{1,0:T(8,128)(2,1)}, bf16[256,8192]{1,0:T(8,128)(2,1)}, u32[]{:S(2)}, u32[]{:S(2)}) collective-permute-start(bf16[256,8192]{1,0:T(8,128)(2,1)} %a_ref.1), channel_id=1, source_target_pairs={{0,4},{4,0},{1,5},{5,1},{2,6},{6,2},{3,7},{7,3},{8,12},{12,8},{9,1... | collective-permute-start | bytes 12582920 | tf_op jit(solution)/shard_map/ppermute | solution.py:35
  10.5 1.1 copy.10
  11.8 2.2 %copy-done = bf16[256,8192]{1,0:T(8,128)(2,1)S(1)} copy-done((bf16[256,8192]{1,0:T(8,128)(2,1)S(1)}, bf16[256,8192]{1,0:T(8,128)(2,1)}, u32[]{:S(2)}) %copy-start) | copy-done | bytes 4194328
  14.0 0.7 copy-done.5
  14.6 2.1 %block_sums.3 = (f32[32,128,256]{2,1,0:T(8,128)S(1)}, f32[8,128,256]{2,1,0:T(8,128)S(1)}, f32[16,128,256]{2,1,0:T(8,128)S(1)}, f32[8,128,256]{2,1,0:T(8,128)S(1)}) custom-call(s32[64]{0:T(128)S(1)} %copy-done.5, bf16[256,8192]{1,0:T(8,128)(2,1)S(1)} %copy-done, bf16[512,256]{1,0:T(8,128)(2,1)S(1)} %bitcast.33), custom_call_target="tpu_custom_call" | custom-call | flops 1073741824 | bytes 12845056 | tf_op jit(solution)/shard_map/block_sums/pallas_call | solution.py:128
  16.7 1.0 copy-done.2
  17.7 4.8 %block_sums.4 = (bf16[32,128,256]{2,1,0:T(8,128)(2,1)}, bf16[8,128,256]{2,1,0:T(8,128)(2,1)S(1)}) custom-call(s32[64]{0:T(128)S(1)} %copy-done.6, bf16[256,8192]{1,0:T(8,128)(2,1)} %collective-permute-done.a_ref, bf16[512,256]{1,0:T(8,128)(2,1)S(1)} %collective-permute-done.1.k_ref, f32[32,128,256]{2,1,0:T(8,128)S(1)} %get-tuple-element.17.refs_0_, ...), custom_call_target="tpu_custom_call" | custom-call | flops 671088640 | bytes 12320768 | tf_op jit(solution)/shard_map/block_sums/pallas_call | solution.py:128
  22.5 0.8 copy-done.7
  23.3 1.1 collective-permute-start.2
  24.4 3.0 %block_sums.5 = (bf16[16,128,256]{2,1,0:T(8,128)(2,1)S(1)}, bf16[8,128,256]{2,1,0:T(8,128)(2,1)S(1)}) custom-call(s32[64]{0:T(128)S(1)} %copy-done.6, bf16[256,8192]{1,0:T(8,128)(2,1)} %collective-permute-done.a_ref, bf16[512,256]{1,0:T(8,128)(2,1)S(1)} %collective-permute-done.1.k_ref, f32[16,128,256]{2,1,0:T(8,128)S(1)} %get-tuple-element.20.refs_0_, ...), custom_call_target="tpu_custom_call" | custom-call | flops 402653184 | bytes 9175040 | tf_op jit(solution)/shard_map/block_sums/pallas_call | solution.py:128
  27.4 4.5 %collective-permute-done.2 = bf16[8,128,256]{2,1,0:T(8,128)(2,1)S(1)} collective-permute-done((bf16[8,128,256]{2,1,0:T(8,128)(2,1)}, bf16[8,128,256]{2,1,0:T(8,128)(2,1)S(1)}, u32[]{:S(2)}, u32[]{:S(2)}) %collective-permute-start.2) | collective-permute-done | bytes 524320 | tf_op jit(solution)/shard_map/ppermute | solution.py:26
  32.2 2.0 %collective-permute-start.3 = (bf16[16,128,256]{2,1,0:T(8,128)(2,1)S(1)}, bf16[16,128,256]{2,1,0:T(8,128)(2,1)S(1)}, u32[]{:S(2)}, u32[]{:S(2)}) collective-permute-start(bf16[16,128,256]{2,1,0:T(8,128)(2,1)S(1)} %pad_maximum_fusion), channel_id=1, source_target_pairs={{0,8},{4,28},{8,16},{12,4},{16,24},{20,12},{24,0},{28,20},{1,9},{5... | collective-permute-start | bytes 3145736 | tf_op jit(solution)/shard_map/ppermute | solution.py:26
  34.2 12.1 %collective-permute-done.3 = bf16[16,128,256]{2,1,0:T(8,128)(2,1)S(1)} collective-permute-done((bf16[16,128,256]{2,1,0:T(8,128)(2,1)S(1)}, bf16[16,128,256]{2,1,0:T(8,128)(2,1)S(1)}, u32[]{:S(2)}, u32[]{:S(2)}) %collective-permute-start.3) | collective-permute-done | bytes 1048608 | tf_op jit(solution)/shard_map/ppermute | solution.py:26
  46.4 4.5 %collective-permute-start.4 = (bf16[8,128,256]{2,1,0:T(8,128)(2,1)S(1)}, bf16[8,128,256]{2,1,0:T(8,128)(2,1)S(1)}, u32[]{:S(2)}, u32[]{:S(2)}) collective-permute-start(bf16[8,128,256]{2,1,0:T(8,128)(2,1)S(1)} %slice.101), channel_id=1, source_target_pairs={{0,4},{4,0},{1,5},{5,1},{2,6},{6,2},{3,7},{7,3},{8,12},{12,8},{9,1... | collective-permute-start | bytes 1572872 | tf_op jit(solution)/shard_map/ppermute | solution.py:35
  50.9 1.5 %collective-permute-done.4 = bf16[8,128,256]{2,1,0:T(8,128)(2,1)S(1)} collective-permute-done((bf16[8,128,256]{2,1,0:T(8,128)(2,1)S(1)}, bf16[8,128,256]{2,1,0:T(8,128)(2,1)S(1)}, u32[]{:S(2)}, u32[]{:S(2)}) %collective-permute-start.4) | collective-permute-done | bytes 524320 | tf_op jit(solution)/shard_map/ppermute | solution.py:35
  52.4 0.2 fusion.9
  52.7 4.4 %collective-permute-start.5 = (bf16[3,128,256]{2,1,0:T(8,128)(2,1)S(1)}, bf16[3,128,256]{2,1,0:T(8,128)(2,1)S(1)}, u32[]{:S(2)}, u32[]{:S(2)}) collective-permute-start(bf16[3,128,256]{2,1,0:T(8,128)(2,1)S(1)} %pad_maximum_fusion.1), channel_id=1, source_target_pairs={{0,64},{4,196},{32,96},{36,228},{64,128},{68,4},{96,160},{100,36},... | collective-permute-start | bytes 589832 | tf_op jit(solution)/shard_map/ppermute | solution.py:26
  57.1 7.5 %collective-permute-done.5 = bf16[3,128,256]{2,1,0:T(8,128)(2,1)S(1)} collective-permute-done((bf16[3,128,256]{2,1,0:T(8,128)(2,1)S(1)}, bf16[3,128,256]{2,1,0:T(8,128)(2,1)S(1)}, u32[]{:S(2)}, u32[]{:S(2)}) %collective-permute-start.5) | collective-permute-done | bytes 196640 | tf_op jit(solution)/shard_map/ppermute | solution.py:26
  64.7 3.9 %collective-permute-start.9 = (bf16[2,128,256]{2,1,0:T(8,128)(2,1)S(1)}, bf16[2,128,256]{2,1,0:T(8,128)(2,1)S(1)}, u32[]{:S(2)}, u32[]{:S(2)}) collective-permute-start(bf16[2,128,256]{2,1,0:T(8,128)(2,1)S(1)} %pad_maximum_fusion.2), channel_id=1, source_target_pairs={{0,64},{4,196},{32,96},{36,228},{64,128},{68,4},{96,160},{100,36},... | collective-permute-start | bytes 393224 | tf_op jit(solution)/shard_map/ppermute | solution.py:26
  68.8 1.0 slice_bitcast_fusion.3
  69.7 1.6 %collective-permute-start.6 = (bf16[128,256]{1,0:T(8,128)(2,1)S(1)}, bf16[128,256]{1,0:T(8,128)(2,1)S(1)}, u32[]{:S(2)}, u32[]{:S(2)}) collective-permute-start(bf16[128,256]{1,0:T(8,128)(2,1)S(1)} %get-tuple-element.43), channel_id=1, source_target_pairs={{0,16},{8,24},{16,0},{24,8},{1,17},{9,25},{17,1},{25,9},{2,18},{10... | collective-permute-start | bytes 196616 | tf_op jit(solution)/shard_map/ppermute | solution.py:31
  71.3 0.2 collective-permute-start.7
  71.5 2.5 %collective-permute-start.8 = (bf16[128,256]{1,0:T(8,128)(2,1)S(1)}, bf16[128,256]{1,0:T(8,128)(2,1)S(1)}, u32[]{:S(2)}, u32[]{:S(2)}) collective-permute-start(bf16[128,256]{1,0:T(8,128)(2,1)S(1)} %get-tuple-element.41), channel_id=1, source_target_pairs={{0,24},{8,0},{16,8},{24,16},{1,25},{9,1},{17,9},{25,17},{2,26},{10... | collective-permute-start | bytes 196616 | tf_op jit(solution)/shard_map/ppermute | solution.py:31
  74.0 3.9 %collective-permute-start.11 = (bf16[128,256]{1,0:T(8,128)(2,1)S(1)}, bf16[128,256]{1,0:T(8,128)(2,1)S(1)}, u32[]{:S(2)}, u32[]{:S(2)}) collective-permute-start(bf16[128,256]{1,0:T(8,128)(2,1)S(1)} %fusion.8), channel_id=1, source_target_pairs={{0,4},{4,0},{1,5},{5,1},{2,6},{6,2},{3,7},{7,3},{8,12},{12,8},{9,1... | collective-permute-start | bytes 196616 | tf_op jit(solution)/shard_map/ppermute | solution.py:35
  77.9 0.9 collective-permute-done.11.refs_7_
  78.9 12.3 %precondition.1 = (f32[512,512]{1,0:T(8,128)}, f32[128,128]{1,0:T(8,128)}, bf16[512,128]{1,0:T(8,128)(2,1)}) custom-call(bf16[128,256]{1,0:T(8,128)(2,1)S(1)} %get-tuple-element.44.refs_0_, bf16[128,256]{1,0:T(8,128)(2,1)S(1)} %collective-permute-done.6.refs_1_, bf16[128,256]{1,0:T(8,128)(2,1)S(1)} %collective-permute-done.7.refs_2_, ...), custom_call_target="tpu_custom_call" | custom-call | tf_op jit(solution)/shard_map/precondition/pallas_call | solution.py:229
  91.2 8.9 %all-to-all-start = ((bf16[64,8,128]{2,1,0:T(8,128)(2,1)}), bf16[64,8,128]{2,1,0:T(8,128)(2,1)S(1)}, u32[]{:S(2)}, u32[]{:S(2)}) async-start(bf16[64,8,128]{2,1,0:T(8,128)(2,1)} %bitcast.15), calls=%async_computation.1 | async-start | bytes 262144 | tf_op jit(solution)/shard_map/all_to_all | solution.py:274
  100.1 0.2 copy.11
  100.7 10.5 %all-to-all-done = bf16[64,8,128]{2,1,0:T(8,128)(2,1)S(1)} async-done(((bf16[64,8,128]{2,1,0:T(8,128)(2,1)}), bf16[64,8,128]{2,1,0:T(8,128)(2,1)S(1)}, u32[]{:S(2)}, u32[]{:S(2)}) %all-to-all-start) | async-done | bytes 131104 | tf_op jit(solution)/shard_map/all_to_all | solution.py:274
  111.2 0.4 fusion
  111.7 27.1 %all_to_all.10 = bf16[256,8,128]{2,1,0:T(8,128)(2,1)S(1)} all-to-all(bf16[256,8,128]{2,1,0:T(8,128)(2,1)S(1)} %bitcast.36), channel_id=1, replica_groups=mesh['dp_0'=8,'dp_1'=4,'dp_2'=2,'tensor'=4] {'dp_0','dp_1','dp_2','tensor'}, dimensions={0} | all-to-all | bytes 1048576 | tf_op jit(solution)/shard_map/all_to_all | solution.py:283
  138.8 1.5 %placed.1 = bf16[2,128,1024]{2,1,0:T(8,128)(2,1)} custom-call(bf16[2048,128]{1,0:T(8,128)(2,1)S(1)} %bitcast.31), custom_call_target="tpu_custom_call" | custom-call | tf_op jit(solution)/shard_map/placed/pallas_call | solution.py:259
  (43 shorter events, 1.3 us)
Async XLA Ops:
  7.2 10.6 %copy-start.6 = (s32[64]{0:T(128)S(1)}, s32[64]{0:T(128)}, u32[]{:S(2)}) copy-start(s32[64]{0:T(128)} %owner_ref.5) | copy-start | bytes 772
  7.2 61.6 %reduce-scatter.2.cloned.1.call-start = ((), (), s32[]{:S(2)}) async-start(), calls=%async_computation.3 | async-start | bytes 2359296 | tf_op jit(solution)/shard_map/reduce_scatter | solution.py:303
  7.2 10.5 %collective-permute-start = (bf16[256,8192]{1,0:T(8,128)(2,1)}, bf16[256,8192]{1,0:T(8,128)(2,1)}, u32[]{:S(2)}, u32[]{:S(2)}) collective-permute-start(bf16[256,8192]{1,0:T(8,128)(2,1)} %a_ref.1), channel_id=1, source_target_pairs={{0,4},{4,0},{1,5},{5,1},{2,6},{6,2},{3,7},{7,3},{8,12},{12,8},{9,1... | collective-permute-start | bytes 12582920 | tf_op jit(solution)/shard_map/ppermute | solution.py:35
  11.7 6.1 %collective-permute-start.1 = (bf16[512,256]{1,0:T(8,128)(2,1)S(1)}, bf16[512,256]{1,0:T(8,128)(2,1)S(1)}, u32[]{:S(2)}, u32[]{:S(2)}) collective-permute-start(bf16[512,256]{1,0:T(8,128)(2,1)S(1)} %bitcast.32), channel_id=1, source_target_pairs={{0,4},{4,0},{1,5},{5,1},{2,6},{6,2},{3,7},{7,3},{8,12},{12,8},{9,1... | collective-permute-start | bytes 786440 | tf_op jit(solution)/shard_map/ppermute | solution.py:35
  11.8 2.2 %copy-start = (bf16[256,8192]{1,0:T(8,128)(2,1)S(1)}, bf16[256,8192]{1,0:T(8,128)(2,1)}, u32[]{:S(2)}) copy-start(bf16[256,8192]{1,0:T(8,128)(2,1)} %a_ref.1) | copy-start | bytes 12582916
  13.9 0.7 copy-start.5
  16.7 1.0 copy-start.2
  17.7 6.7 %copy-start.3 = (f32[8,128,256]{2,1,0:T(8,128)S(1)}, f32[8,128,256]{2,1,0:T(8,128)}, u32[]{:S(2)}) copy-start(f32[8,128,256]{2,1,0:T(8,128)} %copy-done.2) | copy-start | bytes 3145732
  22.5 0.8 copy-start.7
  23.3 8.6 %collective-permute-start.2 = (bf16[8,128,256]{2,1,0:T(8,128)(2,1)}, bf16[8,128,256]{2,1,0:T(8,128)(2,1)S(1)}, u32[]{:S(2)}, u32[]{:S(2)}) collective-permute-start(bf16[8,128,256]{2,1,0:T(8,128)(2,1)} %copy-done.7), channel_id=1, source_target_pairs={{0,8},{4,28},{8,16},{12,4},{16,24},{20,12},{24,0},{28,20},{1,9},{5... | collective-permute-start | bytes 1572872 | tf_op jit(solution)/shard_map/ppermute | solution.py:26
  32.2 46.7 %copy-start.1 = (f32[1,1,512,512]{3,2,1,0:T(8,128)S(1)}, f32[1,1,512,512]{3,2,1,0:T(8,128)}, u32[]{:S(2)}) copy-start(f32[1,1,512,512]{3,2,1,0:T(8,128)} %param.8) | copy-start | bytes 3145732
  32.2 46.7 %copy-start.4 = (f32[1,1,128,128]{3,2,1,0:T(8,128)S(1)}, f32[1,1,128,128]{3,2,1,0:T(8,128)}, u32[]{:S(2)}) copy-start(f32[1,1,128,128]{3,2,1,0:T(8,128)} %param.9) | copy-start | bytes 196612
  32.2 14.1 %collective-permute-start.3 = (bf16[16,128,256]{2,1,0:T(8,128)(2,1)S(1)}, bf16[16,128,256]{2,1,0:T(8,128)(2,1)S(1)}, u32[]{:S(2)}, u32[]{:S(2)}) collective-permute-start(bf16[16,128,256]{2,1,0:T(8,128)(2,1)S(1)} %pad_maximum_fusion), channel_id=1, source_target_pairs={{0,8},{4,28},{8,16},{12,4},{16,24},{20,12},{24,0},{28,20},{1,9},{5... | collective-permute-start | bytes 3145736 | tf_op jit(solution)/shard_map/ppermute | solution.py:26
  46.4 6.0 %collective-permute-start.4 = (bf16[8,128,256]{2,1,0:T(8,128)(2,1)S(1)}, bf16[8,128,256]{2,1,0:T(8,128)(2,1)S(1)}, u32[]{:S(2)}, u32[]{:S(2)}) collective-permute-start(bf16[8,128,256]{2,1,0:T(8,128)(2,1)S(1)} %slice.101), channel_id=1, source_target_pairs={{0,4},{4,0},{1,5},{5,1},{2,6},{6,2},{3,7},{7,3},{8,12},{12,8},{9,1... | collective-permute-start | bytes 1572872 | tf_op jit(solution)/shard_map/ppermute | solution.py:35
  52.7 12.0 %collective-permute-start.5 = (bf16[3,128,256]{2,1,0:T(8,128)(2,1)S(1)}, bf16[3,128,256]{2,1,0:T(8,128)(2,1)S(1)}, u32[]{:S(2)}, u32[]{:S(2)}) collective-permute-start(bf16[3,128,256]{2,1,0:T(8,128)(2,1)S(1)} %pad_maximum_fusion.1), channel_id=1, source_target_pairs={{0,64},{4,196},{32,96},{36,228},{64,128},{68,4},{96,160},{100,36},... | collective-permute-start | bytes 589832 | tf_op jit(solution)/shard_map/ppermute | solution.py:26
  64.7 9.3 %collective-permute-start.9 = (bf16[2,128,256]{2,1,0:T(8,128)(2,1)S(1)}, bf16[2,128,256]{2,1,0:T(8,128)(2,1)S(1)}, u32[]{:S(2)}, u32[]{:S(2)}) collective-permute-start(bf16[2,128,256]{2,1,0:T(8,128)(2,1)S(1)} %pad_maximum_fusion.2), channel_id=1, source_target_pairs={{0,64},{4,196},{32,96},{36,228},{64,128},{68,4},{96,160},{100,36},... | collective-permute-start | bytes 393224 | tf_op jit(solution)/shard_map/ppermute | solution.py:26
  68.6 5.4 %collective-permute-start.10 = (bf16[2,128,256]{2,1,0:T(8,128)(2,1)S(1)}, bf16[2,128,256]{2,1,0:T(8,128)(2,1)S(1)}, u32[]{:S(2)}, u32[]{:S(2)}) collective-permute-start(bf16[2,128,256]{2,1,0:T(8,128)(2,1)S(1)} %pad_maximum_fusion.3), channel_id=1, source_target_pairs={{0,32},{4,228},{32,64},{36,4},{64,96},{68,36},{96,128},{100,68},{1... | collective-permute-start | bytes 393224 | tf_op jit(solution)/shard_map/ppermute | solution.py:26
  69.7 9.1 %collective-permute-start.6 = (bf16[128,256]{1,0:T(8,128)(2,1)S(1)}, bf16[128,256]{1,0:T(8,128)(2,1)S(1)}, u32[]{:S(2)}, u32[]{:S(2)}) collective-permute-start(bf16[128,256]{1,0:T(8,128)(2,1)S(1)} %get-tuple-element.43), channel_id=1, source_target_pairs={{0,16},{8,24},{16,0},{24,8},{1,17},{9,25},{17,1},{25,9},{2,18},{10... | collective-permute-start | bytes 196616 | tf_op jit(solution)/shard_map/ppermute | solution.py:31
  71.3 7.5 %collective-permute-start.7 = (bf16[128,256]{1,0:T(8,128)(2,1)S(1)}, bf16[128,256]{1,0:T(8,128)(2,1)S(1)}, u32[]{:S(2)}, u32[]{:S(2)}) collective-permute-start(bf16[128,256]{1,0:T(8,128)(2,1)S(1)} %get-tuple-element.42), channel_id=1, source_target_pairs={{0,8},{8,16},{16,24},{24,0},{1,9},{9,17},{17,25},{25,1},{2,10},{10... | collective-permute-start | bytes 196616 | tf_op jit(solution)/shard_map/ppermute | solution.py:31
  71.5 7.3 %collective-permute-start.8 = (bf16[128,256]{1,0:T(8,128)(2,1)S(1)}, bf16[128,256]{1,0:T(8,128)(2,1)S(1)}, u32[]{:S(2)}, u32[]{:S(2)}) collective-permute-start(bf16[128,256]{1,0:T(8,128)(2,1)S(1)} %get-tuple-element.41), channel_id=1, source_target_pairs={{0,24},{8,0},{16,8},{24,16},{1,25},{9,1},{17,9},{25,17},{2,26},{10... | collective-permute-start | bytes 196616 | tf_op jit(solution)/shard_map/ppermute | solution.py:31
  74.0 4.8 %collective-permute-start.11 = (bf16[128,256]{1,0:T(8,128)(2,1)S(1)}, bf16[128,256]{1,0:T(8,128)(2,1)S(1)}, u32[]{:S(2)}, u32[]{:S(2)}) collective-permute-start(bf16[128,256]{1,0:T(8,128)(2,1)S(1)} %fusion.8), channel_id=1, source_target_pairs={{0,4},{4,0},{1,5},{5,1},{2,6},{6,2},{3,7},{7,3},{8,12},{12,8},{9,1... | collective-permute-start | bytes 196616 | tf_op jit(solution)/shard_map/ppermute | solution.py:35
  91.2 20.0 %all-to-all-start = ((bf16[64,8,128]{2,1,0:T(8,128)(2,1)}), bf16[64,8,128]{2,1,0:T(8,128)(2,1)S(1)}, u32[]{:S(2)}, u32[]{:S(2)}) async-start(bf16[64,8,128]{2,1,0:T(8,128)(2,1)} %bitcast.15), calls=%async_computation.1 | async-start | bytes 262144 | tf_op jit(solution)/shard_map/all_to_all | solution.py:274
Sparse Core Ops, SparseCore 0:
  23.4 41.0 reduce-scatter.1

commit v7 on v5

--- a/solution.py
+++ b/solution.py
@@ -87,7 +87,7 @@
     return k
 
 
-def block_sums(groups, acts, kvt, block_rows, row_blocks, owner_table, before=None):
+def block_sums(groups, acts, kvt, block_rows, row_blocks, owner_table, before=None, fetch=False):
     half_cols = block_rows // 2
     rows = kvt.shape[0] // 4
     held = F32 if before is None else BF16
@@ -95,8 +95,9 @@
 
     def body(owner_ref, a_ref, k_ref, *refs):
         base_refs = [] if before is None else refs[: len(groups)]
-        out_refs = refs[len(base_refs) :]
+        out_refs = refs[len(base_refs) : len(base_refs) + len(groups)]
         z, y, core = (lax.axis_index(a) for a in DP)
+        work = []
         for g, group in enumerate(groups):
             for n, (half, dz, dy, flip) in enumerate(group):
                 to_z = (z + offset(dz, NZ, core)) % NZ
@@ -107,15 +108,34 @@
                 line = block // (row_blocks * col_blocks) * col_blocks + block % col_blocks
                 cols = pl.ds(pl.multiple_of((row * 2 + half) * half_cols, half_cols), half_cols)
                 lines = pl.ds(pl.multiple_of(line * rows, rows), rows)
-                summed = jnp.dot(k_ref[lines, :], a_ref[:, cols], preferred_element_type=F32)
-                if before is not None:
-                    summed = base_refs[g][n] + summed
-                out_refs[g][n] = summed.astype(held)
+                work.append((g, n, cols, lines))
+        if fetch:
+            held_ref, sems = refs[-2:]
+            copies = [
+                pltpu.make_async_copy(a_ref.at[:, w[2]], held_ref.at[k], sems.at[k])
+                for k, w in enumerate(work)
+            ]
+            for copy in copies:
+                copy.start()
+        for k, (g, n, cols, lines) in enumerate(work):
+            if fetch:
+                copies[k].wait()
+                part = held_ref[k]
+            else:
+                part = a_ref[:, cols]
+            summed = jnp.dot(k_ref[lines, :], part, preferred_element_type=F32)
+            if before is not None:
+                summed = base_refs[g][n] + summed
+            out_refs[g][n] = summed.astype(held)
 
     vmem = pl.BlockSpec(memory_space=pltpu.VMEM)
     smem = pl.BlockSpec(memory_space=pltpu.SMEM)
     inputs = [] if before is None else list(before)
     count = sum(len(g) for g in groups)
+    scratch = []
+    if fetch:
+        scratch = [pltpu.VMEM((count, acts.shape[0], half_cols), BF16)]
+        scratch.append(pltpu.SemaphoreType.DMA((count,)))
     moved = acts.size * 2 + kvt.size * 2 + count * rows * half_cols * (4 if before is None else 6)
     cost = pl.CostEstimate(
         flops=2 * count * rows * half_cols * acts.shape[0], transcendentals=0, bytes_accessed=moved
@@ -123,8 +143,9 @@
     return pl.pallas_call(
         body,
         out_shape=[jax.ShapeDtypeStruct((len(g), rows, half_cols), held) for g in groups],
-        in_specs=[smem, vmem, vmem] + [vmem] * len(inputs),
+        in_specs=[smem, pl.BlockSpec(memory_space=pl.ANY) if fetch else vmem, vmem] + [vmem] * len(inputs),
         out_specs=[vmem for _ in groups],
+        scratch_shapes=scratch,
         compiler_params=pltpu.CompilerParams(vmem_limit_bytes=VMEM_LIMIT),
         cost_estimate=cost,
         name="block_sums",
@@ -288,26 +309,27 @@
 
     four, two = ("fix", 4), ("fix", 2)
     first = [group_a(four, own(GIVE_Y + KEEP_Y)), group_b(two, own(GIVE_Z + KEEP_Z))]
-    rest = [group_a(("sign", k), e) for k in (3, 2, 1) for e in (GIVE_Y, KEEP_Y)]
+    first += [group_a(("sign", 3), e) for e in (GIVE_Y, KEEP_Y)]
+    rest = [group_a(("sign", k), e) for k in (2, 1) for e in (GIVE_Y, KEEP_Y)]
     rest += [group_b(("sign", 1), e) for e in (GIVE_Z, KEEP_Z)]
     rest += [group_a(("fix", 0), KEEP_Y), group_b(("fix", 0), KEEP_Z)]
     sizes = (block_rows, row_blocks, owner_table)
     sums = block_sums(first + rest, activations, kvt, *sizes)
-    a4, b2 = block_sums(first, acts_peer, kvt_peer, *sizes, before=sums[:2])
-    later = block_sums(rest, acts_peer, kvt_peer, *sizes, before=sums[2:])
-    a3g, a3k, a2g, a2k, a1g, a1k, b1g, b1k, a0, b0 = later
+    a4, b2, a3g, a3k = block_sums(
+        first, acts_peer, kvt_peer, *sizes, before=sums[:4], fetch=True
+    )
+    later = block_sums(rest, acts_peer, kvt_peer, *sizes, before=sums[4:])
+    a2g, a2k, a1g, a1k, b1g, b1k, a0, b0 = later
 
     n_a, n_b = len(own(GIVE_Y)), len(own(GIVE_Z))
-    b2 = directed(b2, Y)
+    a4 = directed(a4, Z, 2)
+    b2 = after(directed(b2, Y), a4)
     bg = added_inside(b1g, b2[:n_b], own_at(GIVE_Z))
-    bk = added_inside(b1k, b2[n_b:], own_at(KEEP_Z))
-    a4 = after(directed(a4, Z), bk)
-    ag = added_inside(a3g, a4[:n_a], own_at(GIVE_Y))
-    ak = added_inside(a3k, a4[n_a:], own_at(KEEP_Y))
-    ag = added(a2g, after(directed(ag, Z), ak))
-    bg = after(directed(bg, Y), ag)
-    ak = added(a2k, after(directed(ak, Z), bg))
-    ag = added(a1g, after(directed(ag, Z), ak))
+    bk = added_inside(b1k, after(b2[n_b:], bg), own_at(KEEP_Z))
+    ag = added_inside(wide(a2g, after(directed(a3g, Z), bk)), a4[:n_a], own_at(GIVE_Y))
+    ak = added_inside(wide(a2k, after(directed(a3k, Z), ag)), a4[n_a:], own_at(KEEP_Y))
+    bg = after(directed(bg, Y), ak)
+    ag = added(a1g, after(directed(ag, Z), bg))
     bk = after(directed(bk, Y), ag)
     b = wide(b0, bk, after(swapped(bg), bk))
     ak = added(a1k, after(directed(ak, Z), b))

time: 129 us -> 127 us (0.984)
  waiting for transfers between devices: 25.1 us -> 22.4 us
  Pallas kernels: 22.3 us -> 24.8 us
  starting transfers between devices: 47.7 us -> 46.1 us
    ppermute x15, starting transfers between devices: 30.5 us -> 27.3 us  [directed(): return lax.ppermute(x, (axis, CORE), pairs)]
    ppermute x15, waiting for transfers between devices: 12.6 us -> 9.9 us  [directed(): return lax.ppermute(x, (axis, CORE), pairs)]
    pallas_call x3, Pallas kernels: 8.51 us -> 11 us  [block_sums(): pl.pallas_call(body, out_shape=[jax.ShapeDtypeStruct((len(g), rows, half_...]
    ppermute x6, starting transfers between devices: 9.61 us -> 11 us  [swapped(): return lax.ppermute(x, CORE, [(0, 1), (1, 0)])]
    unnamed x9 -> x11, local copies, waits for them, and re-layouts: 3.95 us -> 3.95 us
  transfers between devices with their start and end apart: 22 -> 22, of which waited for: 10 -> 8; matrix products, arithmetic and copies ran while one was open for 2% -> 2% of each run, Pallas kernels for 5% -> 4%
where the time goes in v7:
time: 127 us
  starting transfers between devices  46.1 us (36%)
  blocking collectives  26.3 us (21%)
  Pallas kernels  24.8 us (20%)
  waiting for transfers between devices  22.4 us (18%)
  local copies, waits for them, and re-layouts  4.67 us (4%)
    ppermute x15, starting transfers between devices, directed(): return lax.ppermute(x, (axis, CORE), pairs)  27.3 us
    all_to_all x1, blocking collectives, routed(): got = lax.all_to_all(copies, (*DP, 'tensor'), 0, 0, tiled=True)  26.3 us
    pallas_call x1, Pallas kernels, precondition(): pl.pallas_call(body, out_shape=[jax.ShapeDtypeStruct(left.shape, F32), ja...  12.3 us
    ppermute x6, starting transfers between devices, swapped(): return lax.ppermute(x, CORE, [(0, 1), (1, 0)])  11 us
    pallas_call x3, Pallas kernels, block_sums(): pl.pallas_call(body, out_shape=[jax.ShapeDtypeStruct((len(g), rows, half_...  11 us
    all_to_all x1, waiting for transfers between devices, routed(): lax.all_to_all(directions.reshape(slots, 8, width), DP, 0, 0, tiled=True)  10.5 us
    ppermute x15, waiting for transfers between devices, directed(): return lax.ppermute(x, (axis, CORE), pairs)  9.9 us
    all_to_all x1, starting transfers between devices, routed(): lax.all_to_all(directions.reshape(slots, 8, width), DP, 0, 0, tiled=True)  7.8 us
  transfers between devices with their start and end apart: 22, of which 8 were waited for; matrix products, arithmetic and copies ran while one was open for 2% of the time, Pallas kernels for 4%

profile of v7, /device:TPU:1, one launch (start us, length us, event | category | flops | bytes accessed | tf_op | source)
XLA Modules:
  0.0 126.7 jit_solution(3200304437631291669)
XLA Ops:
  0.6 3.3 %collective-permute-start = (bf16[256,8192]{1,0:T(8,128)(2,1)}, bf16[256,8192]{1,0:T(8,128)(2,1)}, u32[]{:S(2)}, u32[]{:S(2)}) collective-permute-start(bf16[256,8192]{1,0:T(8,128)(2,1)} %a_ref.1), channel_id=1, source_target_pairs={{0,4},{4,0},{1,5},{5,1},{2,6},{6,2},{3,7},{7,3},{8,12},{12,8},{9,1... | collective-permute-start | bytes 12582920 | tf_op jit(solution)/shard_map/ppermute | solution.py:30
  4.0 1.1 copy.10
  5.2 2.2 %copy-done = bf16[256,8192]{1,0:T(8,128)(2,1)S(1)} copy-done((bf16[256,8192]{1,0:T(8,128)(2,1)S(1)}, bf16[256,8192]{1,0:T(8,128)(2,1)}, u32[]{:S(2)}) %copy-start) | copy-done | bytes 4194328
  8.0 2.1 %block_sums.3 = (f32[4,128,256]{2,1,0:T(8,128)S(1)}, f32[8,128,256]{2,1,0:T(8,128)S(1)}, f32[4,128,256]{2,1,0:T(8,128)S(1)}, f32[4,128,256]{2,1,0:T(8,128)S(1)},...) custom-call(s32[64]{0:T(128)S(1)} %copy-done.3, ...), custom_call_target="tpu_custom_call" | custom-call | flops 1073741824 | bytes 12845056 | tf_op jit(solution)/shard_map/block_sums/pallas_call | solution.py:143
  10.1 1.0 collective-permute-done.1.k_ref
  11.1 5.4 %block_sums.5 = (bf16[4,128,256]{2,1,0:T(8,128)(2,1)S(1)}, bf16[8,128,256]{2,1,0:T(8,128)(2,1)S(1)}, bf16[4,128,256]{2,1,0:T(8,128)(2,1)S(1)}, bf16[4,128,256]{2,1,0:T(8,128)(2,1)S(1)}) custom-call(s32[64]{0:T(128)S(1)} %copy-done.3, bf16[256,8192]{1,0:T(8,128)(2,1)} %collective-permute-done.a_ref, bf16[512,256]{1,0:T(8,128)(2,1)S(1)} %collective-permute-done.1.k_ref, ...), custom_call_target="tpu_custom_call" | custom-call | flops 335544320 | bytes 8388608 | tf_op jit(solution)/shard_map/block_sums/pallas_call | solution.py:143
  16.5 1.1 collective-permute-start.4
  17.6 6.0 %collective-permute-start.5 = (bf16[4,128,256]{2,1,0:T(8,128)(2,1)S(1)}, bf16[4,128,256]{2,1,0:T(8,128)(2,1)S(1)}, u32[]{:S(2)}, u32[]{:S(2)}) collective-permute-start(bf16[4,128,256]{2,1,0:T(8,128)(2,1)S(1)} %get-tuple-element.63), channel_id=1, source_target_pairs={{0,64},{4,196},{32,96},{36,228},{64,128},{68,4},{96,160},{100,36},... | collective-permute-start | bytes 786440 | tf_op jit(solution)/shard_map/ppermute | solution.py:26
  23.6 3.5 %block_sums.4 = (bf16[4,128,256]{2,1,0:T(8,128)(2,1)S(1)}, bf16[4,128,256]{2,1,0:T(8,128)(2,1)S(1)}, bf16[4,128,256]{2,1,0:T(8,128)(2,1)S(1)}, bf16[4,128,256]{2...) custom-call(s32[64]{0:T(128)S(1)} %copy-done.3, ...), custom_call_target="tpu_custom_call" | custom-call | flops 738197504 | bytes 13107200 | tf_op jit(solution)/shard_map/block_sums/pallas_call | solution.py:143
  27.2 0.8 collective-permute-start.3
  28.0 0.7 collective-permute-start.2
  28.7 1.0 collective-permute-done.5
  30.8 2.0 %collective-permute-done.3 = bf16[4,128,256]{2,1,0:T(8,128)(2,1)S(1)} collective-permute-done((bf16[4,128,256]{2,1,0:T(8,128)(2,1)S(1)}, bf16[4,128,256]{2,1,0:T(8,128)(2,1)S(1)}, u32[]{:S(2)}, u32[]{:S(2)}) %collective-permute-start.3) | collective-permute-done | bytes 262176 | tf_op jit(solution)/shard_map/ppermute | solution.py:26
  32.9 2.9 %collective-permute-start.8 = (bf16[4,128,256]{2,1,0:T(8,128)(2,1)S(1)}, bf16[4,128,256]{2,1,0:T(8,128)(2,1)S(1)}, u32[]{:S(2)}, u32[]{:S(2)}) collective-permute-start(bf16[4,128,256]{2,1,0:T(8,128)(2,1)S(1)} %pad_maximum_fusion.2), channel_id=1, source_target_pairs={{0,32},{4,228},{32,64},{36,4},{64,96},{68,36},{96,128},{100,68},{1... | collective-permute-start | bytes 786440 | tf_op jit(solution)/shard_map/ppermute | solution.py:26
  36.0 2.2 %collective-permute-done.9 = bf16[8,128,256]{2,1,0:T(8,128)(2,1)S(1)} collective-permute-done((bf16[8,128,256]{2,1,0:T(8,128)(2,1)S(1)}, bf16[8,128,256]{2,1,0:T(8,128)(2,1)S(1)}, u32[]{:S(2)}, u32[]{:S(2)}) %collective-permute-start.9) | collective-permute-done | bytes 524320 | tf_op jit(solution)/shard_map/ppermute | solution.py:26
  38.3 1.1 collective-permute-start.10
  39.4 3.5 %collective-permute-start.6 = (bf16[4,128,256]{2,1,0:T(8,128)(2,1)S(1)}, bf16[4,128,256]{2,1,0:T(8,128)(2,1)S(1)}, u32[]{:S(2)}, u32[]{:S(2)}) collective-permute-start(bf16[4,128,256]{2,1,0:T(8,128)(2,1)S(1)} %pad_maximum_fusion.3), channel_id=1, source_target_pairs={{0,32},{4,228},{32,64},{36,4},{64,96},{68,36},{96,128},{100,68},{1... | collective-permute-start | bytes 786440 | tf_op jit(solution)/shard_map/ppermute | solution.py:26
  43.0 1.2 collective-permute-start.13
  44.5 3.9 %collective-permute-start.12 = (bf16[3,128,256]{2,1,0:T(8,128)(2,1)S(1)}, bf16[3,128,256]{2,1,0:T(8,128)(2,1)S(1)}, u32[]{:S(2)}, u32[]{:S(2)}) collective-permute-start(bf16[3,128,256]{2,1,0:T(8,128)(2,1)S(1)} %pad_maximum_fusion.4), channel_id=1, source_target_pairs={{0,64},{4,196},{32,96},{36,228},{64,128},{68,4},{96,160},{100,36},... | collective-permute-start | bytes 589832 | tf_op jit(solution)/shard_map/ppermute | solution.py:26
  48.4 1.0 collective-permute-start.11
  49.5 1.7 %collective-permute-done.13 = bf16[4,128,256]{2,1,0:T(8,128)(2,1)S(1)} collective-permute-done((bf16[4,128,256]{2,1,0:T(8,128)(2,1)S(1)}, bf16[4,128,256]{2,1,0:T(8,128)(2,1)S(1)}, u32[]{:S(2)}, u32[]{:S(2)}) %collective-permute-start.13) | collective-permute-done | bytes 262176 | tf_op jit(solution)/shard_map/ppermute | solution.py:26
  51.1 2.9 %collective-permute-done.12 = bf16[3,128,256]{2,1,0:T(8,128)(2,1)S(1)} collective-permute-done((bf16[3,128,256]{2,1,0:T(8,128)(2,1)S(1)}, bf16[3,128,256]{2,1,0:T(8,128)(2,1)S(1)}, u32[]{:S(2)}, u32[]{:S(2)}) %collective-permute-start.12) | collective-permute-done | bytes 196640 | tf_op jit(solution)/shard_map/ppermute | solution.py:26
  54.6 3.1 %collective-permute-start.18 = (bf16[2,128,256]{2,1,0:T(8,128)(2,1)S(1)}, bf16[2,128,256]{2,1,0:T(8,128)(2,1)S(1)}, u32[]{:S(2)}, u32[]{:S(2)}) collective-permute-start(bf16[2,128,256]{2,1,0:T(8,128)(2,1)S(1)} %pad_maximum_fusion.5), channel_id=1, source_target_pairs={{0,64},{4,196},{32,96},{36,228},{64,128},{68,4},{96,160},{100,36},... | collective-permute-start | bytes 393224 | tf_op jit(solution)/shard_map/ppermute | solution.py:26
  57.9 1.8 %collective-permute-start.15 = (bf16[1,128,256]{2,1,0:T(8,128)(2,1)S(1)}, bf16[1,128,256]{2,1,0:T(8,128)(2,1)S(1)}, u32[]{:S(2)}, u32[]{:S(2)}) collective-permute-start(bf16[1,128,256]{2,1,0:T(8,128)(2,1)S(1)} %get-tuple-element.97), channel_id=1, source_target_pairs={{0,16},{4,20},{8,24},{12,28},{16,0},{20,4},{24,8},{28,12},{1,17},{... | collective-permute-start | bytes 196616 | tf_op jit(solution)/shard_map/ppermute | solution.py:26
  59.8 5.6 %collective-permute-start.20 = (bf16[128,256]{1,0:T(8,128)(2,1)S(1)}, bf16[128,256]{1,0:T(8,128)(2,1)S(1)}, u32[]{:S(2)}, u32[]{:S(2)}) collective-permute-start(bf16[128,256]{1,0:T(8,128)(2,1)S(1)} %fusion.10), channel_id=1, source_target_pairs={{0,4},{4,0},{1,5},{5,1},{2,6},{6,2},{3,7},{7,3},{8,12},{12,8},{9,1... | collective-permute-start | bytes 196616 | tf_op jit(solution)/shard_map/ppermute | solution.py:30
  65.5 0.9 collective-permute-start.17
  66.4 0.9 collective-permute-done.17.refs_3_
  67.3 12.3 %precondition.1 = (f32[512,512]{1,0:T(8,128)}, f32[128,128]{1,0:T(8,128)}, bf16[512,128]{1,0:T(8,128)(2,1)}) custom-call(f32[128,256]{1,0:T(8,128)S(1)} %slice_bitcast_fusion.1.refs_0_, bf16[128,256]{1,0:T(8,128)(2,1)S(1)} %bitcast.35, bf16[128,256]{1,0:T(8,128)(2,1)S(1)} %get-tuple-element.99.refs_2_, bf16[128,256]{1,0:T(8,128)(2,1)S(1)} %collective-permute-done.17.refs_3_, ...), custom_call_target="tpu_custom_call" | custom-call | tf_op jit(solution)/shard_map/precondition/pallas_call | solution.py:245
  79.6 7.8 %all-to-all-start = ((bf16[64,8,128]{2,1,0:T(8,128)(2,1)}), bf16[64,8,128]{2,1,0:T(8,128)(2,1)S(1)}, u32[]{:S(2)}, u32[]{:S(2)}) async-start(bf16[64,8,128]{2,1,0:T(8,128)(2,1)} %bitcast.15), calls=%async_computation | async-start | bytes 262144 | tf_op jit(solution)/shard_map/all_to_all | solution.py:290
  88.0 10.5 %all-to-all-done = bf16[64,8,128]{2,1,0:T(8,128)(2,1)S(1)} async-done(((bf16[64,8,128]{2,1,0:T(8,128)(2,1)}), bf16[64,8,128]{2,1,0:T(8,128)(2,1)S(1)}, u32[]{:S(2)}, u32[]{:S(2)}) %all-to-all-start) | async-done | bytes 131104 | tf_op jit(solution)/shard_map/all_to_all | solution.py:290
  99.0 26.3 %all_to_all.10 = bf16[256,8,128]{2,1,0:T(8,128)(2,1)S(1)} all-to-all(bf16[256,8,128]{2,1,0:T(8,128)(2,1)S(1)} %bitcast.36), channel_id=1, replica_groups=mesh['dp_0'=8,'dp_1'=4,'dp_2'=2,'tensor'=4] {'dp_0','dp_1','dp_2','tensor'}, dimensions={0} | all-to-all | bytes 1048576 | tf_op jit(solution)/shard_map/all_to_all | solution.py:299
  125.3 1.5 %placed.1 = bf16[2,128,1024]{2,1,0:T(8,128)(2,1)} custom-call(bf16[2048,128]{1,0:T(8,128)(2,1)S(1)} %bitcast.30), custom_call_target="tpu_custom_call" | custom-call | tf_op jit(solution)/shard_map/placed/pallas_call | solution.py:275
  (69 shorter events, 4.4 us)
Async XLA Ops:
  0.6 10.5 %collective-permute-start = (bf16[256,8192]{1,0:T(8,128)(2,1)}, bf16[256,8192]{1,0:T(8,128)(2,1)}, u32[]{:S(2)}, u32[]{:S(2)}) collective-permute-start(bf16[256,8192]{1,0:T(8,128)(2,1)} %a_ref.1), channel_id=1, source_target_pairs={{0,4},{4,0},{1,5},{5,1},{2,6},{6,2},{3,7},{7,3},{8,12},{12,8},{9,1... | collective-permute-start | bytes 12582920 | tf_op jit(solution)/shard_map/ppermute | solution.py:30
  5.1 6.1 %collective-permute-start.1 = (bf16[512,256]{1,0:T(8,128)(2,1)S(1)}, bf16[512,256]{1,0:T(8,128)(2,1)S(1)}, u32[]{:S(2)}, u32[]{:S(2)}) collective-permute-start(bf16[512,256]{1,0:T(8,128)(2,1)S(1)} %bitcast.32), channel_id=1, source_target_pairs={{0,4},{4,0},{1,5},{5,1},{2,6},{6,2},{3,7},{7,3},{8,12},{12,8},{9,1... | collective-permute-start | bytes 786440 | tf_op jit(solution)/shard_map/ppermute | solution.py:30
  5.2 2.2 %copy-start = (bf16[256,8192]{1,0:T(8,128)(2,1)S(1)}, bf16[256,8192]{1,0:T(8,128)(2,1)}, u32[]{:S(2)}) copy-start(bf16[256,8192]{1,0:T(8,128)(2,1)} %a_ref.1) | copy-start | bytes 12582916
  7.4 0.7 copy-start.3
  16.5 13.2 %collective-permute-start.4 = (bf16[8,128,256]{2,1,0:T(8,128)(2,1)S(1)}, bf16[8,128,256]{2,1,0:T(8,128)(2,1)S(1)}, u32[]{:S(2)}, u32[]{:S(2)}) collective-permute-start(bf16[8,128,256]{2,1,0:T(8,128)(2,1)S(1)} %get-tuple-element.62), channel_id=1, source_target_pairs={{0,8},{4,28},{8,16},{12,4},{16,24},{20,12},{24,0},{28,20},{1,9},{5... | collective-permute-start | bytes 1572872 | tf_op jit(solution)/shard_map/ppermute | solution.py:26
  17.6 12.1 %collective-permute-start.5 = (bf16[4,128,256]{2,1,0:T(8,128)(2,1)S(1)}, bf16[4,128,256]{2,1,0:T(8,128)(2,1)S(1)}, u32[]{:S(2)}, u32[]{:S(2)}) collective-permute-start(bf16[4,128,256]{2,1,0:T(8,128)(2,1)S(1)} %get-tuple-element.63), channel_id=1, source_target_pairs={{0,64},{4,196},{32,96},{36,228},{64,128},{68,4},{96,160},{100,36},... | collective-permute-start | bytes 786440 | tf_op jit(solution)/shard_map/ppermute | solution.py:26
  27.2 5.6 %collective-permute-start.3 = (bf16[4,128,256]{2,1,0:T(8,128)(2,1)S(1)}, bf16[4,128,256]{2,1,0:T(8,128)(2,1)S(1)}, u32[]{:S(2)}, u32[]{:S(2)}) collective-permute-start(bf16[4,128,256]{2,1,0:T(8,128)(2,1)S(1)} %get-tuple-element.60), channel_id=1, source_target_pairs={{0,32},{4,228},{32,64},{36,4},{64,96},{68,36},{96,128},{100,68},{1... | collective-permute-start | bytes 786440 | tf_op jit(solution)/shard_map/ppermute | solution.py:26
  28.0 7.9 %collective-permute-start.2 = (bf16[4,128,256]{2,1,0:T(8,128)(2,1)S(1)}, bf16[4,128,256]{2,1,0:T(8,128)(2,1)S(1)}, u32[]{:S(2)}, u32[]{:S(2)}) collective-permute-start(bf16[4,128,256]{2,1,0:T(8,128)(2,1)S(1)} %get-tuple-element.58), channel_id=1, source_target_pairs={{0,32},{4,228},{32,64},{36,4},{64,96},{68,36},{96,128},{100,68},{1... | collective-permute-start | bytes 786440 | tf_op jit(solution)/shard_map/ppermute | solution.py:26
  29.9 8.4 %collective-permute-start.9 = (bf16[8,128,256]{2,1,0:T(8,128)(2,1)S(1)}, bf16[8,128,256]{2,1,0:T(8,128)(2,1)S(1)}, u32[]{:S(2)}, u32[]{:S(2)}) collective-permute-start(bf16[8,128,256]{2,1,0:T(8,128)(2,1)S(1)} %pad_maximum_fusion), channel_id=1, source_target_pairs={{0,8},{4,28},{8,16},{12,4},{16,24},{20,12},{24,0},{28,20},{1,9},{5... | collective-permute-start | bytes 1572872 | tf_op jit(solution)/shard_map/ppermute | solution.py:26
  30.5 13.6 %collective-permute-start.7 = (bf16[8,128,256]{2,1,0:T(8,128)(2,1)S(1)}, bf16[8,128,256]{2,1,0:T(8,128)(2,1)S(1)}, u32[]{:S(2)}, u32[]{:S(2)}) collective-permute-start(bf16[8,128,256]{2,1,0:T(8,128)(2,1)S(1)} %pad_maximum_fusion.1), channel_id=1, source_target_pairs={{0,8},{4,28},{8,16},{12,4},{16,24},{20,12},{24,0},{28,20},{1,9},{5... | collective-permute-start | bytes 1572872 | tf_op jit(solution)/shard_map/ppermute | solution.py:26
  32.9 10.0 %collective-permute-start.8 = (bf16[4,128,256]{2,1,0:T(8,128)(2,1)S(1)}, bf16[4,128,256]{2,1,0:T(8,128)(2,1)S(1)}, u32[]{:S(2)}, u32[]{:S(2)}) collective-permute-start(bf16[4,128,256]{2,1,0:T(8,128)(2,1)S(1)} %pad_maximum_fusion.2), channel_id=1, source_target_pairs={{0,32},{4,228},{32,64},{36,4},{64,96},{68,36},{96,128},{100,68},{1... | collective-permute-start | bytes 786440 | tf_op jit(solution)/shard_map/ppermute | solution.py:26
  38.3 5.9 %collective-permute-start.10 = (bf16[8,128,256]{2,1,0:T(8,128)(2,1)S(1)}, bf16[8,128,256]{2,1,0:T(8,128)(2,1)S(1)}, u32[]{:S(2)}, u32[]{:S(2)}) collective-permute-start(bf16[8,128,256]{2,1,0:T(8,128)(2,1)S(1)} %collective-permute-done.9), channel_id=1, source_target_pairs={{0,4},{4,0},{1,5},{5,1},{2,6},{6,2},{3,7},{7,3},{8,12},{12,8},{9,1... | collective-permute-start | bytes 1572872 | tf_op jit(solution)/shard_map/ppermute | solution.py:30
  39.4 8.9 %collective-permute-start.6 = (bf16[4,128,256]{2,1,0:T(8,128)(2,1)S(1)}, bf16[4,128,256]{2,1,0:T(8,128)(2,1)S(1)}, u32[]{:S(2)}, u32[]{:S(2)}) collective-permute-start(bf16[4,128,256]{2,1,0:T(8,128)(2,1)S(1)} %pad_maximum_fusion.3), channel_id=1, source_target_pairs={{0,32},{4,228},{32,64},{36,4},{64,96},{68,36},{96,128},{100,68},{1... | collective-permute-start | bytes 786440 | tf_op jit(solution)/shard_map/ppermute | solution.py:26
  43.0 8.2 %collective-permute-start.13 = (bf16[4,128,256]{2,1,0:T(8,128)(2,1)S(1)}, bf16[4,128,256]{2,1,0:T(8,128)(2,1)S(1)}, u32[]{:S(2)}, u32[]{:S(2)}) collective-permute-start(bf16[4,128,256]{2,1,0:T(8,128)(2,1)S(1)} %add_convert_fusion.2), channel_id=1, source_target_pairs={{0,32},{4,228},{32,64},{36,4},{64,96},{68,36},{96,128},{100,68},{1... | collective-permute-start | bytes 786440 | tf_op jit(solution)/shard_map/ppermute | solution.py:26
  44.2 23.1 %copy-start.1 = (f32[1,1,512,512]{3,2,1,0:T(8,128)S(1)}, f32[1,1,512,512]{3,2,1,0:T(8,128)}, u32[]{:S(2)}) copy-start(f32[1,1,512,512]{3,2,1,0:T(8,128)} %param.8) | copy-start | bytes 3145732
  44.2 23.1 %copy-start.2 = (f32[1,1,128,128]{3,2,1,0:T(8,128)S(1)}, f32[1,1,128,128]{3,2,1,0:T(8,128)}, u32[]{:S(2)}) copy-start(f32[1,1,128,128]{3,2,1,0:T(8,128)} %param.9) | copy-start | bytes 196612
  44.4 43.0 %copy-start.4 = (s32[64]{0:T(128)S(1)}, s32[64]{0:T(128)}, u32[]{:S(2)}) copy-start(s32[64]{0:T(128)} %owner_ref.5) | copy-start | bytes 772
  44.5 9.6 %collective-permute-start.12 = (bf16[3,128,256]{2,1,0:T(8,128)(2,1)S(1)}, bf16[3,128,256]{2,1,0:T(8,128)(2,1)S(1)}, u32[]{:S(2)}, u32[]{:S(2)}) collective-permute-start(bf16[3,128,256]{2,1,0:T(8,128)(2,1)S(1)} %pad_maximum_fusion.4), channel_id=1, source_target_pairs={{0,64},{4,196},{32,96},{36,228},{64,128},{68,4},{96,160},{100,36},... | collective-permute-start | bytes 589832 | tf_op jit(solution)/shard_map/ppermute | solution.py:26
  48.4 9.2 %collective-permute-start.11 = (bf16[4,128,256]{2,1,0:T(8,128)(2,1)S(1)}, bf16[4,128,256]{2,1,0:T(8,128)(2,1)S(1)}, u32[]{:S(2)}, u32[]{:S(2)}) collective-permute-start(bf16[4,128,256]{2,1,0:T(8,128)(2,1)S(1)} %add_convert_fusion.1), channel_id=1, source_target_pairs={{0,32},{4,228},{32,64},{36,4},{64,96},{68,36},{96,128},{100,68},{1... | collective-permute-start | bytes 786440 | tf_op jit(solution)/shard_map/ppermute | solution.py:26
  51.1 6.5 %collective-permute-start.14 = (bf16[4,128,256]{2,1,0:T(8,128)(2,1)S(1)}, bf16[4,128,256]{2,1,0:T(8,128)(2,1)S(1)}, u32[]{:S(2)}, u32[]{:S(2)}) collective-permute-start(bf16[4,128,256]{2,1,0:T(8,128)(2,1)S(1)} %collective-permute-done.13), channel_id=1, source_target_pairs={{0,4},{4,0},{1,5},{5,1},{2,6},{6,2},{3,7},{7,3},{8,12},{12,8},{9,1... | collective-permute-start | bytes 786440 | tf_op jit(solution)/shard_map/ppermute | solution.py:30
  54.2 5.6 %collective-permute-start.19 = (bf16[2,128,256]{2,1,0:T(8,128)(2,1)S(1)}, bf16[2,128,256]{2,1,0:T(8,128)(2,1)S(1)}, u32[]{:S(2)}, u32[]{:S(2)}) collective-permute-start(bf16[2,128,256]{2,1,0:T(8,128)(2,1)S(1)} %pad_maximum_fusion.7), channel_id=1, source_target_pairs={{0,32},{4,228},{32,64},{36,4},{64,96},{68,36},{96,128},{100,68},{1... | collective-permute-start | bytes 393224 | tf_op jit(solution)/shard_map/ppermute | solution.py:26
  54.6 5.2 %collective-permute-start.18 = (bf16[2,128,256]{2,1,0:T(8,128)(2,1)S(1)}, bf16[2,128,256]{2,1,0:T(8,128)(2,1)S(1)}, u32[]{:S(2)}, u32[]{:S(2)}) collective-permute-start(bf16[2,128,256]{2,1,0:T(8,128)(2,1)S(1)} %pad_maximum_fusion.5), channel_id=1, source_target_pairs={{0,64},{4,196},{32,96},{36,228},{64,128},{68,4},{96,160},{100,36},... | collective-permute-start | bytes 393224 | tf_op jit(solution)/shard_map/ppermute | solution.py:26
  57.8 7.7 %collective-permute-start.16 = (bf16[2,128,256]{2,1,0:T(8,128)(2,1)S(1)}, bf16[2,128,256]{2,1,0:T(8,128)(2,1)S(1)}, u32[]{:S(2)}, u32[]{:S(2)}) collective-permute-start(bf16[2,128,256]{2,1,0:T(8,128)(2,1)S(1)} %pad_maximum_fusion.6), channel_id=1, source_target_pairs={{0,8},{4,28},{8,16},{12,4},{16,24},{20,12},{24,0},{28,20},{1,9},{5... | collective-permute-start | bytes 393224 | tf_op jit(solution)/shard_map/ppermute | solution.py:26
  57.9 8.4 %collective-permute-start.15 = (bf16[1,128,256]{2,1,0:T(8,128)(2,1)S(1)}, bf16[1,128,256]{2,1,0:T(8,128)(2,1)S(1)}, u32[]{:S(2)}, u32[]{:S(2)}) collective-permute-start(bf16[1,128,256]{2,1,0:T(8,128)(2,1)S(1)} %get-tuple-element.97), channel_id=1, source_target_pairs={{0,16},{4,20},{8,24},{12,28},{16,0},{20,4},{24,8},{28,12},{1,17},{... | collective-permute-start | bytes 196616 | tf_op jit(solution)/shard_map/ppermute | solution.py:26
  59.8 6.6 %collective-permute-start.20 = (bf16[128,256]{1,0:T(8,128)(2,1)S(1)}, bf16[128,256]{1,0:T(8,128)(2,1)S(1)}, u32[]{:S(2)}, u32[]{:S(2)}) collective-permute-start(bf16[128,256]{1,0:T(8,128)(2,1)S(1)} %fusion.10), channel_id=1, source_target_pairs={{0,4},{4,0},{1,5},{5,1},{2,6},{6,2},{3,7},{7,3},{8,12},{12,8},{9,1... | collective-permute-start | bytes 196616 | tf_op jit(solution)/shard_map/ppermute | solution.py:30
  65.5 1.8 %collective-permute-start.17 = (bf16[128,256]{1,0:T(8,128)(2,1)S(1)}, bf16[128,256]{1,0:T(8,128)(2,1)S(1)}, u32[]{:S(2)}, u32[]{:S(2)}) collective-permute-start(bf16[128,256]{1,0:T(8,128)(2,1)S(1)} %get-tuple-element.98), channel_id=1, source_target_pairs={{0,4},{4,0},{1,5},{5,1},{2,6},{6,2},{3,7},{7,3},{8,12},{12,8},{9,1... | collective-permute-start | bytes 196616 | tf_op jit(solution)/shard_map/ppermute | solution.py:30
  79.6 18.9 %all-to-all-start = ((bf16[64,8,128]{2,1,0:T(8,128)(2,1)}), bf16[64,8,128]{2,1,0:T(8,128)(2,1)S(1)}, u32[]{:S(2)}, u32[]{:S(2)}) async-start(bf16[64,8,128]{2,1,0:T(8,128)(2,1)} %bitcast.15), calls=%async_computation | async-start | bytes 262144 | tf_op jit(solution)/shard_map/all_to_all | solution.py:290

commit v8 on v7

--- a/solution.py
+++ b/solution.py
@@ -87,7 +87,7 @@
     return k
 
 
-def block_sums(groups, acts, kvt, block_rows, row_blocks, owner_table, before=None, fetch=False):
+def block_sums(groups, acts, kvt, block_rows, row_blocks, owner_table, before=None):
     half_cols = block_rows // 2
     rows = kvt.shape[0] // 4
     held = F32 if before is None else BF16
@@ -109,21 +109,8 @@
                 cols = pl.ds(pl.multiple_of((row * 2 + half) * half_cols, half_cols), half_cols)
                 lines = pl.ds(pl.multiple_of(line * rows, rows), rows)
                 work.append((g, n, cols, lines))
-        if fetch:
-            held_ref, sems = refs[-2:]
-            copies = [
-                pltpu.make_async_copy(a_ref.at[:, w[2]], held_ref.at[k], sems.at[k])
-                for k, w in enumerate(work)
-            ]
-            for copy in copies:
-                copy.start()
-        for k, (g, n, cols, lines) in enumerate(work):
-            if fetch:
-                copies[k].wait()
-                part = held_ref[k]
-            else:
-                part = a_ref[:, cols]
-            summed = jnp.dot(k_ref[lines, :], part, preferred_element_type=F32)
+        for g, n, cols, lines in work:
+            summed = jnp.dot(k_ref[lines, :], a_ref[:, cols], preferred_element_type=F32)
             if before is not None:
                 summed = base_refs[g][n] + summed
             out_refs[g][n] = summed.astype(held)
@@ -132,10 +119,6 @@
     smem = pl.BlockSpec(memory_space=pltpu.SMEM)
     inputs = [] if before is None else list(before)
     count = sum(len(g) for g in groups)
-    scratch = []
-    if fetch:
-        scratch = [pltpu.VMEM((count, acts.shape[0], half_cols), BF16)]
-        scratch.append(pltpu.SemaphoreType.DMA((count,)))
     moved = acts.size * 2 + kvt.size * 2 + count * rows * half_cols * (4 if before is None else 6)
     cost = pl.CostEstimate(
         flops=2 * count * rows * half_cols * acts.shape[0], transcendentals=0, bytes_accessed=moved
@@ -143,9 +126,8 @@
     return pl.pallas_call(
         body,
         out_shape=[jax.ShapeDtypeStruct((len(g), rows, half_cols), held) for g in groups],
-        in_specs=[smem, pl.BlockSpec(memory_space=pl.ANY) if fetch else vmem, vmem] + [vmem] * len(inputs),
+        in_specs=[smem, vmem, vmem] + [vmem] * len(inputs),
         out_specs=[vmem for _ in groups],
-        scratch_shapes=scratch,
         compiler_params=pltpu.CompilerParams(vmem_limit_bytes=VMEM_LIMIT),
         cost_estimate=cost,
         name="block_sums",
@@ -315,9 +297,7 @@
     rest += [group_a(("fix", 0), KEEP_Y), group_b(("fix", 0), KEEP_Z)]
     sizes = (block_rows, row_blocks, owner_table)
     sums = block_sums(first + rest, activations, kvt, *sizes)
-    a4, b2, a3g, a3k = block_sums(
-        first, acts_peer, kvt_peer, *sizes, before=sums[:4], fetch=True
-    )
+    a4, b2, a3g, a3k = block_sums(first, acts_peer, kvt_peer, *sizes, before=sums[:4])
     later = block_sums(rest, acts_peer, kvt_peer, *sizes, before=sums[4:])
     a2g, a2k, a1g, a1k, b1g, b1k, a0, b0 = later
 

time: 127 us -> 125 us (0.984)
  Pallas kernels: 24.8 us -> 22.3 us
    pallas_call x3, Pallas kernels: 11 us -> 8.48 us  [block_sums(): pl.pallas_call(body, out_shape=[jax.ShapeDtypeStruct((len(g), rows, half_...]
  transfers between devices with their start and end apart: 22 -> 22, of which waited for: 8 -> 9; matrix products, arithmetic and copies ran while one was open for 2% -> 2% of each run, Pallas kernels for 4% -> 4%
where the time goes in v8:
time: 125 us; the launch traced here: 124 us
  starting transfers between devices  46.1 us (37%)
  blocking collectives  26.3 us (21%)
  Pallas kernels  22.3 us (18%)
  waiting for transfers between devices  22.3 us (18%)
  local copies, waits for them, and re-layouts  4.67 us (4%)
    ppermute x15, starting transfers between devices, directed(): return lax.ppermute(x, (axis, CORE), pairs)  27.4 us
    all_to_all x1, blocking collectives, routed(): got = lax.all_to_all(copies, (*DP, 'tensor'), 0, 0, tiled=True)  26.3 us
    pallas_call x1, Pallas kernels, precondition(): pl.pallas_call(body, out_shape=[jax.ShapeDtypeStruct(left.shape, F32), ja...  12.3 us
    ppermute x6, starting transfers between devices, swapped(): return lax.ppermute(x, CORE, [(0, 1), (1, 0)])  10.8 us
    all_to_all x1, waiting for transfers between devices, routed(): lax.all_to_all(directions.reshape(slots, 8, width), DP, 0, 0, tiled=True)  10.5 us
    ppermute x15, waiting for transfers between devices, directed(): return lax.ppermute(x, (axis, CORE), pairs)  9.85 us
    pallas_call x3, Pallas kernels, block_sums(): pl.pallas_call(body, out_shape=[jax.ShapeDtypeStruct((len(g), rows, half_...  8.48 us
    all_to_all x1, starting transfers between devices, routed(): lax.all_to_all(directions.reshape(slots, 8, width), DP, 0, 0, tiled=True)  7.97 us
  transfers between devices with their start and end apart: 22, of which 9 were waited for; matrix products, arithmetic and copies ran while one was open for 2% of the time, Pallas kernels for 4%

profile of v8, /device:TPU:1, one launch (start us, length us, event | category | flops | bytes accessed | tf_op | source)
XLA Modules:
  0.0 124.2 jit_solution(4715477110673955317)
XLA Ops:
  0.6 3.3 %collective-permute-start = (bf16[256,8192]{1,0:T(8,128)(2,1)}, bf16[256,8192]{1,0:T(8,128)(2,1)}, u32[]{:S(2)}, u32[]{:S(2)}) collective-permute-start(bf16[256,8192]{1,0:T(8,128)(2,1)} %a_ref.1), channel_id=1, source_target_pairs={{0,4},{4,0},{1,5},{5,1},{2,6},{6,2},{3,7},{7,3},{8,12},{12,8},{9,1... | collective-permute-start | bytes 12582920 | tf_op jit(solution)/shard_map/ppermute | solution.py:30
  4.0 1.1 copy.10
  5.2 2.2 %copy-done = bf16[256,8192]{1,0:T(8,128)(2,1)S(1)} copy-done((bf16[256,8192]{1,0:T(8,128)(2,1)S(1)}, bf16[256,8192]{1,0:T(8,128)(2,1)}, u32[]{:S(2)}) %copy-start) | copy-done | bytes 4194328
  7.4 0.7 copy-done.3
  8.0 2.1 %block_sums.3 = (f32[4,128,256]{2,1,0:T(8,128)S(1)}, f32[8,128,256]{2,1,0:T(8,128)S(1)}, f32[4,128,256]{2,1,0:T(8,128)S(1)}, f32[4,128,256]{2,1,0:T(8,128)S(1)},...) custom-call(s32[64]{0:T(128)S(1)} %copy-done.3, ...), custom_call_target="tpu_custom_call" | custom-call | flops 1073741824 | bytes 12845056 | tf_op jit(solution)/shard_map/block_sums/pallas_call | solution.py:126
  10.1 1.0 collective-permute-done.1.k_ref
  11.1 2.9 %block_sums.5 = (bf16[4,128,256]{2,1,0:T(8,128)(2,1)S(1)}, bf16[8,128,256]{2,1,0:T(8,128)(2,1)S(1)}, bf16[4,128,256]{2,1,0:T(8,128)(2,1)S(1)}, bf16[4,128,256]{2,1,0:T(8,128)(2,1)S(1)}) custom-call(s32[64]{0:T(128)S(1)} %copy-done.3, bf16[256,8192]{1,0:T(8,128)(2,1)} %collective-permute-done.a_ref, bf16[512,256]{1,0:T(8,128)(2,1)S(1)} %collective-permute-done.1.k_ref, ...), custom_call_target="tpu_custom_call" | custom-call | flops 335544320 | bytes 8388608 | tf_op jit(solution)/shard_map/block_sums/pallas_call | solution.py:126
  14.0 1.1 collective-permute-start.4
  15.1 6.0 %collective-permute-start.5 = (bf16[4,128,256]{2,1,0:T(8,128)(2,1)S(1)}, bf16[4,128,256]{2,1,0:T(8,128)(2,1)S(1)}, u32[]{:S(2)}, u32[]{:S(2)}) collective-permute-start(bf16[4,128,256]{2,1,0:T(8,128)(2,1)S(1)} %get-tuple-element.63), channel_id=1, source_target_pairs={{0,64},{4,196},{32,96},{36,228},{64,128},{68,4},{96,160},{100,36},... | collective-permute-start | bytes 786440 | tf_op jit(solution)/shard_map/ppermute | solution.py:26
  21.1 3.5 %block_sums.4 = (bf16[4,128,256]{2,1,0:T(8,128)(2,1)S(1)}, bf16[4,128,256]{2,1,0:T(8,128)(2,1)S(1)}, bf16[4,128,256]{2,1,0:T(8,128)(2,1)S(1)}, bf16[4,128,256]{2...) custom-call(s32[64]{0:T(128)S(1)} %copy-done.3, ...), custom_call_target="tpu_custom_call" | custom-call | flops 738197504 | bytes 13107200 | tf_op jit(solution)/shard_map/block_sums/pallas_call | solution.py:126
  24.7 0.8 collective-permute-start.3
  25.5 0.7 collective-permute-start.2
  26.2 1.0 collective-permute-done.5
  28.3 2.0 %collective-permute-done.3 = bf16[4,128,256]{2,1,0:T(8,128)(2,1)S(1)} collective-permute-done((bf16[4,128,256]{2,1,0:T(8,128)(2,1)S(1)}, bf16[4,128,256]{2,1,0:T(8,128)(2,1)S(1)}, u32[]{:S(2)}, u32[]{:S(2)}) %collective-permute-start.3) | collective-permute-done | bytes 262176 | tf_op jit(solution)/shard_map/ppermute | solution.py:26
  30.4 3.0 %collective-permute-start.8 = (bf16[4,128,256]{2,1,0:T(8,128)(2,1)S(1)}, bf16[4,128,256]{2,1,0:T(8,128)(2,1)S(1)}, u32[]{:S(2)}, u32[]{:S(2)}) collective-permute-start(bf16[4,128,256]{2,1,0:T(8,128)(2,1)S(1)} %pad_maximum_fusion.2), channel_id=1, source_target_pairs={{0,32},{4,228},{32,64},{36,4},{64,96},{68,36},{96,128},{100,68},{1... | collective-permute-start | bytes 786440 | tf_op jit(solution)/shard_map/ppermute | solution.py:26
  33.6 2.2 %collective-permute-done.9 = bf16[8,128,256]{2,1,0:T(8,128)(2,1)S(1)} collective-permute-done((bf16[8,128,256]{2,1,0:T(8,128)(2,1)S(1)}, bf16[8,128,256]{2,1,0:T(8,128)(2,1)S(1)}, u32[]{:S(2)}, u32[]{:S(2)}) %collective-permute-start.9) | collective-permute-done | bytes 524320 | tf_op jit(solution)/shard_map/ppermute | solution.py:26
  35.8 1.1 collective-permute-start.10
  37.0 3.5 %collective-permute-start.6 = (bf16[4,128,256]{2,1,0:T(8,128)(2,1)S(1)}, bf16[4,128,256]{2,1,0:T(8,128)(2,1)S(1)}, u32[]{:S(2)}, u32[]{:S(2)}) collective-permute-start(bf16[4,128,256]{2,1,0:T(8,128)(2,1)S(1)} %pad_maximum_fusion.3), channel_id=1, source_target_pairs={{0,32},{4,228},{32,64},{36,4},{64,96},{68,36},{96,128},{100,68},{1... | collective-permute-start | bytes 786440 | tf_op jit(solution)/shard_map/ppermute | solution.py:26
  40.5 1.4 %collective-permute-start.13 = (bf16[4,128,256]{2,1,0:T(8,128)(2,1)S(1)}, bf16[4,128,256]{2,1,0:T(8,128)(2,1)S(1)}, u32[]{:S(2)}, u32[]{:S(2)}) collective-permute-start(bf16[4,128,256]{2,1,0:T(8,128)(2,1)S(1)} %add_convert_fusion.2), channel_id=1, source_target_pairs={{0,32},{4,228},{32,64},{36,4},{64,96},{68,36},{96,128},{100,68},{1... | collective-permute-start | bytes 786440 | tf_op jit(solution)/shard_map/ppermute | solution.py:26
  42.2 3.7 %collective-permute-start.12 = (bf16[3,128,256]{2,1,0:T(8,128)(2,1)S(1)}, bf16[3,128,256]{2,1,0:T(8,128)(2,1)S(1)}, u32[]{:S(2)}, u32[]{:S(2)}) collective-permute-start(bf16[3,128,256]{2,1,0:T(8,128)(2,1)S(1)} %pad_maximum_fusion.4), channel_id=1, source_target_pairs={{0,64},{4,196},{32,96},{36,228},{64,128},{68,4},{96,160},{100,36},... | collective-permute-start | bytes 589832 | tf_op jit(solution)/shard_map/ppermute | solution.py:26
  46.0 1.1 collective-permute-start.11
  47.0 1.7 %collective-permute-done.13 = bf16[4,128,256]{2,1,0:T(8,128)(2,1)S(1)} collective-permute-done((bf16[4,128,256]{2,1,0:T(8,128)(2,1)S(1)}, bf16[4,128,256]{2,1,0:T(8,128)(2,1)S(1)}, u32[]{:S(2)}, u32[]{:S(2)}) %collective-permute-start.13) | collective-permute-done | bytes 262176 | tf_op jit(solution)/shard_map/ppermute | solution.py:26
  48.7 3.0 %collective-permute-done.12 = bf16[3,128,256]{2,1,0:T(8,128)(2,1)S(1)} collective-permute-done((bf16[3,128,256]{2,1,0:T(8,128)(2,1)S(1)}, bf16[3,128,256]{2,1,0:T(8,128)(2,1)S(1)}, u32[]{:S(2)}, u32[]{:S(2)}) %collective-permute-start.12) | collective-permute-done | bytes 196640 | tf_op jit(solution)/shard_map/ppermute | solution.py:26
  52.1 3.1 %collective-permute-start.18 = (bf16[2,128,256]{2,1,0:T(8,128)(2,1)S(1)}, bf16[2,128,256]{2,1,0:T(8,128)(2,1)S(1)}, u32[]{:S(2)}, u32[]{:S(2)}) collective-permute-start(bf16[2,128,256]{2,1,0:T(8,128)(2,1)S(1)} %pad_maximum_fusion.5), channel_id=1, source_target_pairs={{0,64},{4,196},{32,96},{36,228},{64,128},{68,4},{96,160},{100,36},... | collective-permute-start | bytes 393224 | tf_op jit(solution)/shard_map/ppermute | solution.py:26
  55.5 1.8 %collective-permute-start.15 = (bf16[1,128,256]{2,1,0:T(8,128)(2,1)S(1)}, bf16[1,128,256]{2,1,0:T(8,128)(2,1)S(1)}, u32[]{:S(2)}, u32[]{:S(2)}) collective-permute-start(bf16[1,128,256]{2,1,0:T(8,128)(2,1)S(1)} %get-tuple-element.97), channel_id=1, source_target_pairs={{0,16},{4,20},{8,24},{12,28},{16,0},{20,4},{24,8},{28,12},{1,17},{... | collective-permute-start | bytes 196616 | tf_op jit(solution)/shard_map/ppermute | solution.py:26
  57.3 5.7 %collective-permute-start.20 = (bf16[128,256]{1,0:T(8,128)(2,1)S(1)}, bf16[128,256]{1,0:T(8,128)(2,1)S(1)}, u32[]{:S(2)}, u32[]{:S(2)}) collective-permute-start(bf16[128,256]{1,0:T(8,128)(2,1)S(1)} %fusion.10), channel_id=1, source_target_pairs={{0,4},{4,0},{1,5},{5,1},{2,6},{6,2},{3,7},{7,3},{8,12},{12,8},{9,1... | collective-permute-start | bytes 196616 | tf_op jit(solution)/shard_map/ppermute | solution.py:30
  63.9 0.7 collective-permute-done.17.refs_3_
  64.6 12.3 %precondition.1 = (f32[512,512]{1,0:T(8,128)}, f32[128,128]{1,0:T(8,128)}, bf16[512,128]{1,0:T(8,128)(2,1)}) custom-call(f32[128,256]{1,0:T(8,128)S(1)} %slice_bitcast_fusion.1.refs_0_, bf16[128,256]{1,0:T(8,128)(2,1)S(1)} %bitcast.35, bf16[128,256]{1,0:T(8,128)(2,1)S(1)} %get-tuple-element.99.refs_2_, bf16[128,256]{1,0:T(8,128)(2,1)S(1)} %collective-permute-done.17.refs_3_, ...), custom_call_target="tpu_custom_call" | custom-call | tf_op jit(solution)/shard_map/precondition/pallas_call | solution.py:227
  76.9 8.0 %all-to-all-start = ((bf16[64,8,128]{2,1,0:T(8,128)(2,1)}), bf16[64,8,128]{2,1,0:T(8,128)(2,1)S(1)}, u32[]{:S(2)}, u32[]{:S(2)}) async-start(bf16[64,8,128]{2,1,0:T(8,128)(2,1)} %bitcast.15), calls=%async_computation | async-start | bytes 262144 | tf_op jit(solution)/shard_map/all_to_all | solution.py:272
  85.5 10.5 %all-to-all-done = bf16[64,8,128]{2,1,0:T(8,128)(2,1)S(1)} async-done(((bf16[64,8,128]{2,1,0:T(8,128)(2,1)}), bf16[64,8,128]{2,1,0:T(8,128)(2,1)S(1)}, u32[]{:S(2)}, u32[]{:S(2)}) %all-to-all-start) | async-done | bytes 131104 | tf_op jit(solution)/shard_map/all_to_all | solution.py:272
  96.4 26.3 %all_to_all.10 = bf16[256,8,128]{2,1,0:T(8,128)(2,1)S(1)} all-to-all(bf16[256,8,128]{2,1,0:T(8,128)(2,1)S(1)} %bitcast.36), channel_id=1, replica_groups=mesh['dp_0'=8,'dp_1'=4,'dp_2'=2,'tensor'=4] {'dp_0','dp_1','dp_2','tensor'}, dimensions={0} | all-to-all | bytes 1048576 | tf_op jit(solution)/shard_map/all_to_all | solution.py:281
  122.7 1.5 %placed.1 = bf16[2,128,1024]{2,1,0:T(8,128)(2,1)} custom-call(bf16[2048,128]{1,0:T(8,128)(2,1)S(1)} %bitcast.30), custom_call_target="tpu_custom_call" | custom-call | tf_op jit(solution)/shard_map/placed/pallas_call | solution.py:257
  (69 shorter events, 4.6 us)
Async XLA Ops:
  0.6 10.5 %collective-permute-start = (bf16[256,8192]{1,0:T(8,128)(2,1)}, bf16[256,8192]{1,0:T(8,128)(2,1)}, u32[]{:S(2)}, u32[]{:S(2)}) collective-permute-start(bf16[256,8192]{1,0:T(8,128)(2,1)} %a_ref.1), channel_id=1, source_target_pairs={{0,4},{4,0},{1,5},{5,1},{2,6},{6,2},{3,7},{7,3},{8,12},{12,8},{9,1... | collective-permute-start | bytes 12582920 | tf_op jit(solution)/shard_map/ppermute | solution.py:30
  5.1 6.1 %collective-permute-start.1 = (bf16[512,256]{1,0:T(8,128)(2,1)S(1)}, bf16[512,256]{1,0:T(8,128)(2,1)S(1)}, u32[]{:S(2)}, u32[]{:S(2)}) collective-permute-start(bf16[512,256]{1,0:T(8,128)(2,1)S(1)} %bitcast.32), channel_id=1, source_target_pairs={{0,4},{4,0},{1,5},{5,1},{2,6},{6,2},{3,7},{7,3},{8,12},{12,8},{9,1... | collective-permute-start | bytes 786440 | tf_op jit(solution)/shard_map/ppermute | solution.py:30
  5.2 2.2 %copy-start = (bf16[256,8192]{1,0:T(8,128)(2,1)S(1)}, bf16[256,8192]{1,0:T(8,128)(2,1)}, u32[]{:S(2)}) copy-start(bf16[256,8192]{1,0:T(8,128)(2,1)} %a_ref.1) | copy-start | bytes 12582916
  7.4 0.7 copy-start.3
  14.0 13.2 %collective-permute-start.4 = (bf16[8,128,256]{2,1,0:T(8,128)(2,1)S(1)}, bf16[8,128,256]{2,1,0:T(8,128)(2,1)S(1)}, u32[]{:S(2)}, u32[]{:S(2)}) collective-permute-start(bf16[8,128,256]{2,1,0:T(8,128)(2,1)S(1)} %get-tuple-element.62), channel_id=1, source_target_pairs={{0,8},{4,28},{8,16},{12,4},{16,24},{20,12},{24,0},{28,20},{1,9},{5... | collective-permute-start | bytes 1572872 | tf_op jit(solution)/shard_map/ppermute | solution.py:26
  15.1 12.2 %collective-permute-start.5 = (bf16[4,128,256]{2,1,0:T(8,128)(2,1)S(1)}, bf16[4,128,256]{2,1,0:T(8,128)(2,1)S(1)}, u32[]{:S(2)}, u32[]{:S(2)}) collective-permute-start(bf16[4,128,256]{2,1,0:T(8,128)(2,1)S(1)} %get-tuple-element.63), channel_id=1, source_target_pairs={{0,64},{4,196},{32,96},{36,228},{64,128},{68,4},{96,160},{100,36},... | collective-permute-start | bytes 786440 | tf_op jit(solution)/shard_map/ppermute | solution.py:26
  24.7 5.6 %collective-permute-start.3 = (bf16[4,128,256]{2,1,0:T(8,128)(2,1)S(1)}, bf16[4,128,256]{2,1,0:T(8,128)(2,1)S(1)}, u32[]{:S(2)}, u32[]{:S(2)}) collective-permute-start(bf16[4,128,256]{2,1,0:T(8,128)(2,1)S(1)} %get-tuple-element.60), channel_id=1, source_target_pairs={{0,32},{4,228},{32,64},{36,4},{64,96},{68,36},{96,128},{100,68},{1... | collective-permute-start | bytes 786440 | tf_op jit(solution)/shard_map/ppermute | solution.py:26
  25.5 7.9 %collective-permute-start.2 = (bf16[4,128,256]{2,1,0:T(8,128)(2,1)S(1)}, bf16[4,128,256]{2,1,0:T(8,128)(2,1)S(1)}, u32[]{:S(2)}, u32[]{:S(2)}) collective-permute-start(bf16[4,128,256]{2,1,0:T(8,128)(2,1)S(1)} %get-tuple-element.58), channel_id=1, source_target_pairs={{0,32},{4,228},{32,64},{36,4},{64,96},{68,36},{96,128},{100,68},{1... | collective-permute-start | bytes 786440 | tf_op jit(solution)/shard_map/ppermute | solution.py:26
  27.4 8.4 %collective-permute-start.9 = (bf16[8,128,256]{2,1,0:T(8,128)(2,1)S(1)}, bf16[8,128,256]{2,1,0:T(8,128)(2,1)S(1)}, u32[]{:S(2)}, u32[]{:S(2)}) collective-permute-start(bf16[8,128,256]{2,1,0:T(8,128)(2,1)S(1)} %pad_maximum_fusion), channel_id=1, source_target_pairs={{0,8},{4,28},{8,16},{12,4},{16,24},{20,12},{24,0},{28,20},{1,9},{5... | collective-permute-start | bytes 1572872 | tf_op jit(solution)/shard_map/ppermute | solution.py:26
  28.1 13.8 %collective-permute-start.7 = (bf16[8,128,256]{2,1,0:T(8,128)(2,1)S(1)}, bf16[8,128,256]{2,1,0:T(8,128)(2,1)S(1)}, u32[]{:S(2)}, u32[]{:S(2)}) collective-permute-start(bf16[8,128,256]{2,1,0:T(8,128)(2,1)S(1)} %pad_maximum_fusion.1), channel_id=1, source_target_pairs={{0,8},{4,28},{8,16},{12,4},{16,24},{20,12},{24,0},{28,20},{1,9},{5... | collective-permute-start | bytes 1572872 | tf_op jit(solution)/shard_map/ppermute | solution.py:26
  30.4 10.0 %collective-permute-start.8 = (bf16[4,128,256]{2,1,0:T(8,128)(2,1)S(1)}, bf16[4,128,256]{2,1,0:T(8,128)(2,1)S(1)}, u32[]{:S(2)}, u32[]{:S(2)}) collective-permute-start(bf16[4,128,256]{2,1,0:T(8,128)(2,1)S(1)} %pad_maximum_fusion.2), channel_id=1, source_target_pairs={{0,32},{4,228},{32,64},{36,4},{64,96},{68,36},{96,128},{100,68},{1... | collective-permute-start | bytes 786440 | tf_op jit(solution)/shard_map/ppermute | solution.py:26
  35.8 6.1 %collective-permute-start.10 = (bf16[8,128,256]{2,1,0:T(8,128)(2,1)S(1)}, bf16[8,128,256]{2,1,0:T(8,128)(2,1)S(1)}, u32[]{:S(2)}, u32[]{:S(2)}) collective-permute-start(bf16[8,128,256]{2,1,0:T(8,128)(2,1)S(1)} %collective-permute-done.9), channel_id=1, source_target_pairs={{0,4},{4,0},{1,5},{5,1},{2,6},{6,2},{3,7},{7,3},{8,12},{12,8},{9,1... | collective-permute-start | bytes 1572872 | tf_op jit(solution)/shard_map/ppermute | solution.py:30
  37.0 8.9 %collective-permute-start.6 = (bf16[4,128,256]{2,1,0:T(8,128)(2,1)S(1)}, bf16[4,128,256]{2,1,0:T(8,128)(2,1)S(1)}, u32[]{:S(2)}, u32[]{:S(2)}) collective-permute-start(bf16[4,128,256]{2,1,0:T(8,128)(2,1)S(1)} %pad_maximum_fusion.3), channel_id=1, source_target_pairs={{0,32},{4,228},{32,64},{36,4},{64,96},{68,36},{96,128},{100,68},{1... | collective-permute-start | bytes 786440 | tf_op jit(solution)/shard_map/ppermute | solution.py:26
  40.5 8.2 %collective-permute-start.13 = (bf16[4,128,256]{2,1,0:T(8,128)(2,1)S(1)}, bf16[4,128,256]{2,1,0:T(8,128)(2,1)S(1)}, u32[]{:S(2)}, u32[]{:S(2)}) collective-permute-start(bf16[4,128,256]{2,1,0:T(8,128)(2,1)S(1)} %add_convert_fusion.2), channel_id=1, source_target_pairs={{0,32},{4,228},{32,64},{36,4},{64,96},{68,36},{96,128},{100,68},{1... | collective-permute-start | bytes 786440 | tf_op jit(solution)/shard_map/ppermute | solution.py:26
  41.9 22.7 %copy-start.1 = (f32[1,1,512,512]{3,2,1,0:T(8,128)S(1)}, f32[1,1,512,512]{3,2,1,0:T(8,128)}, u32[]{:S(2)}) copy-start(f32[1,1,512,512]{3,2,1,0:T(8,128)} %param.8) | copy-start | bytes 3145732
  41.9 22.7 %copy-start.2 = (f32[1,1,128,128]{3,2,1,0:T(8,128)S(1)}, f32[1,1,128,128]{3,2,1,0:T(8,128)}, u32[]{:S(2)}) copy-start(f32[1,1,128,128]{3,2,1,0:T(8,128)} %param.9) | copy-start | bytes 196612
  42.1 42.8 %copy-start.4 = (s32[64]{0:T(128)S(1)}, s32[64]{0:T(128)}, u32[]{:S(2)}) copy-start(s32[64]{0:T(128)} %owner_ref.5) | copy-start | bytes 772
  42.2 9.5 %collective-permute-start.12 = (bf16[3,128,256]{2,1,0:T(8,128)(2,1)S(1)}, bf16[3,128,256]{2,1,0:T(8,128)(2,1)S(1)}, u32[]{:S(2)}, u32[]{:S(2)}) collective-permute-start(bf16[3,128,256]{2,1,0:T(8,128)(2,1)S(1)} %pad_maximum_fusion.4), channel_id=1, source_target_pairs={{0,64},{4,196},{32,96},{36,228},{64,128},{68,4},{96,160},{100,36},... | collective-permute-start | bytes 589832 | tf_op jit(solution)/shard_map/ppermute | solution.py:26
  46.0 9.2 %collective-permute-start.11 = (bf16[4,128,256]{2,1,0:T(8,128)(2,1)S(1)}, bf16[4,128,256]{2,1,0:T(8,128)(2,1)S(1)}, u32[]{:S(2)}, u32[]{:S(2)}) collective-permute-start(bf16[4,128,256]{2,1,0:T(8,128)(2,1)S(1)} %add_convert_fusion.1), channel_id=1, source_target_pairs={{0,32},{4,228},{32,64},{36,4},{64,96},{68,36},{96,128},{100,68},{1... | collective-permute-start | bytes 786440 | tf_op jit(solution)/shard_map/ppermute | solution.py:26
  48.7 6.5 %collective-permute-start.14 = (bf16[4,128,256]{2,1,0:T(8,128)(2,1)S(1)}, bf16[4,128,256]{2,1,0:T(8,128)(2,1)S(1)}, u32[]{:S(2)}, u32[]{:S(2)}) collective-permute-start(bf16[4,128,256]{2,1,0:T(8,128)(2,1)S(1)} %collective-permute-done.13), channel_id=1, source_target_pairs={{0,4},{4,0},{1,5},{5,1},{2,6},{6,2},{3,7},{7,3},{8,12},{12,8},{9,1... | collective-permute-start | bytes 786440 | tf_op jit(solution)/shard_map/ppermute | solution.py:30
  51.7 5.6 %collective-permute-start.19 = (bf16[2,128,256]{2,1,0:T(8,128)(2,1)S(1)}, bf16[2,128,256]{2,1,0:T(8,128)(2,1)S(1)}, u32[]{:S(2)}, u32[]{:S(2)}) collective-permute-start(bf16[2,128,256]{2,1,0:T(8,128)(2,1)S(1)} %pad_maximum_fusion.7), channel_id=1, source_target_pairs={{0,32},{4,228},{32,64},{36,4},{64,96},{68,36},{96,128},{100,68},{1... | collective-permute-start | bytes 393224 | tf_op jit(solution)/shard_map/ppermute | solution.py:26
  52.1 5.2 %collective-permute-start.18 = (bf16[2,128,256]{2,1,0:T(8,128)(2,1)S(1)}, bf16[2,128,256]{2,1,0:T(8,128)(2,1)S(1)}, u32[]{:S(2)}, u32[]{:S(2)}) collective-permute-start(bf16[2,128,256]{2,1,0:T(8,128)(2,1)S(1)} %pad_maximum_fusion.5), channel_id=1, source_target_pairs={{0,64},{4,196},{32,96},{36,228},{64,128},{68,4},{96,160},{100,36},... | collective-permute-start | bytes 393224 | tf_op jit(solution)/shard_map/ppermute | solution.py:26
  55.3 7.7 %collective-permute-start.16 = (bf16[2,128,256]{2,1,0:T(8,128)(2,1)S(1)}, bf16[2,128,256]{2,1,0:T(8,128)(2,1)S(1)}, u32[]{:S(2)}, u32[]{:S(2)}) collective-permute-start(bf16[2,128,256]{2,1,0:T(8,128)(2,1)S(1)} %pad_maximum_fusion.6), channel_id=1, source_target_pairs={{0,8},{4,28},{8,16},{12,4},{16,24},{20,12},{24,0},{28,20},{1,9},{5... | collective-permute-start | bytes 393224 | tf_op jit(solution)/shard_map/ppermute | solution.py:26
  55.5 8.2 %collective-permute-start.15 = (bf16[1,128,256]{2,1,0:T(8,128)(2,1)S(1)}, bf16[1,128,256]{2,1,0:T(8,128)(2,1)S(1)}, u32[]{:S(2)}, u32[]{:S(2)}) collective-permute-start(bf16[1,128,256]{2,1,0:T(8,128)(2,1)S(1)} %get-tuple-element.97), channel_id=1, source_target_pairs={{0,16},{4,20},{8,24},{12,28},{16,0},{20,4},{24,8},{28,12},{1,17},{... | collective-permute-start | bytes 196616 | tf_op jit(solution)/shard_map/ppermute | solution.py:26
  57.3 6.6 %collective-permute-start.20 = (bf16[128,256]{1,0:T(8,128)(2,1)S(1)}, bf16[128,256]{1,0:T(8,128)(2,1)S(1)}, u32[]{:S(2)}, u32[]{:S(2)}) collective-permute-start(bf16[128,256]{1,0:T(8,128)(2,1)S(1)} %fusion.10), channel_id=1, source_target_pairs={{0,4},{4,0},{1,5},{5,1},{2,6},{6,2},{3,7},{7,3},{8,12},{12,8},{9,1... | collective-permute-start | bytes 196616 | tf_op jit(solution)/shard_map/ppermute | solution.py:30
  63.0 1.5 %collective-permute-start.17 = (bf16[128,256]{1,0:T(8,128)(2,1)S(1)}, bf16[128,256]{1,0:T(8,128)(2,1)S(1)}, u32[]{:S(2)}, u32[]{:S(2)}) collective-permute-start(bf16[128,256]{1,0:T(8,128)(2,1)S(1)} %get-tuple-element.98), channel_id=1, source_target_pairs={{0,4},{4,0},{1,5},{5,1},{2,6},{6,2},{3,7},{7,3},{8,12},{12,8},{9,1... | collective-permute-start | bytes 196616 | tf_op jit(solution)/shard_map/ppermute | solution.py:30
  76.9 19.1 %all-to-all-start = ((bf16[64,8,128]{2,1,0:T(8,128)(2,1)}), bf16[64,8,128]{2,1,0:T(8,128)(2,1)S(1)}, u32[]{:S(2)}, u32[]{:S(2)}) async-start(bf16[64,8,128]{2,1,0:T(8,128)(2,1)} %bitcast.15), calls=%async_computation | async-start | bytes 262144 | tf_op jit(solution)/shard_map/all_to_all | solution.py:272
